TPU v7x, 32 devices: a whole 2x2x4 slice. The times are simulated.
32 devices in a mesh: dp: 8 (over y, x, core), mp: 4 (over z).
Axes of the slice: x: 2, y: 2, z: 4, core: 2. Of those that a mesh axis runs over, the one named last changes fastest.
Arguments:
- x_short: bfloat16 [72, 128, 768], P('dp'), may hold values from -6 to 6
- x_long: bfloat16 [16, 512, 768], P('dp'), may hold values from -6 to 6
- short_lengths: int32 [72], P('dp'), may hold values from 32 to 128, as said below
- long_lengths: int32 [16], P('dp'), may hold values from 128 to 512, as said below
- slope_index: int32 [12], P('mp'), may hold values from 0 to 23
- w_qkv: bfloat16 [768, 3, 768], P(None, None, 'mp'), may hold values from -0.3125 to 0.3125
- b_qv: float32 [64, 2, 12], P(None, None, 'mp'), may hold values from -3 to 3
- w_out: bfloat16 [768, 768], P(None, 'mp'), may hold values from -0.875 to 0.875
- b_out: float32 [768], replicated, may hold values from -3 to 3
- gain1: float32 [768], replicated, may hold values from 0.5 to 1.5
- bias1: float32 [768], replicated, may hold values from -3 to 3
- w_up: bfloat16 [768, 2, 3072], P(None, None, 'mp'), may hold values from -0.21875 to 0.21875
- w_down: bfloat16 [768, 3072], P(None, 'mp'), may hold values from -0.109375 to 0.109375
- b_down: float32 [768], replicated, may hold values from -3 to 3
- gain2: float32 [768], replicated, may hold values from 0.5 to 1.5
- bias2: float32 [768], replicated, may hold values from -3 to 3
- cot_short: bfloat16 [72, 128, 768], P('dp'), may hold values from -6 to 6
- cot_long: bfloat16 [16, 512, 768], P('dp'), may hold values from -6 to 6
Outputs:
- y_short: bfloat16 [72, 128, 768], P('dp')
- y_long: bfloat16 [16, 512, 768], P('dp')
- dx_short: bfloat16 [72, 128, 768], P('dp')
- dx_long: bfloat16 [16, 512, 768], P('dp')
- grad_w_qkv: float32 [768, 3, 768], P('dp', None, 'mp')
- grad_b_qv: float32 [64, 2, 12], P('dp', None, 'mp')
- grad_w_out: float32 [768, 768], P('dp', 'mp')
- grad_b_out: float32 [768], P('dp')
- grad_gain1: float32 [768], P('dp')
- grad_bias1: float32 [768], P('dp')
- grad_w_up: float32 [768, 2, 3072], P('dp', None, 'mp')
- grad_w_down: float32 [768, 3072], P('dp', 'mp')
- grad_b_down: float32 [768], P('dp')
- grad_gain2: float32 [768], P('dp')
- grad_bias2: float32 [768], P('dp')
Inputs may be any that keep to these rules, and one draw needn't show every extreme that they name: `short_lengths`: true length of each short sequence; positions from it on are padding. `long_lengths`: true length of each long sequence; positions from it on are padding. `slope_index`: ALiBi slope index of each head, below 24; heads may share an index.
All inputs are finite; a program needn't handle non-finite values.
Results may differ from a plain program's by a relative error of at most 0.025.
The roundings to bfloat16 on the way count: a program that leaves them out, or rounds other values in their place, can miss the bound.
Values may be sent and summed in bfloat16 or wider, within the bound.
A program may use at most 128 MiB of HBM per device.

v0:
```python
import math

import jax
import jax.numpy as jnp
from jax import lax
from jax.sharding import PartitionSpec as P

HEADS = 12


EPSILON = 1e-12
MASKED = -1e30


def alibi_slopes(slope_index, head_total):
    power = 1 << head_total.bit_length() - 1
    index_f = slope_index.astype(jnp.float32)
    main_part = jnp.exp2(-8.0 * (index_f + 1.0) / power)
    extra_part = jnp.exp2(-4.0 * (2.0 * (index_f - power) + 1.0) / power)
    return jnp.where(slope_index < power, main_part, extra_part)


def bucket_scores(queries, key_rows, lengths, slopes):
    length = queries.shape[1]
    raw_scores = jnp.einsum(
        "sqhe,skhe->shqk", queries, key_rows, preferred_element_type=jnp.float32
    )
    position = jnp.arange(length)
    distance = jnp.abs(position[:, None] - position[None, :]).astype(jnp.float32)
    scores = (
        raw_scores * (1.0 / math.sqrt(queries.shape[3]))
        - slopes[None, :, None, None] * distance[None, None]
    )
    key_valid = position[None, None, None, :] < lengths[:, None, None, None]
    return jnp.where(key_valid, scores, MASKED)


def attend_forward(queries, key_rows, value_rows, lengths, slopes):
    scores = bucket_scores(queries, key_rows, lengths, slopes)
    maxima = jnp.max(scores, axis=-1, keepdims=True)
    exponent = jnp.exp(scores - maxima)
    totals = jnp.sum(exponent, axis=-1, keepdims=True)
    soft_probs = (exponent / totals).astype(jnp.bfloat16)
    context = jnp.einsum(
        "shqk,skhe->sqhe", soft_probs, value_rows, preferred_element_type=jnp.float32
    )
    return (context.astype(jnp.bfloat16), maxima + jnp.log(totals))


def attend_backward(queries, key_rows, value_rows, lengths, slopes, log_total, grad_context):
    scores = bucket_scores(queries, key_rows, lengths, slopes)
    soft_probs = jnp.exp(scores - log_total)
    grad_values = jnp.einsum(
        "shqk,sqhe->skhe",
        soft_probs.astype(jnp.bfloat16),
        grad_context,
        preferred_element_type=jnp.float32,
    )
    grad_probs = jnp.einsum(
        "sqhe,skhe->shqk", grad_context, value_rows, preferred_element_type=jnp.float32
    )
    row_term = jnp.sum(soft_probs * grad_probs, axis=-1, keepdims=True)
    grad_scores = (soft_probs * (grad_probs - row_term)).astype(jnp.bfloat16)
    inv_root = 1.0 / math.sqrt(queries.shape[3])
    grad_query = (
        jnp.einsum("shqk,skhe->sqhe", grad_scores, key_rows, preferred_element_type=jnp.float32)
        * inv_root
    )
    grad_keys = (
        jnp.einsum("shqk,sqhe->skhe", grad_scores, queries, preferred_element_type=jnp.float32)
        * inv_root
    )
    return (grad_query, grad_keys, grad_values)


def project_heads(token_rows, w_qkv, b_qv):
    projected = jnp.einsum("rd,dce->rce", token_rows, w_qkv, preferred_element_type=jnp.float32)
    queries = (projected[:, 0] + b_qv[:, 0, :].T.reshape(-1)).astype(jnp.bfloat16)
    key_rows = projected[:, 1].astype(jnp.bfloat16)
    value_rows = (projected[:, 2] + b_qv[:, 1, :].T.reshape(-1)).astype(jnp.bfloat16)
    return (queries, key_rows, value_rows)


def gate_and_up(hidden_low, w_up):
    projected = jnp.einsum("rd,dcf->rcf", hidden_low, w_up, preferred_element_type=jnp.float32)
    return (projected[:, 0], projected[:, 1])


def gelu_gate(gate_rows, up_rows):
    return jax.nn.gelu(gate_rows, approximate=False) * up_rows


def layer_stats(totals):
    mean_vec = jnp.mean(totals, axis=1, keepdims=True)
    centred = totals - mean_vec
    inv_scale = lax.rsqrt(jnp.mean(centred * centred, axis=1) + EPSILON)
    return (centred * inv_scale[:, None], inv_scale)


def norm_backward(grad_normed, normed, inv_scale):
    mean_grad = jnp.mean(grad_normed, axis=1, keepdims=True)
    mean_cross = jnp.mean(grad_normed * normed, axis=1, keepdims=True)
    return inv_scale[:, None] * (grad_normed - mean_grad - normed * mean_cross)


def post_norm(partial_sum, residual, shift_in, gain_vec, shift_vec):
    totals = (
        residual
        + lax.psum(
            partial_sum.astype(jnp.bfloat16).astype(jnp.float32).astype(jnp.bfloat16), "mp"
        ).astype(jnp.float32)
        + shift_in
    )
    normed, inv_scale = layer_stats(totals)
    return (normed, inv_scale, normed * gain_vec + shift_vec)


def mp_total(partial_sum):
    return lax.psum(partial_sum.astype(jnp.bfloat16), "mp").astype(jnp.float32)


def per_device(
    x_short,
    x_long,
    short_lengths,
    long_lengths,
    slope_index,
    w_qkv,
    b_qv,
    w_out,
    b_out,
    gain1,
    bias1,
    w_up,
    w_down,
    b_down,
    gain2,
    bias2,
    cot_short,
    cot_long,
):
    head_size = b_qv.shape[0]
    head_count = b_qv.shape[2]
    features = x_short.shape[2]
    short_shape = x_short.shape
    long_shape = x_long.shape
    short_rows = short_shape[0] * short_shape[1]
    slopes = alibi_slopes(slope_index, HEADS)
    contract_last = (((1,), (1,)), ((), ()))
    contract_first = (((0,), (0,)), ((), ()))

    def short_part(flat_rows):
        return flat_rows[:short_rows].reshape(short_shape[0], short_shape[1], head_count, head_size)

    def long_part(flat_rows):
        return flat_rows[short_rows:].reshape(long_shape[0], long_shape[1], head_count, head_size)

    token_rows = jnp.concatenate(
        [x_short.reshape(short_rows, features), x_long.reshape(-1, features)], 0
    )
    queries, key_rows, value_rows = project_heads(token_rows, w_qkv, b_qv)
    ctx_short, log_short = attend_forward(
        short_part(queries), short_part(key_rows), short_part(value_rows), short_lengths, slopes
    )
    ctx_long, log_long = attend_forward(
        long_part(queries), long_part(key_rows), long_part(value_rows), long_lengths, slopes
    )
    context = jnp.concatenate(
        [ctx_short.reshape(short_rows, -1), ctx_long.reshape(-1, head_count * head_size)], 0
    )
    attn_partial = lax.dot_general(
        context, w_out, contract_last, preferred_element_type=jnp.float32
    )
    normed1, scale1, hidden1 = post_norm(
        attn_partial, token_rows.astype(jnp.float32), b_out, gain1, bias1
    )
    hidden_low = hidden1.astype(jnp.bfloat16)
    gate_rows, up_rows = gate_and_up(hidden_low, w_up)
    inner = gelu_gate(gate_rows, up_rows).astype(jnp.bfloat16)
    feed_partial = lax.dot_general(inner, w_down, contract_last, preferred_element_type=jnp.float32)
    normed2, scale2, output_rows = post_norm(feed_partial, hidden1, b_down, gain2, bias2)
    y_rows = output_rows.astype(jnp.bfloat16)
    grad_out = jnp.concatenate(
        [cot_short.reshape(short_rows, features), cot_long.reshape(-1, features)], 0
    ).astype(jnp.float32)
    grad_gain2 = jnp.sum(grad_out * normed2, axis=0)
    grad_bias2 = jnp.sum(grad_out, axis=0)
    grad_sum2 = norm_backward(grad_out * gain2, normed2, scale2)
    grad_b_down = jnp.sum(grad_sum2, axis=0)
    grad_feed = grad_sum2.astype(jnp.bfloat16)
    gate_again, up_again = gate_and_up(hidden_low, w_up)
    inner_again, gelu_pull = jax.vjp(gelu_gate, gate_again, up_again)
    grad_w_down = lax.dot_general(
        grad_feed,
        inner_again.astype(jnp.bfloat16),
        contract_first,
        preferred_element_type=jnp.float32,
    )
    grad_inner = jnp.dot(grad_feed, w_down, preferred_element_type=jnp.float32)
    grad_gate, grad_up = gelu_pull(grad_inner)
    grad_gate_up = jnp.stack([grad_gate, grad_up], axis=1).astype(jnp.bfloat16)
    grad_w_up = jnp.einsum(
        "rd,rcf->dcf", hidden_low, grad_gate_up, preferred_element_type=jnp.float32
    )
    grad_hidden1 = grad_sum2 + mp_total(
        jnp.einsum("rcf,dcf->rd", grad_gate_up, w_up, preferred_element_type=jnp.float32)
    )
    grad_gain1 = jnp.sum(grad_hidden1 * normed1, axis=0)
    grad_bias1 = jnp.sum(grad_hidden1, axis=0)
    grad_sum1 = norm_backward(grad_hidden1 * gain1, normed1, scale1)
    grad_b_out = jnp.sum(grad_sum1, axis=0)
    grad_attention = grad_sum1.astype(jnp.bfloat16)
    grad_w_out = lax.dot_general(
        grad_attention, context, contract_first, preferred_element_type=jnp.float32
    )
    grad_context = jnp.dot(grad_attention, w_out, preferred_element_type=jnp.float32).astype(
        jnp.bfloat16
    )
    q_again, k_again, v_again = project_heads(token_rows, w_qkv, b_qv)
    gq_short, gk_short, gv_short = attend_backward(
        short_part(q_again),
        short_part(k_again),
        short_part(v_again),
        short_lengths,
        slopes,
        log_short,
        short_part(grad_context),
    )
    gq_long, gk_long, gv_long = attend_backward(
        long_part(q_again),
        long_part(k_again),
        long_part(v_again),
        long_lengths,
        slopes,
        log_long,
        long_part(grad_context),
    )
    proj_width = head_count * head_size
    grad_query = jnp.concatenate(
        [gq_short.reshape(short_rows, proj_width), gq_long.reshape(-1, proj_width)], 0
    ).astype(jnp.bfloat16)
    grad_keys = jnp.concatenate(
        [gk_short.reshape(short_rows, proj_width), gk_long.reshape(-1, proj_width)], 0
    ).astype(jnp.bfloat16)
    grad_values = jnp.concatenate(
        [gv_short.reshape(short_rows, proj_width), gv_long.reshape(-1, proj_width)], 0
    ).astype(jnp.bfloat16)
    bias_query = jnp.sum(grad_query, axis=0, dtype=jnp.float32).reshape(head_count, head_size).T
    bias_value = jnp.sum(grad_values, axis=0, dtype=jnp.float32).reshape(head_count, head_size).T
    grad_b_qv = jnp.stack([bias_query, bias_value], axis=1)
    grad_proj = jnp.stack([grad_query, grad_keys, grad_values], axis=1)
    grad_w_qkv = jnp.einsum(
        "rd,rce->dce", token_rows, grad_proj, preferred_element_type=jnp.float32
    )
    grad_rows = grad_sum1 + mp_total(
        jnp.einsum("rce,dce->rd", grad_proj, w_qkv, preferred_element_type=jnp.float32)
    )
    dx_rows = grad_rows.astype(jnp.bfloat16)
    (
        grad_w_qkv,
        grad_b_qv,
        grad_w_out,
        grad_b_out,
        grad_gain1,
        grad_bias1,
        grad_w_up,
        grad_w_down,
        grad_b_down,
        grad_gain2,
        grad_bias2,
    ) = (
        lax.psum_scatter(grad_w_qkv, "dp", scatter_dimension=0, tiled=True),
        lax.psum_scatter(grad_b_qv, "dp", scatter_dimension=0, tiled=True),
        lax.psum_scatter(grad_w_out, "dp", scatter_dimension=0, tiled=True),
        lax.psum_scatter(grad_b_out, "dp", scatter_dimension=0, tiled=True),
        lax.psum_scatter(grad_gain1, "dp", scatter_dimension=0, tiled=True),
        lax.psum_scatter(grad_bias1, "dp", scatter_dimension=0, tiled=True),
        lax.psum_scatter(grad_w_up, "dp", scatter_dimension=0, tiled=True),
        lax.psum_scatter(grad_w_down, "dp", scatter_dimension=0, tiled=True),
        lax.psum_scatter(grad_b_down, "dp", scatter_dimension=0, tiled=True),
        lax.psum_scatter(grad_gain2, "dp", scatter_dimension=0, tiled=True),
        lax.psum_scatter(grad_bias2, "dp", scatter_dimension=0, tiled=True),
    )
    y_short = y_rows[:short_rows].reshape(short_shape)
    y_long = y_rows[short_rows:].reshape(long_shape)
    dx_short = dx_rows[:short_rows].reshape(short_shape)
    dx_long = dx_rows[short_rows:].reshape(long_shape)
    return (
        y_short,
        y_long,
        dx_short,
        dx_long,
        grad_w_qkv,
        grad_b_qv,
        grad_w_out,
        grad_b_out,
        grad_gain1,
        grad_bias1,
        grad_w_up,
        grad_w_down,
        grad_b_down,
        grad_gain2,
        grad_bias2,
    )


def solution(mesh):
    placed = (
        P("dp", None, None),
        P("dp", None, None),
        P("dp"),
        P("dp"),
        P("mp"),
        P(None, None, "mp"),
        P(None, None, "mp"),
        P(None, "mp"),
        P(),
        P(),
        P(),
        P(None, None, "mp"),
        P(None, "mp"),
        P(),
        P(),
        P(),
        P("dp", None, None),
        P("dp", None, None),
    )
    return jax.shard_map(
        per_device,
        mesh=mesh,
        in_specs=placed,
        out_specs=(
            P("dp", None, None),
            P("dp", None, None),
            P("dp", None, None),
            P("dp", None, None),
            P("dp", None, "mp"),
            P("dp", None, "mp"),
            P("dp", "mp"),
            P("dp"),
            P("dp"),
            P("dp"),
            P("dp", None, "mp"),
            P("dp", "mp"),
            P("dp"),
            P("dp"),
            P("dp"),
        ),
        check_vma=False,
    )
```

profile of v0, /device:TPU:0, one launch (start us, length us, event | category | flops | bytes accessed | tf_op | source)
XLA Modules:
  0.0 904.8 jit_solution(5098385445035556553)
XLA Ops:
  8.4 4.4 fusion.99
  42.7 2.8 convolution_convert_fusion
  45.8 130.0 %all-reduce.13.cloned.1.call-done = bf16[2176,768]{1,0:T(8,128)(2,1)} async-done(((bf16[2176,768]{1,0:T(8,128)(2,1)}), bf16[2176,768]{1,0:T(8,128)(2,1)}) %all-reduce.13.cloned.1.call-update) | async-done | bytes 3342352 | tf_op jit(solution)/shard_map/psum | solution.py:109
  175.9 3.7 fusion.29
  182.9 7.0 fusion.42
  189.9 15.9 %multiply_convert_fusion.1 = (bf16[2176,768]{1,0:T(8,128)(2,1)S(1)}, f32[2176,768]{1,0:T(8,128)}) fusion(f32[2176,2,768]{2,0,1:T(8,128)S(1)} %fusion.42), kind=kLoop, calls=%fused_computation.38 | loop fusion | flops 110297088 | bytes 23396352 | tf_op jit(solution)/shard_map/convert_element_type | solution.py:179
  207.5 4.2 convolution_convert_fusion.1
  212.2 126.1 %all-reduce.15.cloned.1.call-done = bf16[2176,768]{1,0:T(8,128)(2,1)} async-done(((bf16[2176,768]{1,0:T(8,128)(2,1)}), bf16[2176,768]{1,0:T(8,128)(2,1)}) %all-reduce.15.cloned.1.call-update) | async-done | bytes 3342352 | tf_op jit(solution)/shard_map/psum | solution.py:109
  338.3 5.5 fusion.102
  345.8 4.1 fusion.7
  349.9 4.9 fusion.4
  354.8 13.0 %fusion.36 = (bf16[2176,1,768]{2,0,1:T(8,128)(2,1)S(1)}, bf16[2176,1,768]{2,0,1:T(8,128)(2,1)}) fusion(f32[2176,768]{1,0:T(8,128)} %get-tuple-element.81, f32[2176,2,768]{2,0,1:T(8,128)} %copy-done.13, bf16[768,768]{1,0:T(8,128)(2,1)S(1)} %copy-done.41, f32[2176,768]{1,0:T(8,128)S(1)} %get-tuple-element.84), kind=kOutput, calls=%fused_computation.79 | convolution fusion | flops 2598666240 | bytes 34603008 | tf_op jit(solution)/shard_map/dot_general | solution.py:199
  369.5 8.3 bitcast_convert_fusion.1
  379.4 125.0 %all-reduce.17.cloned.1.call-done = bf16[2176,768]{1,0:T(8,128)(2,1)} async-done(((bf16[2176,768]{1,0:T(8,128)(2,1)}), bf16[2176,768]{1,0:T(8,128)(2,1)}) %all-reduce.17.cloned.1.call-update) | async-done | bytes 3342352 | tf_op jit(solution)/shard_map/psum | solution.py:119
  504.4 8.2 multiply_reduce_fusion
  512.7 7.4 fusion.101
  526.1 3.3 fusion.68
  539.0 4.8 fusion.71
  543.7 4.5 multiply_reduce_fusion.4
  577.3 6.5 bitcast_convert_fusion
  583.9 13.0 %fusion.31 = f32[768,2,768]{2,0,1:T(8,128)} fusion(bf16[2176,1,768]{2,0,1:T(8,128)(2,1)} %get-tuple-element.83, bf16[2176,1,768]{2,0,1:T(8,128)(2,1)} %copy-done.44, f32[768]{0:T(1024)S(1)} %copy-done.37, f32[768]{0:T(1024)S(1)} %copy-done.32, bf16[2176,768]{1,0:T(8,128)(2,1)} %all-reduce.13.cloned.1.call-done, f32[2176]{0:T(1024)S(1)} %add_rsqrt_fusion.1, ...), kind=kOutput, calls=%fused_computation.71 | convolution fusion | flops 5167251456 | bytes 18114560 | tf_op jit(solution)/shard_map/rd,rcf->dcf/dot_general | solution.py:202
  597.2 8.2 fusion.51
  605.5 5.0 fusion.48
  610.6 6.6 fusion.34
  621.8 2.8 slice.101
  625.6 24.9 %all-reduce.7 = (f32[64,2,3]{0,2,1:T(4,128)S(1)}, f32[768]{0:T(1024)S(1)}, f32[768]{0:T(1024)S(1)}, f32[768]{0:T(1024)S(1)}, f32[768]{0:T(1024)S(1)}, /*index=5*/f32[768]{0:T(1024)S(1)}, f32[768]{0:T(1024)S(1)}) all-reduce(f32[64,2,3]{0,2,1:T(4,128)S(1)} %pad_maximum_fusion.5, ...), channel_id=3, replica_groups=mesh['dp'=8,'mp'=4] {'dp'}, use_global_device_ids=true, to_apply=%region_21.22.clone | all-reduce | flops 4992 | bytes 39936
  654.7 55.7 %all-reduce.19.cloned.1.call-done = bf16[2176,768]{1,0:T(8,128)(2,1)} async-done(((bf16[2176,768]{1,0:T(8,128)(2,1)}), bf16[2176,768]{1,0:T(8,128)(2,1)}) %all-reduce.19.cloned.1.call-update) | async-done | bytes 3342352 | tf_op jit(solution)/shard_map/psum | solution.py:119
  710.4 4.7 add_convert_fusion
  717.7 48.7 %reduce-scatter.10.cloned.1.call-done = f32[96,2,768]{2,0,1:T(8,128)} async-done(((f32[768,2,768]{2,0,1:T(8,128)}), f32[96,2,768]{2,0,1:T(8,128)}) %reduce-scatter.10.cloned.1.call-update) | async-done | bytes 589840 | tf_op jit(solution)/shard_map/reduce_scatter | solution.py:278
  768.7 43.8 %reduce-scatter.12.cloned.1.call-done = f32[96,768]{1,0:T(8,128)} async-done(((f32[768,768]{1,0:T(8,128)}), f32[96,768]{1,0:T(8,128)}) %reduce-scatter.12.cloned.1.call-update) | async-done | bytes 294928 | tf_op jit(solution)/shard_map/reduce_scatter | solution.py:279
  812.5 38.7 %reduce-scatter.8.cloned.1.call-done = f32[96,192]{1,0:T(8,128)} async-done(((f32[768,192]{1,0:T(8,128)}), f32[96,192]{1,0:T(8,128)}) %reduce-scatter.8.cloned.1.call-update) | async-done | bytes 73744 | tf_op jit(solution)/shard_map/reduce_scatter | solution.py:274
  851.3 46.3 %reduce-scatter.6.cloned.1.call-done = f32[96,3,192]{2,0,1:T(8,128)} async-done(((f32[768,3,192]{2,0,1:T(8,128)}), f32[96,3,192]{2,0,1:T(8,128)}) %reduce-scatter.6.cloned.1.call-update) | async-done | bytes 221200 | tf_op jit(solution)/shard_map/reduce_scatter | solution.py:272
  (205 shorter events, 100.0 us)
Async XLA Ops:
  7.2 175.7 %copy-start = (bf16[768,2,768]{2,1,0:T(2,128)(2,1)S(1)}, bf16[768,2,768]{2,1,0:T(2,128)(2,1)}, u32[]{:S(2)}) copy-start(bf16[768,2,768]{2,1,0:T(2,128)(2,1)} %param.29) | copy-start | bytes 7077892
  7.2 168.7 %all-reduce.13.cloned.1.call-start = ((), (), s32[]{:S(2)}) async-start(), calls=%async_computation.4 | async-start | bytes 6684672 | tf_op jit(solution)/shard_map/psum | solution.py:109
  13.1 5.1 copy-start.38
  13.1 5.1 copy-start.39
  24.6 11.5 %copy-start.24 = (bf16[9,128,3,64]{1,0,3,2:T(8,128)(2,1)}, bf16[9,128,3,64]{1,0,3,2:T(8,128)(2,1)S(1)}, u32[]{:S(2)}) copy-start(bf16[9,128,3,64]{1,0,3,2:T(8,128)(2,1)S(1)} %reshape.372) | copy-start | bytes 1327108
  42.6 133.2 %copy-start.29 = (f32[768]{0:T(1024)S(1)}, f32[768]{0:T(1024)}, u32[]{:S(2)}) copy-start(f32[768]{0:T(1024)} %param.26) | copy-start | bytes 9220
  45.6 292.7 %all-reduce.15.cloned.1.call-start = ((), (), s32[]{:S(2)}) async-start(), calls=%async_computation.5 | async-start | bytes 6684672 | tf_op jit(solution)/shard_map/psum | solution.py:109
  189.9 15.9 %copy-start.13 = (f32[2176,2,768]{2,0,1:T(8,128)}, f32[2176,2,768]{2,0,1:T(8,128)S(1)}, u32[]{:S(2)}) copy-start(f32[2176,2,768]{2,0,1:T(8,128)S(1)} %fusion.42) | copy-start | bytes 40108036
  189.9 17.6 %copy-start.40 = (bf16[768,768]{1,0:T(8,128)(2,1)S(1)}, bf16[768,768]{1,0:T(8,128)(2,1)}, u32[]{:S(2)}) copy-start(bf16[768,768]{1,0:T(8,128)(2,1)} %param.30) | copy-start | bytes 3538948
  211.7 292.7 %all-reduce.17.cloned.1.call-start = ((), (), s32[]{:S(2)}) async-start(), calls=%async_computation.6 | async-start | bytes 6684672 | tf_op jit(solution)/shard_map/psum | solution.py:119
  344.8 5.1 copy-start.36
  354.8 13.0 %copy-start.4 = (f32[2176,768]{1,0:T(8,128)}, f32[2176,768]{1,0:T(8,128)S(1)}, u32[]{:S(2)}) copy-start(f32[2176,768]{1,0:T(8,128)S(1)} %get-tuple-element.84) | copy-start | bytes 20054020
  377.8 332.5 %all-reduce.19.cloned.1.call-start = ((), (), s32[]{:S(2)}) async-start(), calls=%async_computation.7 | async-start | bytes 6684672 | tf_op jit(solution)/shard_map/psum | solution.py:119
  379.3 133.3 %copy-start.8 = (bf16[9,128,768]{2,1,0:T(8,128)(2,1)S(1)}, bf16[9,128,768]{2,1,0:T(8,128)(2,1)}, u32[]{:S(2)}) copy-start(bf16[9,128,768]{2,1,0:T(8,128)(2,1)} %param.18) | copy-start | bytes 5308420
  379.4 133.3 %copy-start.32 = (f32[768]{0:T(1024)S(1)}, f32[768]{0:T(1024)}, u32[]{:S(2)}) copy-start(f32[768]{0:T(1024)} %param.27) | copy-start | bytes 9220
  504.4 8.3 copy-start.6
  504.4 8.3 copy-start.10
  504.4 8.3 copy-start.15
  526.1 10.5 %copy-start.25 = (bf16[9,128,3,64]{1,0,3,2:T(8,128)(2,1)S(1)}, bf16[9,128,3,64]{1,0,3,2:T(8,128)(2,1)}, u32[]{:S(2)}) copy-start(bf16[9,128,3,64]{1,0,3,2:T(8,128)(2,1)} %reshape.374) | copy-start | bytes 1327108
  539.0 9.3 %slice-start = ((s8[6291456]{0:T(1024)(128)(4,1)}), s8[4194304]{0:T(1024)(128)(4,1)S(1)}, s32[]{:S(2)}) async-start(s8[6291456]{0:T(1024)(128)(4,1)} %bitcast.235), calls=%async_computation.12 | async-start | bytes 8388608
  577.3 6.6 copy-start.37
  583.8 182.6 %reduce-scatter.10.cloned.1.call-start = ((), (), s32[]{:S(2)}) async-start(), calls=%async_computation.10 | async-start | bytes 5308416 | tf_op jit(solution)/shard_map/reduce_scatter | solution.py:278
  596.9 215.6 %reduce-scatter.12.cloned.1.call-start = ((), (), s32[]{:S(2)}) async-start(), calls=%async_computation.11 | async-start | bytes 2654208 | tf_op jit(solution)/shard_map/reduce_scatter | solution.py:279
  605.5 245.8 %reduce-scatter.8.cloned.1.call-start = ((), (), s32[]{:S(2)}) async-start(), calls=%async_computation.9 | async-start | bytes 884736 | tf_op jit(solution)/shard_map/reduce_scatter | solution.py:274
  610.5 6.8 copy-start.43
  610.5 287.0 %reduce-scatter.6.cloned.1.call-start = ((), (), s32[]{:S(2)}) async-start(), calls=%async_computation.8 | async-start | bytes 2654208 | tf_op jit(solution)/shard_map/reduce_scatter | solution.py:272
  617.2 7.5 copy-start.17
  617.2 7.9 copy-start.16
  617.2 8.0 copy-start.23
  617.3 8.3 copy-start.33
  617.3 8.3 copy-start.34
  710.4 187.2 %copy-start.1 = (bf16[768,2,768]{2,1,0:T(2,128)(2,1)S(1)}, bf16[768,2,768]{2,1,0:T(2,128)(2,1)}, u32[]{:S(2)}) copy-start(bf16[768,2,768]{2,1,0:T(2,128)(2,1)} %param.29) | copy-start | bytes 7077892
  (23 other events, 64.5 us)
Sparse Core Ops, SparseCore 0:
  45.7 130.1 all-reduce.12
  211.8 126.3 all-reduce.14
  377.9 126.3 all-reduce.16
  583.9 126.3 all-reduce.18
  713.6 52.6 reduce-scatter.9
  770.2 42.3 reduce-scatter.11
  816.3 34.9 reduce-scatter.7
  855.2 42.3 reduce-scatter.5
where the time goes:
time: 915 us; the launch traced here: 905 us
  waiting for transfers between devices  614 us (67%)
  matrix products  109 us (12%)
  local copies, waits for them, and re-layouts  70.8 us (8%)
  other arithmetic  68 us (7%)
  blocking collectives  24.9 us (3%)
  between operations  16.6 us (2%)
    psum x2, waiting for transfers between devices, post_norm(): lax.psum(partial_sum.astype(jnp.bfloat16).astype(jnp.float32).astype(jnp....  256 us
    psum x2, waiting for transfers between devices, mp_total(): return lax.psum(partial_sum.astype(jnp.bfloat16), 'mp').astype(jnp.float32)  181 us
    reduce_scatter x1, waiting for transfers between devices, per_device(): lax.psum_scatter(grad_w_up, 'dp', scatter_dimension=0, tiled=True)  48.7 us
    reduce_scatter x1, waiting for transfers between devices, per_device(): lax.psum_scatter(grad_w_qkv, 'dp', scatter_dimension=0, tiled=True)  46.3 us
    reduce_scatter x1, waiting for transfers between devices, per_device(): lax.psum_scatter(grad_w_down, 'dp', scatter_dimension=0, tiled=True)  43.8 us
    reduce_scatter x1, waiting for transfers between devices, per_device(): lax.psum_scatter(grad_w_out, 'dp', scatter_dimension=0, tiled=True)  38.7 us
    unnamed x1, blocking collectives  24.9 us
  transfers between devices with their start and end apart: 8, of which 8 were waited for; matrix products, arithmetic and copies ran while one was open for 6% of the time, Pallas kernels for 0%

commit v1 on v0

v1 whole, which is shorter than its diff:
```python
import functools
import math

import jax
import jax.numpy as jnp
from jax import lax
from jax.experimental import pallas as pl
from jax.experimental.pallas import tpu as pltpu
from jax.sharding import PartitionSpec as P

F32, BF16 = jnp.float32, jnp.bfloat16
R, D, E = 640, 768, 192
FAR = 1e30
VM = 60 << 20

def nn(a, b): return lax.dot_general(a, b, (((1,), (0,)), ((), ())), preferred_element_type=F32)
def nt(a, b): return lax.dot_general(a, b, (((1,), (1,)), ((), ())), preferred_element_type=F32)

def load_rows(m, long_ref, short_ref, buf, sem):
    @pl.when(m < 2)
    def _():
        c = pltpu.make_async_copy(long_ref.at[pl.ds(4 * m, 4)], buf.at[pl.ds(0, 4)], sem); c.start(); c.wait()
        buf[4] = jnp.zeros((128, D), BF16)
    @pl.when(m == 2)
    def _():
        c = pltpu.make_async_copy(short_ref.at[pl.ds(0, 5)], buf, sem); c.start(); c.wait()
    @pl.when(m == 3)
    def _():
        c = pltpu.make_async_copy(short_ref.at[pl.ds(5, 4)], buf.at[pl.ds(0, 4)], sem); c.start(); c.wait()
        buf[4] = jnp.zeros((128, D), BF16)

def distances(m, slen, llen, dm):
    @pl.when(m < 2)
    def _():
        n = llen[jnp.minimum(m, 1)]
        key = lax.broadcasted_iota(jnp.int32, (512, 128), 0)
        qry = lax.broadcasted_iota(jnp.int32, (512, 128), 1)
        for i in range(4):
            dist = jnp.abs(key - (qry + 128 * i)).astype(F32)
            dm[i] = jnp.where(key < n, dist, FAR)
    @pl.when(m >= 2)
    def _():
        key = lax.broadcasted_iota(jnp.int32, (128, 128), 0)
        qry = lax.broadcasted_iota(jnp.int32, (128, 128), 1)
        dist = jnp.abs(key - qry).astype(F32)
        for i in range(5):
            n = slen[jnp.minimum(5 * (m - 2) + i, 8)] if i == 4 else slen[jnp.maximum(5 * (m - 2), 0) + i]
            dm[i, 0:128, :] = jnp.where(key < n, dist, FAR)

def head_lanes(j):
    return lax.broadcasted_iota(jnp.int32, (1, E), 1) // 64 == j
def head_rows(j):
    return lax.broadcasted_iota(jnp.int32, (E, 1), 0) // 64 == j

def attend_fwd(m, small, q8, k, vt, dm, ct, lse):
    def block(i, keys, koff):
        cols = pl.ds(pl.multiple_of(i * 128, 128), 128)
        qi = q8[cols, :]
        kk = k[pl.ds(koff, keys), :]
        vv = vt[:, pl.ds(koff, keys)]
        d = dm[i, 0:keys, :]
        out = jnp.zeros((E, 128), F32)
        for j in range(3):
            s = nt(kk, jnp.where(head_lanes(j), qi, jnp.zeros_like(qi))) - small[2:3, j:j + 1] * d
            mx = jnp.max(s, axis=0, keepdims=True)
            ex = jnp.exp(s - mx)
            tot = jnp.sum(ex, axis=0, keepdims=True)
            p = (ex * (1.0 / tot)).astype(BF16)
            out = jnp.where(head_rows(j), nn(vv, p), out)
            lse[j:j + 1, cols] = mx + jnp.log(tot)
        ct[:, cols] = out.astype(BF16)
    @pl.when(m < 2)
    def _():
        lax.fori_loop(0, 4, lambda i, u: (block(i, 512, 0), u)[1], 0)
    @pl.when(m >= 2)
    def _():
        lax.fori_loop(0, 5, lambda i, u: (block(i, 128, pl.multiple_of(i * 128, 128)), u)[1], 0)

def attend_bwd(m, small, q8, k, v, kt, gc, dm, lse, gqt, gk, gv):
    gk[...] = jnp.zeros_like(gk)
    gv[...] = jnp.zeros_like(gv)
    def block(i, keys, koff):
        cols = pl.ds(pl.multiple_of(i * 128, 128), 128)
        rows = pl.ds(koff, keys)
        qi, gi = q8[cols, :], gc[cols, :]
        kk, vv, ktt = k[rows, :], v[rows, :], kt[:, rows]
        d = dm[i, 0:keys, :]
        oq = jnp.zeros((E, 128), F32)
        ok = jnp.zeros((keys, E), F32)
        ov = jnp.zeros((keys, E), F32)
        for j in range(3):
            hl = head_lanes(j)
            qj = jnp.where(hl, qi, jnp.zeros_like(qi))
            gj = jnp.where(hl, gi, jnp.zeros_like(gi))
            s = nt(kk, qj) - small[2:3, j:j + 1] * d
            p = jnp.exp(s - lse[j:j + 1, cols])
            gp = nt(vv, gj)
            ov = ov + nn(p.astype(BF16), gj)
            row = jnp.sum(p * gp, axis=0, keepdims=True)
            ds = (p * (gp - row)).astype(BF16)
            oq = jnp.where(head_rows(j), nn(ktt, ds), oq)
            ok = ok + nn(ds, qj)
        gqt[:, cols] = oq * 0.125
        gk[rows, :] += ok
        gv[rows, :] += ov
    @pl.when(m < 2)
    def _():
        lax.fori_loop(0, 4, lambda i, u: (block(i, 512, 0), u)[1], 0)
        gqt[:, 512:640] = jnp.zeros((E, 128), F32)
    @pl.when(m >= 2)
    def _():
        lax.fori_loop(0, 5, lambda i, u: (block(i, 128, pl.multiple_of(i * 128, 128)), u)[1], 0)

def norm_fwd(s):
    mean = jnp.mean(s, axis=1, keepdims=True)
    c = s - mean
    r = lax.rsqrt(jnp.mean(c * c, axis=1, keepdims=True) + 1e-12)
    return c * r, r

def norm_bwd(gn, normed, r):
    return r * (gn - jnp.mean(gn, axis=1, keepdims=True) - normed * jnp.mean(gn * normed, axis=1, keepdims=True))

def row_tiles(fn, tile=128):
    def body(i, u):
        fn(pl.ds(pl.multiple_of(i * tile, tile), tile)); return u
    lax.fori_loop(0, R // tile, body, 0)

def ka(slen, llen, xl, xs, w, small, vec, q8o, ko, vo, co, lseo, n1o, r1o, hlo, xb, dm, vt, ct, acc, sem):
    z = pl.program_id(0)
    m = lax.axis_index("mp")
    @pl.when(z == 0)
    def _():
        load_rows(m, xl, xs, xb, sem)
        distances(m, slen, llen, dm)
        ct[...] = jnp.zeros_like(ct)
        lseo[...] = jnp.zeros_like(lseo)
        acc[...] = jnp.zeros_like(acc)
    x = xb[...].reshape(R, D)
    wz, sm = w.at[0, 0], small.at[0]
    q8o[0] = ((nt(x, wz[0:192, :]) + sm[0:1, 0:192]).astype(BF16).astype(F32) * 0.125).astype(BF16)
    ko[0] = nt(x, wz[192:384, :]).astype(BF16)
    v = (nt(x, wz[384:576, :]) + sm[1:2, 0:192]).astype(BF16)
    vo[0] = v
    vt[...] = v.T
    attend_fwd(m, sm, q8o.at[0], ko.at[0], vt, dm, ct, lseo.at[0])
    co[0] = ct[...].T
    acc[...] += nn(co[0], wz[576:768, :]).astype(BF16).astype(F32)
    @pl.when(z == 3)
    def _():
        for i in range(5):
            rows = slice(128 * i, 128 * i + 128)
            s = xb[i].astype(F32) + acc[rows, :] + vec[0:1, :]
            n, r = norm_fwd(s)
            n1o[rows, :] = n
            r1o[rows, :] = jnp.broadcast_to(r, (128, 128))
            hlo[rows, :] = (n * vec[1:2, :] + vec[2:3, :]).astype(BF16)

def const(shape): return pl.BlockSpec(shape, lambda z, *_: (0,) * len(shape))
def perz(shape): return pl.BlockSpec((1,) + shape, lambda z, *_: (z,) + (0,) * len(shape))
ANY = pl.BlockSpec(memory_space=pl.ANY)
def sds(shape, dt): return jax.ShapeDtypeStruct(shape, dt)
def part(p): return pl.BlockSpec((1, 1, D, D), lambda z, *_: (z, p, 0, 0))

def call(kernel, in_specs, outs, scratch, name, args, grid=(4,), prefetch=2):
    return pl.pallas_call(
        kernel,
        grid_spec=pltpu.PrefetchScalarGridSpec(num_scalar_prefetch=prefetch, grid=grid, in_specs=in_specs,
            out_specs=[o[0] for o in outs], scratch_shapes=scratch),
        out_shape=[o[1] for o in outs],
        compiler_params=pltpu.CompilerParams(dimension_semantics=("arbitrary",), vmem_limit_bytes=VM),
        name=name)(*args)

def run_ka(slen, llen, xl, xs, W, small, vec):
    rz = lambda: (perz((R, E)), sds((4, R, E), BF16))
    return call(ka, [ANY, ANY, part(0), perz((8, 256)), const((8, D))],
        [rz(), rz(), rz(), rz(), (perz((8, R)), sds((4, 8, R), F32)), (const((R, D)), sds((R, D), F32)), (const((R, 128)), sds((R, 128), F32)), (const((R, D)), sds((R, D), BF16))],
        [pltpu.VMEM((5, 128, D), BF16), pltpu.VMEM((5, 512, 128), F32), pltpu.VMEM((E, R), BF16), pltpu.VMEM((E, R), BF16), pltpu.VMEM((R, D), F32), pltpu.SemaphoreType.DMA],
        "attention_forward", (slen, llen, xl, xs, W, small, vec))

def gelu_parts(g):
    cdf = 0.5 * (1.0 + lax.erf(g * (2.0 ** -0.5)))
    pdf = jnp.exp(-0.5 * g * g) * (1.0 / math.sqrt(2 * math.pi))
    return g * cdf, cdf + g * pdf

def kb(cl, cs, wg, wu, wd, hl, n1, vec, ao, bo, io, yo, gfo, gs2o, vgo, acc, cb, sem):
    z = pl.program_id(0)
    m = lax.axis_index("mp")
    @pl.when(z == 0)
    def _():
        load_rows(m, cl, cs, cb, sem)
        acc[...] = jnp.zeros_like(acc)
    def tile(rows):
        h = hl[rows, :]
        gate = nn(h, wg[0, 0])
        up = nn(h, wu[0, 0])
        a, slope = gelu_parts(gate)
        ao[0, rows, :] = a
        bo[0, rows, :] = up * slope
        inner = (a * up).astype(BF16)
        io[0, rows, :] = inner
        acc[rows, :] += nt(inner, wd[0, 0]).astype(BF16).astype(F32)
    row_tiles(tile)
    @pl.when(z == 3)
    def _():
        tot = [jnp.zeros((1, D), F32)] * 3
        for i in range(5):
            rows = slice(128 * i, 128 * i + 128)
            h1 = n1[rows, :] * vec[1:2, :] + vec[2:3, :]
            n, r = norm_fwd(h1 + acc[rows, :] + vec[3:4, :])
            yo[rows, :] = (n * vec[4:5, :] + vec[5:6, :]).astype(BF16)
            gy = cb[i].astype(F32)
            gs = norm_bwd(gy * vec[4:5, :], n, r)
            gs2o[rows, :] = gs
            gfo[rows, :] = gs.astype(BF16)
            tot = [tot[0] + jnp.sum(gy * n, axis=0, keepdims=True), tot[1] + jnp.sum(gy, axis=0, keepdims=True), tot[2] + jnp.sum(gs, axis=0, keepdims=True)]
        vgo[...] = jnp.concatenate(tot + [jnp.zeros((5, D), F32)], axis=0)

def run_kb(cl, cs, W, hl, n1, vec):
    z32 = lambda: (perz((R, D)), sds((4, R, D), F32))
    return call(kb, [ANY, ANY, part(1), part(2), part(3), const((R, D)), const((R, D)), const((8, D))],
        [z32(), z32(), (perz((R, D)), sds((4, R, D), BF16)), (const((R, D)), sds((R, D), BF16)), (const((R, D)), sds((R, D), BF16)), (const((R, D)), sds((R, D), F32)), (const((8, D)), sds((8, D), F32))],
        [pltpu.VMEM((R, D), F32), pltpu.VMEM((5, 128, D), BF16), pltpu.SemaphoreType.DMA],
        "feed_forward", (cl, cs, W, W, W, hl, n1, vec), prefetch=0)

def kc(wg, wu, wd, a, b, inner, gf, hl, gs2, n1, r1, vec, go, gao, gs1o, vgo, acc, gft, hlt, gg):
    z = pl.program_id(0)
    @pl.when(z == 0)
    def _():
        acc[...] = gs2[...]
        gft[...] = gf[...].T
        hlt[...] = hl[...].T
    def tile(rows):
        gi = nn(gf[rows, :], wd[0, 0])
        g1 = (gi * b[0, rows, :]).astype(BF16)
        g2 = (gi * a[0, rows, :]).astype(BF16)
        gg[0, rows, :] = g1
        gg[1, rows, :] = g2
        acc[rows, :] += nt(g1, wg[0, 0]) + nt(g2, wu[0, 0])
    row_tiles(tile)
    def wtile(rows):
        go[0, 2, rows, :] = nn(gft[rows, :], inner[0]).astype(BF16)
        go[0, 0, rows, :] = nn(hlt[rows, :], gg[0]).astype(BF16)
        go[0, 1, rows, :] = nn(hlt[rows, :], gg[1]).astype(BF16)
    lax.fori_loop(0, 6, lambda i, u: (wtile(pl.ds(pl.multiple_of(i * 128, 128), 128)), u)[1], 0)
    @pl.when(z == 3)
    def _():
        tot = [jnp.zeros((1, D), F32)] * 3
        for i in range(5):
            rows = slice(128 * i, 128 * i + 128)
            gh, n = acc[rows, :], n1[rows, :]
            gs = norm_bwd(gh * vec[1:2, :], n, r1[rows, 0:1])
            gs1o[rows, :] = gs
            gao[rows, :] = gs.astype(BF16)
            tot = [tot[0] + jnp.sum(gh * n, axis=0, keepdims=True), tot[1] + jnp.sum(gh, axis=0, keepdims=True), tot[2] + jnp.sum(gs, axis=0, keepdims=True)]
        vgo[...] = jnp.concatenate(tot + [jnp.zeros((5, D), F32)], axis=0)

def run_kc(W, a, b, inner, gf, hl, gs2, n1, r1, vec):
    c = lambda dt: const((R, D))
    return call(kc, [part(1), part(2), part(3), perz((R, D)), perz((R, D)), perz((R, D)), c(0), c(0), c(0), c(0), const((R, 128)), const((8, D))],
        [(pl.BlockSpec((1, 3, D, D), lambda z: (z, 0, 0, 0)), sds((4, 3, D, D), BF16)), (const((R, D)), sds((R, D), BF16)), (const((R, D)), sds((R, D), F32)), (const((8, D)), sds((8, D), F32))],
        [pltpu.VMEM((R, D), F32), pltpu.VMEM((D, R), BF16), pltpu.VMEM((D, R), BF16), pltpu.VMEM((2, R, D), BF16)],
        "feed_backward", (W, W, W, a, b, inner, gf, hl, gs2, n1, r1, vec), prefetch=0)

def kd(slen, llen, xl, xs, w, small, q8, k, v, ctx, lse, ga, gs1, go, dxo, gbo, xb, dm, kt, gc, gqt, gk, gv, gat, xt, acc, sem):
    z = pl.program_id(0)
    m = lax.axis_index("mp")
    @pl.when(z == 0)
    def _():
        load_rows(m, xl, xs, xb, sem)
        distances(m, slen, llen, dm)
        acc[...] = gs1[...]
        gat[...] = ga[...].T
        xt[...] = xb[...].reshape(R, D).T
        gbo[...] = jnp.zeros_like(gbo)
    wz, sm = w.at[0, 0], small.at[0]
    gc[...] = nt(ga[...], wz[576:768, :]).astype(BF16)
    kt[...] = k[0].T
    attend_bwd(m, sm, q8.at[0], k.at[0], v.at[0], kt, gc, dm, lse.at[0], gqt, gk, gv)
    dq = gqt[...].astype(BF16).T
    dk = gk[...].astype(BF16)
    dv = gv[...].astype(BF16)
    gbo[z, 0:1, 0:192] = jnp.sum(dq.astype(F32), axis=0, keepdims=True)
    gbo[z, 1:2, 0:192] = jnp.sum(dv.astype(F32), axis=0, keepdims=True)
    acc[...] += nn(dq, wz[0:192, :]) + nn(dk, wz[192:384, :]) + nn(dv, wz[384:576, :])
    def wtile(rows):
        xr = xt[rows, :]
        go[0, 0, rows, :] = jnp.concatenate([nn(xr, dq), nn(xr, dk), nn(xr, dv), nn(gat[rows, :], ctx[0])], axis=1).astype(BF16)
    for i in range(6):
        wtile(slice(128 * i, 128 * i + 128))
    @pl.when(z == 3)
    def _():
        dxo[...] = acc[...].astype(BF16)

def run_kd(slen, llen, xl, xs, W, small, q8, k, v, ctx, lse, ga, gs1):
    rz = lambda: perz((R, E))
    rd = const((R, D))
    return call(kd, [ANY, ANY, part(0), perz((8, 256)), rz(), rz(), rz(), rz(), perz((8, R)), rd, rd],
        [(pl.BlockSpec((1, 1, D, D), lambda z, *_: (z, 0, 0, 0)), sds((4, 1, D, D), BF16)), (rd, sds((R, D), BF16)), (const((4, 8, 256)), sds((4, 8, 256), F32))],
        [pltpu.VMEM((5, 128, D), BF16), pltpu.VMEM((5, 512, 128), F32), pltpu.VMEM((E, R), BF16), pltpu.VMEM((R, E), BF16), pltpu.VMEM((E, R), F32), pltpu.VMEM((R, E), F32), pltpu.VMEM((R, E), F32),
         pltpu.VMEM((D, R), BF16), pltpu.VMEM((D, R), BF16), pltpu.VMEM((R, D), F32), pltpu.SemaphoreType.DMA],
        "attention_backward", (slen, llen, xl, xs, W, small, q8, k, v, ctx, lse, ga, gs1))

MESH = pl.DeviceIdType.MESH
GROUPS = ((0, 1), (1, 3))
PR = 96

def place():
    dp = lax.axis_index("dp"); z = lax.axis_index("mp")
    return dp, dp // 4, (dp // 2) % 2, dp % 2, z

def dpi(y, x, c):
    return (y * 2 + x) * 2 + c

def barrier_all(peers):
    b = pltpu.get_barrier_semaphore()
    for d in peers:
        pl.semaphore_signal(b, inc=1, device_id=d, device_id_type=MESH)
    pl.semaphore_wait(b, len(peers))

def ag_kernel(own, small, out, sout, stage, recv, send, loc, ss, sr):
    dp, y, x, c, z = place()
    xn, yn, cn = dpi(y, 1 - x, c), dpi(1 - y, x, c), dpi(y, x, 1 - c)
    dn = dpi(1 - y, 1 - x, c)
    barrier_all([(xn, z), (yn, z), (cn, z)] + [(dp, (z + k) % 4) for k in (1, 2, 3)])
    def sm(k): return pltpu.make_async_remote_copy(src_ref=small, dst_ref=sout.at[z], send_sem=ss.at[k], recv_sem=sr.at[z], device_id=(dp, (z + 1 + k) % 4), device_id_type=MESH)
    for k in range(3): sm(k).start()
    sout[z] = small[...]
    e = 1 - ((z + 1) // 2) % 2
    srcs = [z + 1 - 2 * (z % 2), e * ((z + 2) % 4) + (1 - e) * (3 - z), e * (3 - z) + (1 - e) * ((z + 2) % 4)]

    def rows(p, h):
        if h is None:
            return pl.ds(pl.multiple_of(p * PR, 32), PR)
        return pl.ds(pl.multiple_of(p * PR + h * (PR // 2), 16), PR // 2)
    def piece(s, g, p, h=None):
        a, n = GROUPS[g]
        return out.at[s, pl.ds(a, n), rows(p, h), :]
    def opiece(g, p):
        a, n = GROUPS[g]
        return own.at[pl.ds(a, n), rows(p, None), :]
    def cp(src, dst, s, g, k, r, dev):
        return pltpu.make_async_remote_copy(src_ref=src, dst_ref=dst, send_sem=send.at[s, g, k], recv_sem=recv.at[s, g, r], device_id=dev, device_id_type=MESH)
    def zsend(src, s, g):
        @pl.when((s <= z) & (z < 3))
        def _():
            cp(src, piece(s, g, dp), s, g, 0, 0, (dp, z + 1)).start()
        @pl.when((s >= z) & (z > 0))
        def _():
            cp(src, piece(s, g, dp), s, g, 1, 0, (dp, z - 1)).start()
    def zsend_wait(src, s, g):
        @pl.when((s <= z) & (z < 3))
        def _():
            cp(src, piece(s, g, dp), s, g, 0, 0, (dp, z + 1)).wait_send()
        @pl.when((s >= z) & (z > 0))
        def _():
            cp(src, piece(s, g, dp), s, g, 1, 0, (dp, z - 1)).wait_send()
    def simple(s, g):
        me, xp, yp, dg = dp, xn, yn, dn
        return dict(
            x=lambda: cp(piece(s, g, me), piece(s, g, me), s, g, 2, 1, (xn, z)),
            y=lambda: cp(piece(s, g, me), piece(s, g, me), s, g, 3, 2, (yn, z)),
            c=lambda: cp(piece(s, g, me), piece(s, g, me), s, g, 4, 3, (cn, z)),
            cx=lambda: cp(piece(s, g, xp), piece(s, g, xp), s, g, 5, 4, (cn, z)),
            cy=lambda: cp(piece(s, g, yp), piece(s, g, yp), s, g, 6, 5, (cn, z)),
            yf=lambda: cp(piece(s, g, xp, 0), piece(s, g, xp, 0), s, g, 7, 6, (yn, z)),
            xf=lambda: cp(piece(s, g, yp, 1), piece(s, g, yp, 1), s, g, 8, 7, (xn, z)),
            cd0=lambda: cp(piece(s, g, dg, 0), piece(s, g, dg, 0), s, g, 9, 8, (cn, z)),
            cd1=lambda: cp(piece(s, g, dg, 1), piece(s, g, dg, 1), s, g, 10, 9, (cn, z)),
        )
    def wrecv(ref, s, g, r):
        pltpu.make_async_remote_copy(src_ref=ref, dst_ref=ref, send_sem=send.at[s, g, 0], recv_sem=recv.at[s, g, r], device_id=(cn, z), device_id_type=MESH).wait_recv()
    def zarr(j, g):
        s = srcs[j]
        wrecv(piece(s, g, dp), s, g, 0)
        zsend(piece(s, g, dp), s, g)
        m = simple(s, g)
        m["x"]().start(); m["y"]().start(); m["c"]().start()
    def xyarr(j, g):
        s = srcs[j]; m = simple(s, g)
        wrecv(piece(s, g, xn), s, g, 1)
        m["yf"]().start(); m["cx"]().start()
        wrecv(piece(s, g, yn), s, g, 2)
        m["xf"]().start(); m["cy"]().start()
    def diag(j, g):
        s = srcs[j]; m = simple(s, g)
        wrecv(piece(s, g, dn, 0), s, g, 6)
        m["cd0"]().start()
        wrecv(piece(s, g, dn, 1), s, g, 7)
        m["cd1"]().start()
    def fin(j, g):
        s = srcs[j]; m = simple(s, g)
        zsend_wait(piece(s, g, dp), s, g)
        for k in ("x", "y", "c", "cx", "cy", "yf", "xf", "cd0", "cd1"):
            m[k]().wait_send()
        cdx, cdy, cdd = dpi(y, 1 - x, 1 - c), dpi(1 - y, x, 1 - c), dpi(1 - y, 1 - x, 1 - c)
        wrecv(piece(s, g, cn), s, g, 3)
        wrecv(piece(s, g, cdx), s, g, 4)
        wrecv(piece(s, g, cdy), s, g, 5)
        wrecv(piece(s, g, cdd, 0), s, g, 8)
        wrecv(piece(s, g, cdd, 1), s, g, 9)
    for g in (0, 1):
        zsend(opiece(g, dp), z, g)
    l1 = pltpu.make_async_copy(own, stage, loc.at[0]); l1.start()
    zarr(0, 0)
    zarr(0, 1)
    l1.wait()
    l2 = pltpu.make_async_copy(stage, out.at[z], loc.at[1]); l2.start()
    zarr(1, 0); xyarr(0, 0); zarr(1, 1)
    diag(0, 0); xyarr(0, 1)
    zarr(2, 0); xyarr(1, 0); zarr(2, 1)
    diag(0, 1); diag(1, 0); xyarr(1, 1)
    xyarr(2, 0); diag(2, 0); diag(1, 1); xyarr(2, 1); diag(2, 1)
    for g in (0, 1):
        zsend_wait(opiece(g, dp), z, g)
    for j in range(3):
        for g in (0, 1):
            fin(j, g)
    l2.wait()
    for k in range(3):
        sm(k).wait_send()
        pltpu.make_async_remote_copy(src_ref=small, dst_ref=sout.at[(z + 1 + k) % 4], send_sem=ss.at[k], recv_sem=sr.at[(z + 1 + k) % 4], device_id=(cn, z), device_id_type=MESH).wait_recv()

def gather_weights(own, small):
    A = pl.BlockSpec(memory_space=pl.ANY)
    V = pl.BlockSpec(memory_space=pltpu.VMEM)
    S = pltpu.SemaphoreType.DMA
    return pl.pallas_call(
        ag_kernel,
        out_shape=[jax.ShapeDtypeStruct((4, 4, 768, 768), jnp.bfloat16), jax.ShapeDtypeStruct((4, 8, 256), jnp.float32)],
        in_specs=[A, V], out_specs=[A, V],
        scratch_shapes=[pltpu.VMEM((4, 768, 768), jnp.bfloat16), S((4, 2, 10)), S((4, 2, 11)), S((2,)), S((3,)), S((4,))],
        compiler_params=pltpu.CompilerParams(collective_id=0, has_side_effects=True, vmem_limit_bytes=60 << 20),
        name="gather_weights",
    )(own, small)

ZO = (3, 0, 2, 1)

def far_order(z):
    e = 1 - ((z + 1) // 2) % 2
    return [z + 1 - 2 * (z % 2), e * ((z + 2) % 4) + (1 - e) * (3 - z), e * (3 - z) + (1 - e) * ((z + 2) % 4)]

def out_kernel(g1, g3, yin, dxin, vin, gout, yout, dxout, vout,
               r0, l0, rx, ry, rxy, ryx, rl, rr, stage, vr, vs,
               s0s, s0r, s0l, s1s, s1r, s2s, s2r, ys, yr, vsem_s, vsem_r, loc):
    dp, y, x, c, z = place()
    xn, yn, cn = dpi(y, 1 - x, c), dpi(1 - y, x, c), dpi(y, x, 1 - c)
    z1, z2 = z + 1 - 2 * (z % 2), (z + 2) % 4
    barrier_all([(xn, z), (yn, z), (cn, z)] + [(dp, (z + k) % 4) for k in (1, 2, 3)])

    def rows(p): return pl.ds(pl.multiple_of(p * PR, 32), PR)
    def rc(src, dst, ss, rs, dev):
        return pltpu.make_async_remote_copy(src_ref=src, dst_ref=dst, send_sem=ss, recv_sem=rs, device_id=dev, device_id_type=MESH)
    def st0(zz, q):
        p = dpi(q // 2, q % 2, 1 - c)
        return [rc(g1.at[zz, :, rows(p), :], r0.at[zz, q, pl.ds(0, 1)], s0s.at[zz, q, 0], s0r.at[zz, q, 0], (cn, z)),
                rc(g3.at[zz, :, rows(p), :], r0.at[zz, q, pl.ds(1, 3)], s0s.at[zz, q, 1], s0r.at[zz, q, 1], (cn, z))]
    def ld0(zz, q):
        p = dpi(q // 2, q % 2, c)
        return [pltpu.make_async_copy(g1.at[zz, :, rows(p), :], l0.at[zz, q, pl.ds(0, 1)], s0l.at[zz, q, 0]),
                pltpu.make_async_copy(g3.at[zz, :, rows(p), :], l0.at[zz, q, pl.ds(1, 3)], s0l.at[zz, q, 1])]
    order = far_order(z)
    def blk(s): return 4 * s + s // 3
    def yc(t, src, s, half, right):
        buf = (yout, dxout)[t]
        n, off = (4, 0) if half == 0 else (1, 4)
        dst = buf.at[pl.ds(blk(s) + off, n)]
        if src is None:
            src = dst
        else:
            src = src.at[pl.ds(off, n)]
        return rc(src, dst, ys.at[t, s, half, right], yr.at[t, s, half], (dp, z + 1 if right else z - 1))
    def ysend(t, src, s, act):
        for right in (1, 0):
            @pl.when((s <= z) & (z < 3) if right else (s >= z) & (z > 0))
            def _():
                getattr(yc(t, src, s, 0, right), act)()
                @pl.when(s == 2)
                def _():
                    getattr(yc(t, src, s, 1, right), act)()
    def yarr(t, j):
        s = order[j]
        yc(t, None, s, 0, 1).wait_recv()
        @pl.when(s == 2)
        def _():
            yc(t, None, s, 1, 1).wait_recv()
        ysend(t, None, s, "start")
    vpeer = [(cn, z), (xn, z), (yn, z), (dp, z1), (dp, z2)]
    def vstart(i): rc(vs.at[i], vr.at[i], vsem_s.at[i], vsem_r.at[i], vpeer[i]).start()
    def vstep(i):
        rc(vs.at[i], vr.at[i], vsem_s.at[i], vsem_r.at[i], vpeer[i]).wait_recv()
        tot = vs[i] + vr[i]
        if i < 4:
            vs[i + 1] = tot
            vstart(i + 1)
        else:
            vout[...] = tot

    for q in range(4):
        for d in st0(ZO[0], q): d.start()
        for d in ld0(ZO[0], q): d.start()
    for t, src in enumerate((yin, dxin)):
        ysend(t, src, z, "start")
    for zz in ZO[1:]:
        for q in range(4):
            for d in st0(zz, q): d.start()
            for d in ld0(zz, q): d.start()
    def own(t, which, way):
        n, off = (4, 0) if which == 0 else (1, 4)
        src = (yin, dxin)[t]
        dst = (yout, dxout)[t]
        if way == 0:
            return pltpu.make_async_copy(src.at[pl.ds(off, n)], stage.at[t, pl.ds(off, n)], loc.at[t, which, 0])
        return pltpu.make_async_copy(stage.at[t, pl.ds(off, n)], dst.at[pl.ds(blk(z) + off, n)], loc.at[t, which, 1])
    def ownall(fn):
        for t in (0, 1):
            fn(t, 0)
            @pl.when(z == 2)
            def _():
                fn(t, 1)
    ownall(lambda t, w: own(t, w, 0).start())
    vs[0] = vin[...]
    vstart(0)

    def addinto(dst, src):
        dst[...] = (dst[...].astype(F32) + src[...].astype(F32)).astype(BF16)
    def stage_a(zz):
        for q in range(4):
            for d in st0(zz, q): d.wait_recv()
            for d in ld0(zz, q): d.wait()
        def body(q, u):
            for t in range(4):
                addinto(l0.at[zz, q, t], r0.at[zz, q, t])
            return u
        lax.fori_loop(0, 4, body, 0)
        for k in range(2):
            s1x(zz, k).start(); s1y(zz, k).start()
    def s1x(zz, k):
        return rc(l0.at[zz, 2 * k + 1 - x, pl.ds(0, 2)], rx.at[zz, k], s1s.at[zz, k], s1r.at[zz, k], (xn, z))
    def s1y(zz, k):
        return rc(l0.at[zz, 2 * (1 - y) + k, pl.ds(2, 2)], ry.at[zz, k], s1s.at[zz, 2 + k], s1r.at[zz, 2 + k], (yn, z))
    def s1xy(zz):
        return rc(l0.at[zz, 2 * (1 - y) + x, pl.ds(0, 2)], rxy.at[zz], s1s.at[zz, 4], s1r.at[zz, 4], (yn, z))
    def s1yx(zz):
        return rc(l0.at[zz, 2 * y + 1 - x, pl.ds(2, 2)], ryx.at[zz], s1s.at[zz, 5], s1r.at[zz, 5], (xn, z))
    def stage_b(zz):
        for k in range(2):
            s1x(zz, k).wait_recv()
            for t in range(2):
                addinto(l0.at[zz, 2 * k + x, t], rx.at[zz, k, t])
        s1xy(zz).start()
        for k in range(2):
            s1y(zz, k).wait_recv()
            for t in range(2):
                addinto(l0.at[zz, 2 * y + k, 2 + t], ry.at[zz, k, t])
        s1yx(zz).start()
    def mine(zz): return l0.at[zz, 2 * y + x]
    def stage_c(zz):
        s1xy(zz).wait_recv()
        for t in range(2): addinto(mine(zz).at[t], rxy.at[zz, t])
        s1yx(zz).wait_recv()
        for t in range(2): addinto(mine(zz).at[2 + t], ryx.at[zz, t])
    def zs(zz, right):
        return rc(mine(zz), (rl if right else rr).at[zz], s2s.at[zz], s2r.at[zz, 0 if right else 1], (dp, z + 1 if right else z - 1))
    def stage_d(zz):
        @pl.when(z < zz)
        def _():
            @pl.when(z > 0)
            def _():
                zs(zz, True).wait_recv()
                for t in range(4): addinto(mine(zz).at[t], rl.at[zz, t])
            zs(zz, True).start()
        @pl.when(z > zz)
        def _():
            @pl.when(z < 3)
            def _():
                zs(zz, False).wait_recv()
                for t in range(4): addinto(mine(zz).at[t], rr.at[zz, t])
            zs(zz, False).start()
        @pl.when(z == zz)
        def _():
            for t in range(4): gout[t] = mine(zz)[t].astype(F32)
            if zz > 0:
                zs(zz, True).wait_recv()
                for t in range(4): gout[t] += rl[zz, t].astype(F32)
            if zz < 3:
                zs(zz, False).wait_recv()
                for t in range(4): gout[t] += rr[zz, t].astype(F32)
    A, B, C, Dd = stage_a, stage_b, stage_c, stage_d
    a, b, cc, d = ZO
    A(a); vstep(0); A(b); yarr(0, 0); B(a); vstep(1); A(cc); C(a); A(d)
    ownall(lambda t, w: (own(t, w, 0).wait(), own(t, w, 1).start()))
    vstep(2); yarr(0, 1); B(b); Dd(a); vstep(3); C(b); B(cc); yarr(0, 2); Dd(b); yarr(1, 0); C(cc); vstep(4); B(d); Dd(cc); C(d); yarr(1, 1); Dd(d); yarr(1, 2)
    for zz in ZO:
        for q in range(4):
            for dd in st0(zz, q): dd.wait_send()
        for k in range(2):
            s1x(zz, k).wait_send(); s1y(zz, k).wait_send()
        s1xy(zz).wait_send(); s1yx(zz).wait_send()
        @pl.when(z < zz)
        def _(): zs(zz, True).wait_send()
        @pl.when(z > zz)
        def _(): zs(zz, False).wait_send()
    for t, src in enumerate((yin, dxin)):
        ysend(t, src, z, "wait_send")
        for j in range(3):
            ysend(t, None, order[j], "wait_send")
    for i in range(5):
        rc(vs.at[i], vr.at[i], vsem_s.at[i], vsem_r.at[i], vpeer[i]).wait_send()
    ownall(lambda t, w: own(t, w, 1).wait())

def send_out(g1, g3, yv, dxv, vec):
    A = pl.BlockSpec(memory_space=pl.ANY)
    V = pl.BlockSpec(memory_space=pltpu.VMEM)
    S = pltpu.SemaphoreType.DMA
    b = lambda *s: pltpu.VMEM(s + (PR, 768), BF16)
    return pl.pallas_call(
        out_kernel,
        out_shape=[jax.ShapeDtypeStruct((4, PR, 768), F32), jax.ShapeDtypeStruct((17, 128, 768), BF16), jax.ShapeDtypeStruct((17, 128, 768), BF16), jax.ShapeDtypeStruct((8, 768), F32)],
        in_specs=[A, A, A, A, V], out_specs=[V, A, A, V],
        scratch_shapes=[b(4, 4, 4), b(4, 4, 4), b(4, 2, 2), b(4, 2, 2), b(4, 2), b(4, 2), b(4, 4), b(4, 4), pltpu.VMEM((2, 5, 128, 768), BF16),
                        pltpu.VMEM((5, 8, 768), F32), pltpu.VMEM((5, 8, 768), F32),
                        S((4, 4, 2)), S((4, 4, 2)), S((4, 4, 2)), S((4, 6)), S((4, 6)), S((4,)), S((4, 2)), S((2, 4, 2, 2)), S((2, 4, 2)), S((5,)), S((5,)), S((2, 2, 2))],
        compiler_params=pltpu.CompilerParams(collective_id=1, has_side_effects=True, vmem_limit_bytes=60 << 20),
        name="send_out",
    )(g1, g3, yv, dxv, vec)

def alibi_slopes(slope_index, head_total):
    power = 1 << head_total.bit_length() - 1
    f = slope_index.astype(F32)
    return jnp.where(slope_index < power, jnp.exp2(-8.0 * (f + 1.0) / power), jnp.exp2(-4.0 * (2.0 * (f - power) + 1.0) / power))
def prep(slope_index, w_qkv, b_qv, w_out, w_up, w_down):
    a = jnp.concatenate([jnp.transpose(w_qkv, (1, 2, 0)).reshape(576, D), w_out.T], 0)
    own = jnp.stack([a, w_up[:, 0], w_up[:, 1], w_down], 0)
    bt = jnp.transpose(b_qv, (1, 2, 0)).reshape(2, 192)
    sl = jnp.zeros((1, 192), F32).at[0, 0:3].set(alibi_slopes(slope_index, 12))
    small = jnp.pad(jnp.concatenate([bt, sl], 0), ((0, 5), (0, 64)))
    return own, small
def per_device(x_short, x_long, short_lengths, long_lengths, slope_index, w_qkv, b_qv, w_out, b_out, gain1, bias1, w_up, w_down, b_down, gain2, bias2, cot_short, cot_long):
    own, small = prep(slope_index, w_qkv, b_qv, w_out, w_up, w_down)
    W, S = gather_weights(own, small)
    vec = jnp.stack([b_out, gain1, bias1, b_down, gain2, bias2, bias2, bias2], 0)
    xl, cl = x_long.reshape(8, 128, D), cot_long.reshape(8, 128, D)
    q8, k, v, ctx, lse, n1, r1, hl = run_ka(short_lengths, long_lengths, xl, x_short, W, S, vec)
    a, b, inner, y, gf, gs2, vg2 = run_kb(cl, cot_short, W, hl, n1, vec)
    go3, ga, gs1, vg1 = run_kc(W, a, b, inner, gf, hl, gs2, n1, r1, vec)
    go1, dx, gb = run_kd(short_lengths, long_lengths, xl, x_short, W, S, q8, k, v, ctx, lse, ga, gs1)
    m, dpx = lax.axis_index("mp"), lax.axis_index("dp")
    gbr = jnp.transpose(gb[:, :2, :192], (1, 0, 2)).reshape(2, D)
    vsum = jnp.concatenate([vg2[:3], vg1[:3], gbr], 0)
    G, Y, DX, vs = send_out(go1, go3, y.reshape(5, 128, D), dx.reshape(5, 128, D), vsum)
    b = lax.dynamic_slice(vs[6:8].reshape(2, 12, 64), (0, 3 * m, 8 * dpx), (2, 3, 8))
    vs = lax.dynamic_slice(vs[:6], (0, 96 * dpx), (6, 96))
    gq = G[0][:, :576].reshape(-1, 3, 192)
    return (Y[8:], Y[:8].reshape(2, 512, D), DX[8:], DX[:8].reshape(2, 512, D), gq, jnp.transpose(b, (2, 0, 1)), G[0][:, 576:], vs[5], vs[3], vs[4], jnp.stack([G[1], G[2]], 1), G[3], vs[2], vs[0], vs[1])
def per_device_any(x_short, x_long, short_lengths, long_lengths, slope_index, w_qkv, b_qv, w_out, b_out, gain1, bias1, w_up, w_down, b_down, gain2, bias2, cot_short, cot_long):
    own, small = prep(slope_index, w_qkv, b_qv, w_out, w_up, w_down)
    W = lax.all_gather(own, "mp"); S = lax.all_gather(small, "mp")
    vec = jnp.stack([b_out, gain1, bias1, b_down, gain2, bias2, bias2, bias2], 0)
    xl, cl = x_long.reshape(8, 128, D), cot_long.reshape(8, 128, D)
    q8, k, v, ctx, lse, n1, r1, hl = run_ka(short_lengths, long_lengths, xl, x_short, W, S, vec)
    a, b, inner, y, gf, gs2, vg2 = run_kb(cl, cot_short, W, hl, n1, vec)
    go3, ga, gs1, vg1 = run_kc(W, a, b, inner, gf, hl, gs2, n1, r1, vec)
    go1, dx, gb = run_kd(short_lengths, long_lengths, xl, x_short, W, S, q8, k, v, ctx, lse, ga, gs1)
    m = lax.axis_index("mp")
    def spread(r):
        g = lax.all_gather(r, "mp")
        return jnp.concatenate([g[2], g[3][:512]], 0).reshape(9, 128, D), jnp.stack([g[0][:512], g[1][:512]], 0)
    ys, yl = spread(y); ds, dl = spread(dx)
    G = jnp.concatenate([go1, go3], 1).astype(F32)
    G = lax.psum_scatter(G, "mp", scatter_dimension=0, tiled=True)[0]
    G = lax.psum_scatter(G, "dp", scatter_dimension=1, tiled=True)
    vs = lax.psum(jnp.concatenate([vg2[:3], vg1[:3]], 0), "mp")
    vs = lax.psum_scatter(vs, "dp", scatter_dimension=1, tiled=True)
    gb = lax.psum_scatter(gb[:, :2, :192], "mp", scatter_dimension=0, tiled=True)[0]
    gb = jnp.transpose(gb.reshape(2, 3, 64), (2, 0, 1))
    gb = lax.psum_scatter(gb, "dp", scatter_dimension=0, tiled=True)
    gq = jnp.transpose(G[0][:, :576].reshape(-1, 3, 192), (0, 1, 2))
    return (ys, yl, ds, dl, gq, gb, G[0][:, 576:], vs[5], vs[3], vs[4], jnp.stack([G[1], G[2]], 1), G[3], vs[2], vs[0], vs[1])
def solution(mesh):
    fn = per_device if mesh.shape["dp"] == 8 else per_device_any
    d3 = P("dp", None, None)
    return jax.shard_map(fn, mesh=mesh,
        in_specs=(d3, d3, P("dp"), P("dp"), P("mp"), P(None, None, "mp"), P(None, None, "mp"), P(None, "mp"), P(), P(), P(), P(None, None, "mp"), P(None, "mp"), P(), P(), P(), d3, d3),
        out_specs=(d3, d3, d3, d3, P("dp", None, "mp"), P("dp", None, "mp"), P("dp", "mp"), P("dp"), P("dp"), P("dp"), P("dp", None, "mp"), P("dp", "mp"), P("dp"), P("dp"), P("dp")),
        check_vma=False)
```

time: 915 us -> 500 us (0.55); the launches traced: 905 us -> 500 us
  waiting for transfers between devices: 614 us -> 0 us
  Pallas kernels: 0 us -> 468 us
  matrix products: 109 us -> 0 us
  other arithmetic: 68 us -> 4.55 us
  local copies, waits for them, and re-layouts: 70.8 us -> 25.9 us
  blocking collectives: 24.9 us -> 0 us
  between operations: 16.6 us -> 0.93 us
    pallas_call x0 -> x6, Pallas kernels: none -> 468 us  [the longest x1 232 us: send_out(): pl.pallas_call(out_kernel, out_shape=[jax.ShapeDtypeStruct((4, PR, 768),...]
    psum x4 -> x0, waiting for transfers between devices: 437 us -> none  [the longest x2 256 us: post_norm(): lax.psum(partial_sum.astype(jnp.bfloat16).astype(jnp.float32).astype(jnp....]
    reduce_scatter x4 -> x0, waiting for transfers between devices: 178 us -> none  [the longest x1 48.7 us: per_device(): lax.psum_scatter(grad_w_up, 'dp', scatter_dimension=0, tiled=True)]
    dot_general x23 -> x0, matrix products: 104 us -> none  [the longest x1 13 us: per_device(): jnp.einsum('rd,rcf->dcf', hidden_low, grad_gate_up, preferred_element_typ...]
    reduce_sum x11 -> x0, other arithmetic: 33.5 us -> none  [the longest x2 9.23 us: layer_stats(): mean_vec = jnp.mean(totals, axis=1, keepdims=True)]
    unnamed x1 -> x0, blocking collectives: 24.9 us -> none
    convert_element_type x7 -> x0, other arithmetic: 24.8 us -> none  [the longest x1 15.9 us: per_device(): inner = gelu_gate(gate_rows, up_rows).astype(jnp.bfloat16)]
    reshape x10 -> x3, local copies, waits for them, and re-layouts: 14.4 us -> 0.25 us  [the longest x1 0.09 us: per_device(): gbr = jnp.transpose(gb[:, :2, :192], (1, 0, 2)).reshape(2, D)]
  transfers between devices with their start and end apart: 8 -> 0, of which waited for: 8 -> 0; matrix products, arithmetic and copies ran while one was open for 6% -> 0% of each run, Pallas kernels for 0% -> 0%
where the time goes in v1:
time: 500 us
  Pallas kernels  468 us (94%)
  local copies, waits for them, and re-layouts  25.9 us (5%)
    pallas_call x1, Pallas kernels, send_out(): pl.pallas_call(out_kernel, out_shape=[jax.ShapeDtypeStruct((4, PR, 768),...  232 us
    pallas_call x4, Pallas kernels, call(): pl.pallas_call(kernel, grid_spec=pltpu.PrefetchScalarGridSpec(num_scalar_...  156 us
    pallas_call x1, Pallas kernels, gather_weights(): pl.pallas_call(ag_kernel, out_shape=[jax.ShapeDtypeStruct((4, 4, 768, 768...  81.1 us

profile of v1, /device:TPU:0, one launch (start us, length us, event | category | flops | bytes accessed | tf_op | source)
XLA Modules:
  0.0 499.7 jit_solution(7932610355778454465)
XLA Ops:
  0.6 6.5 %fusion.1 = (bf16[768,1,768]{2,1,0:T(2,128)(2,1)S(1)}, bf16[768,1,768]{2,1,0:T(2,128)(2,1)S(1)}) fusion(bf16[768,2,768]{2,1,0:T(2,128)(2,1)} %param.31), kind=kLoop, calls=%fused_computation.25 | loop fusion | bytes 4718592 | tf_op jit(solution)/shard_map/slice | solution.py:633
  7.2 0.4 copy_bitcast_fusion
  7.6 0.7 copy-done.3
  8.5 0.5 copy-done.1
  9.0 2.5 pad_maximum_fusion.own
  11.5 0.6 compare_reduce_fusion
  12.1 0.7 fusion
  12.9 0.6 pad.9.small
  13.5 81.1 %gather_weights.1 = (bf16[4,4,768,768]{3,2,1,0:T(8,128)(2,1)}, f32[4,8,256]{2,1,0:T(8,128)}) custom-call(bf16[4,768,768]{2,1,0:T(8,128)(2,1)} %pad_maximum_fusion.own, f32[8,256]{1,0:T(8,128)} %pad.9.small), custom_call_target="tpu_custom_call" | custom-call | tf_op jit(solution)/shard_map/gather_weights/pallas_call | solution.py:427
  94.8 0.7 stack.44.vec
  95.4 32.6 %attention_forward.1 = (bf16[4,640,192]{2,1,0:T(8,128)(2,1)}, bf16[4,640,192]{2,1,0:T(8,128)(2,1)}, bf16[4,640,192]{2,1,0:T(8,128)(2,1)}, bf16[4,640,192]{2,1,0:...) custom-call(s32[9]{0:T(128)} %slen.3, s32[2]{0:T(128)} %llen.3, ...), custom_call_target="tpu_custom_call" | custom-call | tf_op jit(solution)/shard_map/attention_forward/pallas_call | solution.py:165
  128.0 27.8 %feed_forward.1 = (f32[4,640,768]{2,1,0:T(8,128)}, f32[4,640,768]{2,1,0:T(8,128)}, bf16[4,640,768]{2,1,0:T(8,128)(2,1)}, bf16[640,768]{1,0:T(8,128)(2,1)}, bf16[...) custom-call(bf16[8,128,768]{2,1,0:T(8,128)(2,1)} %bitcast.50, bf16[9,128,768]{2,1,0:T(8,128)(2,1)} %cs.1, ...), custom_call_target="tpu_custom_call" | custom-call | tf_op jit(solution)/shard_map/feed_forward/pallas_call | solution.py:165
  155.9 48.3 %feed_backward.1 = (bf16[4,3,768,768]{3,2,1,0:T(8,128)(2,1)}, bf16[640,768]{1,0:T(8,128)(2,1)}, f32[640,768]{1,0:T(8,128)}, f32[8,768]{1,0:T(8,128)}) custom-call(bf16[4,4,768,768]{3,2,1,0:T(8,128)(2,1)} %get-tuple-element.55.w.wg.wu.wd, bf16[4,4,768,768]{3,2,1,0:T(8,128)(2,1)} %get-tuple-element.55.w.wg.wu.wd, ...), custom_call_target="tpu_custom_call" | custom-call | tf_op jit(solution)/shard_map/feed_backward/pallas_call | solution.py:165
  204.2 46.9 %attention_backward.1 = (bf16[4,1,768,768]{3,2,1,0:T(8,128)(2,1)}, bf16[640,768]{1,0:T(8,128)(2,1)}, f32[4,8,256]{2,1,0:T(8,128)}) custom-call(s32[9]{0:T(128)} %slen.3, s32[2]{0:T(128)} %llen.3, bf16[8,128,768]{2,1,0:T(8,128)(2,1)} %bitcast.47, bf16[9,128,768]{2,1,0:T(8,128)(2,1)} %xs.3, bf16[4,4,768,768]{3,2,1,0:T(8,128)(2,1)} %get-tuple-element.55.w.wg.wu.wd, ...), custom_call_target="tpu_custom_call" | custom-call | tf_op jit(solution)/shard_map/attention_backward/pallas_call | solution.py:165
  251.0 0.8 slice_bitcast_fusion.4
  251.8 0.1 reshape.100
  251.9 0.6 pad_maximum_fusion.2.vin
  252.5 231.7 %send_out.1 = (f32[4,96,768]{2,1,0:T(8,128)}, bf16[17,128,768]{2,1,0:T(8,128)(2,1)}, bf16[17,128,768]{2,1,0:T(8,128)(2,1)}, f32[8,768]{1,0:T(8,128)}) custom-call(bf16[4,1,768,768]{3,2,1,0:T(8,128)(2,1)} %get-tuple-element.72.g1, bf16[4,3,768,768]{3,2,1,0:T(8,128)(2,1)} %get-tuple-element.73.g3, bf16[5,128,768]{2,1,0:T(8,128)(2,1)} %bitcast.53, ...), custom_call_target="tpu_custom_call" | custom-call | tf_op jit(solution)/shard_map/send_out/pallas_call | solution.py:616
  484.3 2.9 slice.91
  487.2 2.7 slice.92
  489.9 1.3 slice.93
  491.2 1.2 slice.94
  492.5 0.6 copy-done.2
  493.0 0.8 slice_bitcast_fusion
  493.9 0.1 copy.44
  494.0 0.9 copy.45
  494.9 0.7 slice.97
  495.8 0.6 copy.46
  496.4 0.7 slice.110
  497.1 0.8 constant_dynamic-slice_fusion
  497.9 0.5 slice_bitcast_fusion.5
  498.5 1.3 copy.47
  (44 shorter events, 0.5 us)
Async XLA Ops:
  7.2 1.2 copy-start.3
  7.2 1.2 copy-start.4
  7.6 1.4 copy-start.1
  9.0 3.2 copy-start.14
  9.0 3.8 copy-start.13
  13.5 81.2 %copy-start.7 = (f32[768]{0:T(1024)S(1)}, f32[768]{0:T(1024)}, u32[]{:S(2)}) copy-start(f32[768]{0:T(1024)} %param.28) | copy-start | bytes 9220
  13.5 81.2 %copy-start.8 = (f32[768]{0:T(1024)S(1)}, f32[768]{0:T(1024)}, u32[]{:S(2)}) copy-start(f32[768]{0:T(1024)} %param.29) | copy-start | bytes 9220
  13.5 81.2 %copy-start.9 = (f32[768]{0:T(1024)S(1)}, f32[768]{0:T(1024)}, u32[]{:S(2)}) copy-start(f32[768]{0:T(1024)} %param.30) | copy-start | bytes 9220
  13.5 81.2 %copy-start.10 = (f32[768]{0:T(1024)S(1)}, f32[768]{0:T(1024)}, u32[]{:S(2)}) copy-start(f32[768]{0:T(1024)} %param.33) | copy-start | bytes 9220
  13.5 81.2 %copy-start.11 = (f32[768]{0:T(1024)S(1)}, f32[768]{0:T(1024)}, u32[]{:S(2)}) copy-start(f32[768]{0:T(1024)} %param.34) | copy-start | bytes 9220
  13.5 81.3 %copy-start.12 = (f32[768]{0:T(1024)S(1)}, f32[768]{0:T(1024)}, u32[]{:S(2)}) copy-start(f32[768]{0:T(1024)} %param.35) | copy-start | bytes 9220
  204.1 47.8 %copy-start.6 = (f32[8,768]{1,0:T(8,128)S(1)}, f32[8,768]{1,0:T(8,128)}, u32[]{:S(2)}) copy-start(f32[8,768]{1,0:T(8,128)} %get-tuple-element.77) | copy-start | bytes 73732
  204.2 47.8 %copy-start.5 = (f32[8,768]{1,0:T(8,128)S(1)}, f32[8,768]{1,0:T(8,128)}, u32[]{:S(2)}) copy-start(f32[8,768]{1,0:T(8,128)} %get-tuple-element.76) | copy-start | bytes 73732
  484.3 5.6 %copy-start = (bf16[17,128,768]{2,1,0:T(8,128)(2,1)S(1)}, bf16[17,128,768]{2,1,0:T(8,128)(2,1)}, u32[]{:S(2)}) copy-start(bf16[17,128,768]{2,1,0:T(8,128)(2,1)} %get-tuple-element.80) | copy-start | bytes 10027012
  491.2 1.8 copy-start.2

commit v2 on v1

--- a/solution.py
+++ b/solution.py
@@ -120,7 +120,7 @@
 def norm_bwd(gn, normed, r):
     return r * (gn - jnp.mean(gn, axis=1, keepdims=True) - normed * jnp.mean(gn * normed, axis=1, keepdims=True))
 
-def row_tiles(fn, tile=128):
+def row_tiles(fn, tile=640):
     def body(i, u):
         fn(pl.ds(pl.multiple_of(i * tile, tile), tile)); return u
     lax.fori_loop(0, R // tile, body, 0)
@@ -222,7 +222,7 @@
         [pltpu.VMEM((R, D), F32), pltpu.VMEM((5, 128, D), BF16), pltpu.SemaphoreType.DMA],
         "feed_forward", (cl, cs, W, W, W, hl, n1, vec), prefetch=0)
 
-def kc(wg, wu, wd, a, b, inner, gf, hl, gs2, n1, r1, vec, go, gao, gs1o, vgo, acc, gft, hlt, gg):
+def kc(wg, wu, wd, a, b, inner, gf, hl, gs2, n1, r1, vec, go, gs1o, vgo, acc, gft, hlt, gg):
     z = pl.program_id(0)
     @pl.when(z == 0)
     def _():
@@ -241,7 +241,7 @@
         go[0, 2, rows, :] = nn(gft[rows, :], inner[0]).astype(BF16)
         go[0, 0, rows, :] = nn(hlt[rows, :], gg[0]).astype(BF16)
         go[0, 1, rows, :] = nn(hlt[rows, :], gg[1]).astype(BF16)
-    lax.fori_loop(0, 6, lambda i, u: (wtile(pl.ds(pl.multiple_of(i * 128, 128), 128)), u)[1], 0)
+    wtile(slice(0, D))
     @pl.when(z == 3)
     def _():
         tot = [jnp.zeros((1, D), F32)] * 3
@@ -250,14 +250,13 @@
             gh, n = acc[rows, :], n1[rows, :]
             gs = norm_bwd(gh * vec[1:2, :], n, r1[rows, 0:1])
             gs1o[rows, :] = gs
-            gao[rows, :] = gs.astype(BF16)
             tot = [tot[0] + jnp.sum(gh * n, axis=0, keepdims=True), tot[1] + jnp.sum(gh, axis=0, keepdims=True), tot[2] + jnp.sum(gs, axis=0, keepdims=True)]
         vgo[...] = jnp.concatenate(tot + [jnp.zeros((5, D), F32)], axis=0)
 
 def run_kc(W, a, b, inner, gf, hl, gs2, n1, r1, vec):
     c = lambda dt: const((R, D))
     return call(kc, [part(1), part(2), part(3), perz((R, D)), perz((R, D)), perz((R, D)), c(0), c(0), c(0), c(0), const((R, 128)), const((8, D))],
-        [(pl.BlockSpec((1, 3, D, D), lambda z: (z, 0, 0, 0)), sds((4, 3, D, D), BF16)), (const((R, D)), sds((R, D), BF16)), (const((R, D)), sds((R, D), F32)), (const((8, D)), sds((8, D), F32))],
+        [(pl.BlockSpec((1, 3, D, D), lambda z: (z, 0, 0, 0)), sds((4, 3, D, D), BF16)), (const((R, D)), sds((R, D), F32)), (const((8, D)), sds((8, D), F32))],
         [pltpu.VMEM((R, D), F32), pltpu.VMEM((D, R), BF16), pltpu.VMEM((D, R), BF16), pltpu.VMEM((2, R, D), BF16)],
         "feed_backward", (W, W, W, a, b, inner, gf, hl, gs2, n1, r1, vec), prefetch=0)
 
@@ -439,36 +438,113 @@
     e = 1 - ((z + 1) // 2) % 2
     return [z + 1 - 2 * (z % 2), e * ((z + 2) % 4) + (1 - e) * (3 - z), e * (3 - z) + (1 - e) * ((z + 2) % 4)]
 
-def out_kernel(g1, g3, yin, dxin, vin, gout, yout, dxout, vout,
-               r0, l0, rx, ry, rxy, ryx, rl, rr, stage, vr, vs,
-               s0s, s0r, s0l, s1s, s1r, s2s, s2r, ys, yr, vsem_s, vsem_r, loc):
+H = PR // 2
+
+def zo(g):
+    h, e = g // 2, g * (3 - g) // 2
+    return (1 - e) * (3 - 2 * h) + e * 2 * h
+
+def add_into(n, dst, src):
+    def body(i, u):
+        d, r = dst(i), src(i)
+        d[...] = (d[...].astype(F32) + r[...].astype(F32)).astype(BF16)
+        return u
+    lax.fori_loop(0, n, body, 0)
+
+def kx(slen, llen, xl, xs, w, small, q8, k, v, ctx, lse, gs1, g3, yin, vin, gout, yout, dxout, vout,
+       xb, dm, kt, gc, gqt, gk, gv, ga, gat, xt, acc, gob, dxs, gbs, stage, vr, vs, l0,
+       r03, rx3, ry3, rxy3, ryx3, rl3, rr3, r01, rx1, ry1, rxy1, ryx1, rl1, rr1,
+       sem, s0s, s0r, s0l, s1s, s1r, s2s, s2r, ys, yr, vsem_s, vsem_r, loc):
+    g = pl.program_id(0)
     dp, y, x, c, z = place()
     xn, yn, cn = dpi(y, 1 - x, c), dpi(1 - y, x, c), dpi(y, x, 1 - c)
     z1, z2 = z + 1 - 2 * (z % 2), (z + 2) % 4
-    barrier_all([(xn, z), (yn, z), (cn, z)] + [(dp, (z + k) % 4) for k in (1, 2, 3)])
-
+    parts = (1, 3)
+    r0, rx, ry, rxy, ryx, rl, rr = (r01, r03), (rx1, rx3), (ry1, ry3), (rxy1, rxy3), (ryx1, ryx3), (rl1, rl3), (rr1, rr3)
     def rows(p): return pl.ds(pl.multiple_of(p * PR, 32), PR)
     def rc(src, dst, ss, rs, dev):
         return pltpu.make_async_remote_copy(src_ref=src, dst_ref=dst, send_sem=ss, recv_sem=rs, device_id=dev, device_id_type=MESH)
-    def st0(zz, q):
-        p = dpi(q // 2, q % 2, 1 - c)
-        return [rc(g1.at[zz, :, rows(p), :], r0.at[zz, q, pl.ds(0, 1)], s0s.at[zz, q, 0], s0r.at[zz, q, 0], (cn, z)),
-                rc(g3.at[zz, :, rows(p), :], r0.at[zz, q, pl.ds(1, 3)], s0s.at[zz, q, 1], s0r.at[zz, q, 1], (cn, z))]
+    def blk(kd, zz, q):
+        return l0.at[zz, q] if kd else gob.at[zz, :, rows(2 * q + c), :]
+    def half(kd, zz, q, h):
+        return l0.at[zz, q, :, pl.ds(h * H, H), :] if kd else gob.at[zz, :, pl.ds(pl.multiple_of((2 * q + c) * PR + h * H, 16), H), :]
+    def st0(kd, zz, q):
+        src = (g3 if kd else gob).at[zz, :, rows(2 * q + 1 - c), :]
+        return rc(src, r0[kd].at[zz, q], s0s.at[kd, zz, q], s0r.at[kd, zz, q], (cn, z))
     def ld0(zz, q):
-        p = dpi(q // 2, q % 2, c)
-        return [pltpu.make_async_copy(g1.at[zz, :, rows(p), :], l0.at[zz, q, pl.ds(0, 1)], s0l.at[zz, q, 0]),
-                pltpu.make_async_copy(g3.at[zz, :, rows(p), :], l0.at[zz, q, pl.ds(1, 3)], s0l.at[zz, q, 1])]
+        return pltpu.make_async_copy(g3.at[zz, :, rows(2 * q + c), :], l0.at[zz, q], s0l.at[zz, q])
+    def stage_0(kd, zz):
+        for q in range(4):
+            st0(kd, zz, q).start()
+            if kd: ld0(zz, q).start()
+    def stage_a(kd, zz):
+        for q in range(4):
+            st0(kd, zz, q).wait_recv()
+            if kd: ld0(zz, q).wait()
+        n = parts[kd]
+        add_into(4 * n, lambda i: blk(kd, zz, i // n).at[i % n], lambda i: r0[kd].at[zz, i // n, i % n])
+        for j in range(2):
+            s1x(kd, zz, j).start(); s1y(kd, zz, j).start()
+    def s1x(kd, zz, j):
+        return rc(half(kd, zz, 2 * j + 1 - x, 0), rx[kd].at[zz, j], s1s.at[kd, zz, j], s1r.at[kd, zz, j], (xn, z))
+    def s1y(kd, zz, j):
+        return rc(half(kd, zz, 2 * (1 - y) + j, 1), ry[kd].at[zz, j], s1s.at[kd, zz, 2 + j], s1r.at[kd, zz, 2 + j], (yn, z))
+    def s1xy(kd, zz):
+        return rc(half(kd, zz, 2 * (1 - y) + x, 0), rxy[kd].at[zz], s1s.at[kd, zz, 4], s1r.at[kd, zz, 4], (yn, z))
+    def s1yx(kd, zz):
+        return rc(half(kd, zz, 2 * y + 1 - x, 1), ryx[kd].at[zz], s1s.at[kd, zz, 5], s1r.at[kd, zz, 5], (xn, z))
+    def stage_b(kd, zz):
+        n = parts[kd]
+        for j in range(2): s1x(kd, zz, j).wait_recv()
+        add_into(2 * n, lambda i: half(kd, zz, 2 * (i // n) + x, 0).at[i % n], lambda i: rx[kd].at[zz, i // n, i % n])
+        s1xy(kd, zz).start()
+        for j in range(2): s1y(kd, zz, j).wait_recv()
+        add_into(2 * n, lambda i: half(kd, zz, 2 * y + i // n, 1).at[i % n], lambda i: ry[kd].at[zz, i // n, i % n])
+        s1yx(kd, zz).start()
+    def stage_c(kd, zz):
+        n = parts[kd]
+        s1xy(kd, zz).wait_recv()
+        add_into(n, lambda i: half(kd, zz, 2 * y + x, 0).at[i], lambda i: rxy[kd].at[zz, i])
+        s1yx(kd, zz).wait_recv()
+        add_into(n, lambda i: half(kd, zz, 2 * y + x, 1).at[i], lambda i: ryx[kd].at[zz, i])
+    def mine(kd, zz): return blk(kd, zz, 2 * y + x)
+    def zs(kd, zz, right):
+        return rc(mine(kd, zz), (rl if right else rr)[kd].at[zz], s2s.at[kd, zz], s2r.at[kd, zz, 0 if right else 1], (dp, z + 1 if right else z - 1))
+    def stage_d(kd, zz, hop):
+        n = parts[kd]
+        if hop < zz:
+            @pl.when(z == hop)
+            def _():
+                if hop > 0:
+                    zs(kd, zz, True).wait_recv()
+                    add_into(n, lambda i: mine(kd, zz).at[i], lambda i: rl[kd].at[zz, i])
+                zs(kd, zz, True).start()
+        if 3 - hop > zz:
+            @pl.when(z == 3 - hop)
+            def _():
+                if hop > 0:
+                    zs(kd, zz, False).wait_recv()
+                    add_into(n, lambda i: mine(kd, zz).at[i], lambda i: rr[kd].at[zz, i])
+                zs(kd, zz, False).start()
+        if hop == max(zz, 3 - zz):
+            @pl.when(z == zz)
+            def _():
+                if zz > 0: zs(kd, zz, True).wait_recv()
+                if zz < 3: zs(kd, zz, False).wait_recv()
+                def body(i, u):
+                    t = mine(kd, zz)[i].astype(F32)
+                    if zz > 0: t += rl[kd][zz, i].astype(F32)
+                    if zz < 3: t += rr[kd][zz, i].astype(F32)
+                    gout[kd + i] = t
+                    return u
+                lax.fori_loop(0, n, body, 0)
     order = far_order(z)
-    def blk(s): return 4 * s + s // 3
-    def yc(t, src, s, half, right):
-        buf = (yout, dxout)[t]
-        n, off = (4, 0) if half == 0 else (1, 4)
-        dst = buf.at[pl.ds(blk(s) + off, n)]
-        if src is None:
-            src = dst
-        else:
-            src = src.at[pl.ds(off, n)]
-        return rc(src, dst, ys.at[t, s, half, right], yr.at[t, s, half], (dp, z + 1 if right else z - 1))
+    def yb(s): return 4 * s + s // 3
+    def yc(t, src, s, hf, right):
+        n, off = (4, 0) if hf == 0 else (1, 4)
+        dst = (yout, dxout)[t].at[pl.ds(yb(s) + off, n)]
+        src = dst if src is None else src.at[pl.ds(off, n)]
+        return rc(src, dst, ys.at[t, s, hf, right], yr.at[t, s, hf], (dp, z + 1 if right else z - 1))
     def ysend(t, src, s, act):
         for right in (1, 0):
             @pl.when((s <= z) & (z < 3) if right else (s >= z) & (z > 0))
@@ -484,145 +560,129 @@
         def _():
             yc(t, None, s, 1, 1).wait_recv()
         ysend(t, None, s, "start")
+    def own(t, hf, way):
+        n, off = (4, 0) if hf == 0 else (1, 4)
+        if way == 0:
+            return pltpu.make_async_copy(yin.at[pl.ds(off, n)], stage.at[pl.ds(off, n)], loc.at[t, hf, 0])
+        return pltpu.make_async_copy((stage, dxs)[t].at[pl.ds(off, n)], (yout, dxout)[t].at[pl.ds(yb(z) + off, n)], loc.at[t, hf, 1])
+    def ownall(fn):
+        fn(0)
+        @pl.when(z == 2)
+        def _():
+            fn(1)
     vpeer = [(cn, z), (xn, z), (yn, z), (dp, z1), (dp, z2)]
-    def vstart(i): rc(vs.at[i], vr.at[i], vsem_s.at[i], vsem_r.at[i], vpeer[i]).start()
+    def vcopy(i): return rc(vs.at[i], vr.at[i], vsem_s.at[i], vsem_r.at[i], vpeer[i])
     def vstep(i):
-        rc(vs.at[i], vr.at[i], vsem_s.at[i], vsem_r.at[i], vpeer[i]).wait_recv()
+        vcopy(i).wait_recv()
         tot = vs[i] + vr[i]
         if i < 4:
             vs[i + 1] = tot
-            vstart(i + 1)
+            vcopy(i + 1).start()
         else:
             vout[...] = tot
-
-    for q in range(4):
-        for d in st0(ZO[0], q): d.start()
-        for d in ld0(ZO[0], q): d.start()
-    for t, src in enumerate((yin, dxin)):
-        ysend(t, src, z, "start")
-    for zz in ZO[1:]:
-        for q in range(4):
-            for d in st0(zz, q): d.start()
-            for d in ld0(zz, q): d.start()
-    def own(t, which, way):
-        n, off = (4, 0) if which == 0 else (1, 4)
-        src = (yin, dxin)[t]
-        dst = (yout, dxout)[t]
-        if way == 0:
-            return pltpu.make_async_copy(src.at[pl.ds(off, n)], stage.at[t, pl.ds(off, n)], loc.at[t, which, 0])
-        return pltpu.make_async_copy(stage.at[t, pl.ds(off, n)], dst.at[pl.ds(blk(z) + off, n)], loc.at[t, which, 1])
-    def ownall(fn):
-        for t in (0, 1):
-            fn(t, 0)
-            @pl.when(z == 2)
-            def _():
-                fn(t, 1)
-    ownall(lambda t, w: own(t, w, 0).start())
-    vs[0] = vin[...]
-    vstart(0)
-
-    def addinto(dst, src):
-        dst[...] = (dst[...].astype(F32) + src[...].astype(F32)).astype(BF16)
-    def stage_a(zz):
-        for q in range(4):
-            for d in st0(zz, q): d.wait_recv()
-            for d in ld0(zz, q): d.wait()
-        def body(q, u):
-            for t in range(4):
-                addinto(l0.at[zz, q, t], r0.at[zz, q, t])
-            return u
-        lax.fori_loop(0, 4, body, 0)
-        for k in range(2):
-            s1x(zz, k).start(); s1y(zz, k).start()
-    def s1x(zz, k):
-        return rc(l0.at[zz, 2 * k + 1 - x, pl.ds(0, 2)], rx.at[zz, k], s1s.at[zz, k], s1r.at[zz, k], (xn, z))
-    def s1y(zz, k):
-        return rc(l0.at[zz, 2 * (1 - y) + k, pl.ds(2, 2)], ry.at[zz, k], s1s.at[zz, 2 + k], s1r.at[zz, 2 + k], (yn, z))
-    def s1xy(zz):
-        return rc(l0.at[zz, 2 * (1 - y) + x, pl.ds(0, 2)], rxy.at[zz], s1s.at[zz, 4], s1r.at[zz, 4], (yn, z))
-    def s1yx(zz):
-        return rc(l0.at[zz, 2 * y + 1 - x, pl.ds(2, 2)], ryx.at[zz], s1s.at[zz, 5], s1r.at[zz, 5], (xn, z))
-    def stage_b(zz):
-        for k in range(2):
-            s1x(zz, k).wait_recv()
-            for t in range(2):
-                addinto(l0.at[zz, 2 * k + x, t], rx.at[zz, k, t])
-        s1xy(zz).start()
-        for k in range(2):
-            s1y(zz, k).wait_recv()
-            for t in range(2):
-                addinto(l0.at[zz, 2 * y + k, 2 + t], ry.at[zz, k, t])
-        s1yx(zz).start()
-    def mine(zz): return l0.at[zz, 2 * y + x]
-    def stage_c(zz):
-        s1xy(zz).wait_recv()
-        for t in range(2): addinto(mine(zz).at[t], rxy.at[zz, t])
-        s1yx(zz).wait_recv()
-        for t in range(2): addinto(mine(zz).at[2 + t], ryx.at[zz, t])
-    def zs(zz, right):
-        return rc(mine(zz), (rl if right else rr).at[zz], s2s.at[zz], s2r.at[zz, 0 if right else 1], (dp, z + 1 if right else z - 1))
-    def stage_d(zz):
-        @pl.when(z < zz)
-        def _():
-            @pl.when(z > 0)
-            def _():
-                zs(zz, True).wait_recv()
-                for t in range(4): addinto(mine(zz).at[t], rl.at[zz, t])
-            zs(zz, True).start()
-        @pl.when(z > zz)
-        def _():
-            @pl.when(z < 3)
-            def _():
-                zs(zz, False).wait_recv()
-                for t in range(4): addinto(mine(zz).at[t], rr.at[zz, t])
-            zs(zz, False).start()
-        @pl.when(z == zz)
-        def _():
-            for t in range(4): gout[t] = mine(zz)[t].astype(F32)
-            if zz > 0:
-                zs(zz, True).wait_recv()
-                for t in range(4): gout[t] += rl[zz, t].astype(F32)
-            if zz < 3:
-                zs(zz, False).wait_recv()
-                for t in range(4): gout[t] += rr[zz, t].astype(F32)
-    A, B, C, Dd = stage_a, stage_b, stage_c, stage_d
-    a, b, cc, d = ZO
-    A(a); vstep(0); A(b); yarr(0, 0); B(a); vstep(1); A(cc); C(a); A(d)
-    ownall(lambda t, w: (own(t, w, 0).wait(), own(t, w, 1).start()))
-    vstep(2); yarr(0, 1); B(b); Dd(a); vstep(3); C(b); B(cc); yarr(0, 2); Dd(b); yarr(1, 0); C(cc); vstep(4); B(d); Dd(cc); C(d); yarr(1, 1); Dd(d); yarr(1, 2)
-    for zz in ZO:
-        for q in range(4):
-            for dd in st0(zz, q): dd.wait_send()
-        for k in range(2):
-            s1x(zz, k).wait_send(); s1y(zz, k).wait_send()
-        s1xy(zz).wait_send(); s1yx(zz).wait_send()
-        @pl.when(z < zz)
-        def _(): zs(zz, True).wait_send()
-        @pl.when(z > zz)
-        def _(): zs(zz, False).wait_send()
-    for t, src in enumerate((yin, dxin)):
-        ysend(t, src, z, "wait_send")
-        for j in range(3):
-            ysend(t, None, order[j], "wait_send")
-    for i in range(5):
-        rc(vs.at[i], vr.at[i], vsem_s.at[i], vsem_r.at[i], vpeer[i]).wait_send()
-    ownall(lambda t, w: own(t, w, 1).wait())
-
-def send_out(g1, g3, yv, dxv, vec):
-    A = pl.BlockSpec(memory_space=pl.ANY)
-    V = pl.BlockSpec(memory_space=pltpu.VMEM)
-    S = pltpu.SemaphoreType.DMA
-    b = lambda *s: pltpu.VMEM(s + (PR, 768), BF16)
+    F, T, o = 1, 0, ZO
+    def S0(kd, u): stage_0(kd, o[u])
+    def A(kd, u): stage_a(kd, o[u])
+    def B(kd, u): stage_b(kd, o[u])
+    def C(kd, u): stage_c(kd, o[u])
+    def Z(kd, u, hop): stage_d(kd, o[u], hop)
+
+    @pl.when(g == 0)
+    def _():
+        barrier_all([(xn, z), (yn, z), (cn, z)] + [(dp, (z + j) % 4) for j in (1, 2, 3)])
+        S0(F, 0)
+        ysend(0, yin, z, "start")
+        ownall(lambda h: own(0, h, 0).start())
+        for j in (1, 2, 3): S0(F, j)
+        cg = pltpu.make_async_copy(gs1, acc, sem.at[1]); cg.start()
+        load_rows(z, xl, xs, xb, sem.at[0])
+        distances(z, slen, llen, dm)
+        xt[...] = xb[...].reshape(R, D).T
+        gbs[...] = jnp.zeros_like(gbs)
+        cg.wait()
+        ga[...] = acc[...].astype(BF16)
+        gat[...] = ga[...].T
+        ownall(lambda h: (own(0, h, 0).wait(), own(0, h, 1).start()))
+    wz, sm = w.at[0, 0], small.at[0]
+    gc[...] = nt(ga[...], wz[576:768, :]).astype(BF16)
+    kt[...] = k[0].T
+    attend_bwd(z, sm, q8.at[0], k.at[0], v.at[0], kt, gc, dm, lse.at[0], gqt, gk, gv)
+    @pl.when(g == 0)
+    def _(): A(F, 0)
+    @pl.when(g == 1)
+    def _(): A(T, 0); B(F, 0)
+    @pl.when(g == 2)
+    def _(): A(T, 1); B(F, 1); C(F, 0); Z(F, 0, 0)
+    @pl.when(g == 3)
+    def _(): A(T, 2); B(F, 2); C(F, 1); Z(F, 0, 1); Z(F, 1, 0)
+    zg = zo(g)
+    dq = gqt[...].astype(BF16).T
+    dk = gk[...].astype(BF16)
+    dv = gv[...].astype(BF16)
+    gbs[zg, 0:1, 0:192] = jnp.sum(dq.astype(F32), axis=0, keepdims=True)
+    gbs[zg, 1:2, 0:192] = jnp.sum(dv.astype(F32), axis=0, keepdims=True)
+    acc[...] += nn(dq, wz[0:192, :]) + nn(dk, wz[192:384, :]) + nn(dv, wz[384:576, :])
+    @pl.when(g == 3)
+    def _():
+        for i in range(5):
+            dxs[i] = acc[128 * i:128 * i + 128, :].astype(BF16)
+        ysend(1, dxs, z, "start")
+        ownall(lambda h: own(1, h, 1).start())
+        vs[0] = vin[...]
+        for i in range(4):
+            vs[0, 6 + 2 * i:8 + 2 * i, 0:192] = gbs[i, 0:2, 0:192]
+        vcopy(0).start()
+    for i in range(6):
+        rw = slice(128 * i, 128 * i + 128)
+        gob[zg, 0, rw, :] = jnp.concatenate([nn(xt[rw, :], dq), nn(xt[rw, :], dk), nn(xt[rw, :], dv), nn(gat[rw, :], ctx[0])], axis=1).astype(BF16)
+    @pl.when(g == 0)
+    def _(): S0(T, 0); A(F, 1)
+    @pl.when(g == 1)
+    def _(): S0(T, 1); A(F, 2); yarr(0, 0)
+    @pl.when(g == 2)
+    def _(): S0(T, 2); A(F, 3); B(T, 0); yarr(0, 1)
+    @pl.when(g == 3)
+    def _():
+        S0(T, 3); C(T, 0); B(T, 1); Z(T, 0, 0); yarr(0, 2); vstep(0); A(T, 3); Z(F, 0, 2); Z(F, 1, 1); B(F, 3); C(F, 2); Z(F, 2, 0)
+        B(T, 2); C(T, 1); Z(T, 1, 0); Z(T, 0, 1); vstep(1); B(T, 3); yarr(1, 0); Z(F, 0, 3); Z(F, 1, 2); Z(F, 2, 1); C(F, 3); Z(F, 3, 0); vstep(2)
+        C(T, 2); Z(T, 2, 0); C(T, 3); Z(T, 3, 0); Z(T, 0, 2); Z(T, 1, 1); yarr(1, 1); vstep(3); Z(F, 1, 3); Z(F, 2, 2); Z(F, 3, 1)
+        Z(T, 1, 2); Z(T, 2, 1); Z(T, 3, 1); Z(T, 0, 3); Z(T, 1, 3); Z(F, 3, 2); Z(T, 2, 2); Z(T, 3, 2); vstep(4); yarr(1, 2)
+        for kd in (0, 1):
+            for zz in ZO:
+                for q in range(4): st0(kd, zz, q).wait_send()
+                for j in range(2):
+                    s1x(kd, zz, j).wait_send(); s1y(kd, zz, j).wait_send()
+                s1xy(kd, zz).wait_send(); s1yx(kd, zz).wait_send()
+                @pl.when(z < zz)
+                def _(): zs(kd, zz, True).wait_send()
+                @pl.when(z > zz)
+                def _(): zs(kd, zz, False).wait_send()
+        for t, src in enumerate((yin, dxs)):
+            ysend(t, src, z, "wait_send")
+            for j in range(3):
+                ysend(t, None, order[j], "wait_send")
+            ownall(lambda h: own(t, h, 1).wait())
+        for i in range(5): vcopy(i).wait_send()
+
+def run_kx(slen, llen, xl, xs, W, small, q8, k, v, ctx, lse, gs1, g3, yv, vec):
+    pz = lambda *s: pl.BlockSpec((1,) + s, lambda g, *_: (zo(g),) + (0,) * len(s))
+    rz = lambda: pz(R, E)
+    V, S = pltpu.VMEM, pltpu.SemaphoreType.DMA
+    b = lambda *s: V(s + (PR, D), BF16)
+    h = lambda *s: V(s + (H, D), BF16)
+    bufs = lambda n: [b(4, 4, n), h(4, 2, n), h(4, 2, n), h(4, n), h(4, n), b(4, n), b(4, n)]
+    scratch = [V((5, 128, D), BF16), V((5, 512, 128), F32), V((E, R), BF16), V((R, E), BF16), V((E, R), F32), V((R, E), F32), V((R, E), F32),
+               V((R, D), BF16), V((D, R), BF16), V((D, R), BF16), V((R, D), F32), V((4, 1, D, D), BF16), V((5, 128, D), BF16), V((4, 8, 256), F32),
+               V((5, 128, D), BF16), V((5, 16, D), F32), V((5, 16, D), F32), b(4, 4, 3)] + bufs(3) + bufs(1) + [
+               S((2,)), S((2, 4, 4)), S((2, 4, 4)), S((4, 4)), S((2, 4, 6)), S((2, 4, 6)), S((2, 4)), S((2, 4, 2)), S((2, 4, 2, 2)), S((2, 4, 2)), S((5,)), S((5,)), S((2, 2, 2))]
     return pl.pallas_call(
-        out_kernel,
-        out_shape=[jax.ShapeDtypeStruct((4, PR, 768), F32), jax.ShapeDtypeStruct((17, 128, 768), BF16), jax.ShapeDtypeStruct((17, 128, 768), BF16), jax.ShapeDtypeStruct((8, 768), F32)],
-        in_specs=[A, A, A, A, V], out_specs=[V, A, A, V],
-        scratch_shapes=[b(4, 4, 4), b(4, 4, 4), b(4, 2, 2), b(4, 2, 2), b(4, 2), b(4, 2), b(4, 4), b(4, 4), pltpu.VMEM((2, 5, 128, 768), BF16),
-                        pltpu.VMEM((5, 8, 768), F32), pltpu.VMEM((5, 8, 768), F32),
-                        S((4, 4, 2)), S((4, 4, 2)), S((4, 4, 2)), S((4, 6)), S((4, 6)), S((4,)), S((4, 2)), S((2, 4, 2, 2)), S((2, 4, 2)), S((5,)), S((5,)), S((2, 2, 2))],
-        compiler_params=pltpu.CompilerParams(collective_id=1, has_side_effects=True, vmem_limit_bytes=60 << 20),
-        name="send_out",
-    )(g1, g3, yv, dxv, vec)
+        kx,
+        grid_spec=pltpu.PrefetchScalarGridSpec(num_scalar_prefetch=2, grid=(4,),
+            in_specs=[ANY, ANY, pl.BlockSpec((1, 1, D, D), lambda g, *_: (zo(g), 0, 0, 0)), pz(8, 256), rz(), rz(), rz(), rz(), pz(8, R), ANY, ANY, ANY, const((16, D))],
+            out_specs=[const((4, PR, D)), ANY, ANY, const((16, D))], scratch_shapes=scratch),
+        out_shape=[sds((4, PR, D), F32), sds((17, 128, D), BF16), sds((17, 128, D), BF16), sds((16, D), F32)],
+        compiler_params=pltpu.CompilerParams(dimension_semantics=("arbitrary",), collective_id=1, has_side_effects=True, vmem_limit_bytes=VM),
+        name="attention_backward_send")(slen, llen, xl, xs, W, small, q8, k, v, ctx, lse, gs1, g3, yv, vec)
 
 def alibi_slopes(slope_index, head_total):
     power = 1 << head_total.bit_length() - 1
@@ -642,13 +702,11 @@
     xl, cl = x_long.reshape(8, 128, D), cot_long.reshape(8, 128, D)
     q8, k, v, ctx, lse, n1, r1, hl = run_ka(short_lengths, long_lengths, xl, x_short, W, S, vec)
     a, b, inner, y, gf, gs2, vg2 = run_kb(cl, cot_short, W, hl, n1, vec)
-    go3, ga, gs1, vg1 = run_kc(W, a, b, inner, gf, hl, gs2, n1, r1, vec)
-    go1, dx, gb = run_kd(short_lengths, long_lengths, xl, x_short, W, S, q8, k, v, ctx, lse, ga, gs1)
+    go3, gs1, vg1 = run_kc(W, a, b, inner, gf, hl, gs2, n1, r1, vec)
     m, dpx = lax.axis_index("mp"), lax.axis_index("dp")
-    gbr = jnp.transpose(gb[:, :2, :192], (1, 0, 2)).reshape(2, D)
-    vsum = jnp.concatenate([vg2[:3], vg1[:3], gbr], 0)
-    G, Y, DX, vs = send_out(go1, go3, y.reshape(5, 128, D), dx.reshape(5, 128, D), vsum)
-    b = lax.dynamic_slice(vs[6:8].reshape(2, 12, 64), (0, 3 * m, 8 * dpx), (2, 3, 8))
+    vsum = jnp.concatenate([vg2[:3], vg1[:3], jnp.zeros((10, D), F32)], 0)
+    G, Y, DX, vs = run_kx(short_lengths, long_lengths, xl, x_short, W, S, q8, k, v, ctx, lse, gs1, go3, y.reshape(5, 128, D), vsum)
+    b = lax.dynamic_slice(vs[6:14, :192].reshape(4, 2, 3, 64), (m, 0, 0, 8 * dpx), (1, 2, 3, 8))[0]
     vs = lax.dynamic_slice(vs[:6], (0, 96 * dpx), (6, 96))
     gq = G[0][:, :576].reshape(-1, 3, 192)
     return (Y[8:], Y[:8].reshape(2, 512, D), DX[8:], DX[:8].reshape(2, 512, D), gq, jnp.transpose(b, (2, 0, 1)), G[0][:, 576:], vs[5], vs[3], vs[4], jnp.stack([G[1], G[2]], 1), G[3], vs[2], vs[0], vs[1])
@@ -659,8 +717,8 @@
     xl, cl = x_long.reshape(8, 128, D), cot_long.reshape(8, 128, D)
     q8, k, v, ctx, lse, n1, r1, hl = run_ka(short_lengths, long_lengths, xl, x_short, W, S, vec)
     a, b, inner, y, gf, gs2, vg2 = run_kb(cl, cot_short, W, hl, n1, vec)
-    go3, ga, gs1, vg1 = run_kc(W, a, b, inner, gf, hl, gs2, n1, r1, vec)
-    go1, dx, gb = run_kd(short_lengths, long_lengths, xl, x_short, W, S, q8, k, v, ctx, lse, ga, gs1)
+    go3, gs1, vg1 = run_kc(W, a, b, inner, gf, hl, gs2, n1, r1, vec)
+    go1, dx, gb = run_kd(short_lengths, long_lengths, xl, x_short, W, S, q8, k, v, ctx, lse, gs1.astype(BF16), gs1)
     m = lax.axis_index("mp")
     def spread(r):
         g = lax.all_gather(r, "mp")

time: 500 us -> 360 us (0.72)
  Pallas kernels: 468 us -> 329 us
    pallas_call x1, Pallas kernels: 232 us -> 162 us  [run_kx(): pl.pallas_call(kx, grid_spec=pltpu.PrefetchScalarGridSpec(num_scalar_pref...]
    pallas_call x4 -> x3, Pallas kernels: 156 us -> 86.5 us  [call(): pl.pallas_call(kernel, grid_spec=pltpu.PrefetchScalarGridSpec(num_scalar_...]
where the time goes in v2:
time: 360 us; the launch traced here: 359 us
  Pallas kernels  329 us (91%)
  local copies, waits for them, and re-layouts  24.4 us (7%)
  other arithmetic  4.63 us (1%)
    pallas_call x1, Pallas kernels, run_kx(): pl.pallas_call(kx, grid_spec=pltpu.PrefetchScalarGridSpec(num_scalar_pref...  162 us
    pallas_call x3, Pallas kernels, call(): pl.pallas_call(kernel, grid_spec=pltpu.PrefetchScalarGridSpec(num_scalar_...  86.5 us
    pallas_call x1, Pallas kernels, gather_weights(): pl.pallas_call(ag_kernel, out_shape=[jax.ShapeDtypeStruct((4, 4, 768, 768...  81.1 us

profile of v2, /device:TPU:0, one launch (start us, length us, event | category | flops | bytes accessed | tf_op | source)
XLA Modules:
  0.0 359.4 jit_solution(18295922660599657543)
XLA Ops:
  0.6 6.5 %fusion.1 = (bf16[768,1,768]{2,1,0:T(2,128)(2,1)S(1)}, bf16[768,1,768]{2,1,0:T(2,128)(2,1)S(1)}) fusion(bf16[768,2,768]{2,1,0:T(2,128)(2,1)} %param.31), kind=kLoop, calls=%fused_computation.25 | loop fusion | bytes 4718592 | tf_op jit(solution)/shard_map/slice | solution.py:693
  7.2 0.4 copy_bitcast_fusion
  7.6 0.7 copy-done.3
  8.4 0.1 maximum_bitcast_fusion
  8.5 0.5 copy-done.1
  9.0 2.5 pad_maximum_fusion.own
  11.5 0.6 compare_reduce_fusion
  12.1 0.7 fusion
  12.8 0.1 reshape.89
  12.9 0.6 pad.9.small
  13.5 81.1 %gather_weights.1 = (bf16[4,4,768,768]{3,2,1,0:T(8,128)(2,1)}, f32[4,8,256]{2,1,0:T(8,128)}) custom-call(bf16[4,768,768]{2,1,0:T(8,128)(2,1)} %pad_maximum_fusion.own, f32[8,256]{1,0:T(8,128)} %pad.9.small), custom_call_target="tpu_custom_call" | custom-call | tf_op jit(solution)/shard_map/gather_weights/pallas_call | solution.py:426
  94.8 0.7 stack.44.vec
  95.4 32.6 %attention_forward.1 = (bf16[4,640,192]{2,1,0:T(8,128)(2,1)}, bf16[4,640,192]{2,1,0:T(8,128)(2,1)}, bf16[4,640,192]{2,1,0:T(8,128)(2,1)}, bf16[4,640,192]{2,1,0:...) custom-call(s32[9]{0:T(128)} %slen.3, s32[2]{0:T(128)} %llen.3, ...), custom_call_target="tpu_custom_call" | custom-call | tf_op jit(solution)/shard_map/attention_forward/pallas_call | solution.py:165
  128.0 22.1 %feed_forward.1 = (f32[4,640,768]{2,1,0:T(8,128)}, f32[4,640,768]{2,1,0:T(8,128)}, bf16[4,640,768]{2,1,0:T(8,128)(2,1)}, bf16[640,768]{1,0:T(8,128)(2,1)}, bf16[...) custom-call(bf16[8,128,768]{2,1,0:T(8,128)(2,1)} %bitcast.49, bf16[9,128,768]{2,1,0:T(8,128)(2,1)} %cs.1, ...), custom_call_target="tpu_custom_call" | custom-call | tf_op jit(solution)/shard_map/feed_forward/pallas_call | solution.py:165
  150.2 31.8 %feed_backward.1 = (bf16[4,3,768,768]{3,2,1,0:T(8,128)(2,1)}, f32[640,768]{1,0:T(8,128)}, f32[8,768]{1,0:T(8,128)}) custom-call(bf16[4,4,768,768]{3,2,1,0:T(8,128)(2,1)} %get-tuple-element.51.w.wg.wu.wd, bf16[4,4,768,768]{3,2,1,0:T(8,128)(2,1)} %get-tuple-element.51.w.wg.wu.wd, bf16[4,4,768,768]{3,2,1,0:T(8,128)(2,1)} %get-tuple-element.51.w.wg.wu.wd, ...), custom_call_target="tpu_custom_call" | custom-call | tf_op jit(solution)/shard_map/feed_backward/pallas_call | solution.py:165
  182.0 0.7 slice.86
  182.7 0.1 pad.14.clone
  182.8 0.7 maximum_maximum_fusion.vin
  183.5 161.9 %attention_backward_send.1 = (f32[4,96,768]{2,1,0:T(8,128)}, bf16[17,128,768]{2,1,0:T(8,128)(2,1)}, bf16[17,128,768]{2,1,0:T(8,128)(2,1)}, f32[16,768]{1,0:T(8,128)}) custom-call(s32[9]{0:T(128)} %slen.3, s32[2]{0:T(128)} %llen.3, bf16[8,128,768]{2,1,0:T(8,128)(2,1)} %bitcast.46, bf16[9,128,768]{2,1,0:T(8,128)(2,1)} %xs.3, ...), custom_call_target="tpu_custom_call" | custom-call | tf_op jit(solution)/shard_map/attention_backward_send/pallas_call | solution.py:678
  345.4 2.9 slice.87
  348.3 2.7 slice.88
  351.0 1.3 slice.89
  352.3 1.2 slice.90
  353.5 0.6 copy-done.2
  354.1 0.8 slice_bitcast_fusion
  355.0 0.1 copy.42
  355.1 0.9 copy.44
  356.0 0.1 reshape.96
  356.1 0.6 copy.51
  356.7 0.7 slice.106
  357.5 0.5 slice_bitcast_fusion.4
  358.1 1.3 copy.45
  (43 shorter events, 0.4 us)
Async XLA Ops:
  7.2 1.2 copy-start.3
  7.2 1.2 copy-start.4
  7.6 1.4 copy-start.1
  9.0 3.2 copy-start.14
  9.0 3.8 %copy-start.13 = (f32[64,2,3]{0,1,2:T(2,128)S(1)}, f32[64,2,3]{0,1,2:T(2,128)}, u32[]{:S(2)}) copy-start(f32[64,2,3]{0,1,2:T(2,128)} %param.26) | copy-start | bytes 4612
  13.5 81.2 %copy-start.7 = (f32[768]{0:T(1024)S(1)}, f32[768]{0:T(1024)}, u32[]{:S(2)}) copy-start(f32[768]{0:T(1024)} %param.28) | copy-start | bytes 9220
  13.5 81.2 %copy-start.8 = (f32[768]{0:T(1024)S(1)}, f32[768]{0:T(1024)}, u32[]{:S(2)}) copy-start(f32[768]{0:T(1024)} %param.29) | copy-start | bytes 9220
  13.5 81.2 %copy-start.9 = (f32[768]{0:T(1024)S(1)}, f32[768]{0:T(1024)}, u32[]{:S(2)}) copy-start(f32[768]{0:T(1024)} %param.30) | copy-start | bytes 9220
  13.5 81.2 %copy-start.10 = (f32[768]{0:T(1024)S(1)}, f32[768]{0:T(1024)}, u32[]{:S(2)}) copy-start(f32[768]{0:T(1024)} %param.33) | copy-start | bytes 9220
  13.5 81.2 %copy-start.11 = (f32[768]{0:T(1024)S(1)}, f32[768]{0:T(1024)}, u32[]{:S(2)}) copy-start(f32[768]{0:T(1024)} %param.34) | copy-start | bytes 9220
  13.5 81.2 %copy-start.12 = (f32[768]{0:T(1024)S(1)}, f32[768]{0:T(1024)}, u32[]{:S(2)}) copy-start(f32[768]{0:T(1024)} %param.35) | copy-start | bytes 9220
  150.2 32.5 %copy-start.6 = (f32[8,768]{1,0:T(8,128)S(1)}, f32[8,768]{1,0:T(8,128)}, u32[]{:S(2)}) copy-start(f32[8,768]{1,0:T(8,128)} %get-tuple-element.69) | copy-start | bytes 73732
  345.4 5.6 %copy-start = (bf16[17,128,768]{2,1,0:T(8,128)(2,1)S(1)}, bf16[17,128,768]{2,1,0:T(8,128)(2,1)}, u32[]{:S(2)}) copy-start(bf16[17,128,768]{2,1,0:T(8,128)(2,1)} %get-tuple-element.72) | copy-start | bytes 10027012
  352.3 1.8 copy-start.2
  354.1 1.9 copy-start.5

commit v3 on v2

--- a/solution.py
+++ b/solution.py
@@ -52,7 +52,7 @@
 def head_rows(j):
     return lax.broadcasted_iota(jnp.int32, (E, 1), 0) // 64 == j
 
-def attend_fwd(m, small, q8, k, vt, dm, ct, lse):
+def attend_fwd(m, small, q8, k, vt, dm, ct, lse, hook=lambda i: None):
     def block(i, keys, koff):
         cols = pl.ds(pl.multiple_of(i * 128, 128), 128)
         qi = q8[cols, :]
@@ -71,10 +71,10 @@
         ct[:, cols] = out.astype(BF16)
     @pl.when(m < 2)
     def _():
-        lax.fori_loop(0, 4, lambda i, u: (block(i, 512, 0), u)[1], 0)
+        lax.fori_loop(0, 4, lambda i, u: (block(i, 512, 0), hook(i), u)[2], 0)
     @pl.when(m >= 2)
     def _():
-        lax.fori_loop(0, 5, lambda i, u: (block(i, 128, pl.multiple_of(i * 128, 128)), u)[1], 0)
+        lax.fori_loop(0, 5, lambda i, u: (block(i, 128, pl.multiple_of(i * 128, 128)), hook(i), u)[2], 0)
 
 def attend_bwd(m, small, q8, k, v, kt, gc, dm, lse, gqt, gk, gv):
     gk[...] = jnp.zeros_like(gk)
@@ -300,7 +300,6 @@
         "attention_backward", (slen, llen, xl, xs, W, small, q8, k, v, ctx, lse, ga, gs1))
 
 MESH = pl.DeviceIdType.MESH
-GROUPS = ((0, 1), (1, 3))
 PR = 96
 
 def place():
@@ -316,14 +315,13 @@
         pl.semaphore_signal(b, inc=1, device_id=d, device_id_type=MESH)
     pl.semaphore_wait(b, len(peers))
 
-def ag_kernel(own, small, out, sout, stage, recv, send, loc, ss, sr):
+def kg(slen, llen, own, small, xl, xs, vec, out, sout, q8o, ko, vo, co, lseo, n1o, r1o, hlo,
+       stage, ssm, xb, dm, vt, ct, acc, wz, recv, send, loc, ss, sr, sem):
+    g = pl.program_id(0)
     dp, y, x, c, z = place()
     xn, yn, cn = dpi(y, 1 - x, c), dpi(1 - y, x, c), dpi(y, x, 1 - c)
     dn = dpi(1 - y, 1 - x, c)
-    barrier_all([(xn, z), (yn, z), (cn, z)] + [(dp, (z + k) % 4) for k in (1, 2, 3)])
-    def sm(k): return pltpu.make_async_remote_copy(src_ref=small, dst_ref=sout.at[z], send_sem=ss.at[k], recv_sem=sr.at[z], device_id=(dp, (z + 1 + k) % 4), device_id_type=MESH)
-    for k in range(3): sm(k).start()
-    sout[z] = small[...]
+    def sm(j): return pltpu.make_async_remote_copy(src_ref=small, dst_ref=ssm.at[z], send_sem=ss.at[j], recv_sem=sr.at[z], device_id=(dp, (z + 1 + j) % 4), device_id_type=MESH)
     e = 1 - ((z + 1) // 2) % 2
     srcs = [z + 1 - 2 * (z % 2), e * ((z + 2) % 4) + (1 - e) * (3 - z), e * (3 - z) + (1 - e) * ((z + 2) % 4)]
 
@@ -332,11 +330,9 @@
             return pl.ds(pl.multiple_of(p * PR, 32), PR)
         return pl.ds(pl.multiple_of(p * PR + h * (PR // 2), 16), PR // 2)
     def piece(s, g, p, h=None):
-        a, n = GROUPS[g]
-        return out.at[s, pl.ds(a, n), rows(p, h), :]
+        return out.at[s, g, rows(p, h), :]
     def opiece(g, p):
-        a, n = GROUPS[g]
-        return own.at[pl.ds(a, n), rows(p, None), :]
+        return own.at[g, rows(p, None), :]
     def cp(src, dst, s, g, k, r, dev):
         return pltpu.make_async_remote_copy(src_ref=src, dst_ref=dst, send_sem=send.at[s, g, k], recv_sem=recv.at[s, g, r], device_id=dev, device_id_type=MESH)
     def zsend(src, s, g):
@@ -386,51 +382,113 @@
         m["cd0"]().start()
         wrecv(piece(s, g, dn, 1), s, g, 7)
         m["cd1"]().start()
-    def fin(j, g):
-        s = srcs[j]; m = simple(s, g)
-        zsend_wait(piece(s, g, dp), s, g)
-        for k in ("x", "y", "c", "cx", "cy", "yf", "xf", "cd0", "cd1"):
-            m[k]().wait_send()
+    def landed(j, g):
+        s = srcs[j]
         cdx, cdy, cdd = dpi(y, 1 - x, 1 - c), dpi(1 - y, x, 1 - c), dpi(1 - y, 1 - x, 1 - c)
         wrecv(piece(s, g, cn), s, g, 3)
         wrecv(piece(s, g, cdx), s, g, 4)
         wrecv(piece(s, g, cdy), s, g, 5)
         wrecv(piece(s, g, cdd, 0), s, g, 8)
         wrecv(piece(s, g, cdd, 1), s, g, 9)
-    for g in (0, 1):
-        zsend(opiece(g, dp), z, g)
-    l1 = pltpu.make_async_copy(own, stage, loc.at[0]); l1.start()
-    zarr(0, 0)
-    zarr(0, 1)
-    l1.wait()
-    l2 = pltpu.make_async_copy(stage, out.at[z], loc.at[1]); l2.start()
-    zarr(1, 0); xyarr(0, 0); zarr(1, 1)
-    diag(0, 0); xyarr(0, 1)
-    zarr(2, 0); xyarr(1, 0); zarr(2, 1)
-    diag(0, 1); diag(1, 0); xyarr(1, 1)
-    xyarr(2, 0); diag(2, 0); diag(1, 1); xyarr(2, 1); diag(2, 1)
-    for g in (0, 1):
-        zsend_wait(opiece(g, dp), z, g)
-    for j in range(3):
-        for g in (0, 1):
-            fin(j, g)
-    l2.wait()
-    for k in range(3):
-        sm(k).wait_send()
-        pltpu.make_async_remote_copy(src_ref=small, dst_ref=sout.at[(z + 1 + k) % 4], send_sem=ss.at[k], recv_sem=sr.at[(z + 1 + k) % 4], device_id=(cn, z), device_id_type=MESH).wait_recv()
-
-def gather_weights(own, small):
-    A = pl.BlockSpec(memory_space=pl.ANY)
-    V = pl.BlockSpec(memory_space=pltpu.VMEM)
-    S = pltpu.SemaphoreType.DMA
+    def sent(j, g):
+        s = srcs[j]; m = simple(s, g)
+        zsend_wait(piece(s, g, dp), s, g)
+        for k in ("x", "y", "c", "cx", "cy", "yf", "xf", "cd0", "cd1"):
+            m[k]().wait_send()
+    l1 = pltpu.make_async_copy(own, stage, loc.at[0])
+    l2 = pltpu.make_async_copy(stage, out.at[z], loc.at[1])
+    def fetch(j):
+        landed(j, 0)
+        cw = pltpu.make_async_copy(out.at[srcs[j], 0], wz, sem.at[1]); cw.start()
+        pltpu.make_async_remote_copy(src_ref=small, dst_ref=ssm.at[srcs[j]], send_sem=ss.at[j], recv_sem=sr.at[srcs[j]], device_id=(cn, z), device_id_type=MESH).wait_recv()
+        cw.wait()
+    Z, XY, DG = zarr, xyarr, diag
+    def mine(p): zsend(opiece(p, dp), z, p)
+    def at(n, fn):
+        @pl.when(g == n)
+        def _(): fn()
+
+    @pl.when(g == 0)
+    def _():
+        barrier_all([(xn, z), (yn, z), (cn, z)] + [(dp, (z + j) % 4) for j in (1, 2, 3)])
+        mine(0); mine(2); mine(3)
+        for j in range(3): sm(j).start()
+        cw = pltpu.make_async_copy(own.at[0], wz, sem.at[1]); cw.start()
+        l1.start()
+        ssm[z] = small[...]
+        load_rows(z, xl, xs, xb, sem.at[0])
+        distances(z, slen, llen, dm)
+        ct[...] = jnp.zeros_like(ct)
+        lseo[...] = jnp.zeros_like(lseo)
+        acc[...] = jnp.zeros_like(acc)
+        cw.wait()
+        Z(0, 0); mine(1)
+    zz = jnp.where(g == 0, z, jnp.where(g == 1, srcs[0], jnp.where(g == 2, srcs[1], srcs[2])))
+    xv = xb[...].reshape(R, D)
+    bs = ssm.at[zz]
+    q8o[zz] = ((nt(xv, wz[0:192, :]) + bs[0:1, 0:192]).astype(BF16).astype(F32) * 0.125).astype(BF16)
+    ko[zz] = nt(xv, wz[192:384, :]).astype(BF16)
+    v = (nt(xv, wz[384:576, :]) + bs[1:2, 0:192]).astype(BF16)
+    vo[zz] = v
+    vt[...] = v.T
+    at(0, lambda: Z(0, 2))
+    at(1, lambda: XY(0, 3))
+    at(3, lambda: DG(0, 3))
+    def hook(i):
+        def on(n, j, fn):
+            @pl.when((g == n) & (i == j))
+            def _(): fn()
+        on(0, 0, lambda: (Z(0, 3), XY(0, 0), Z(1, 0), Z(2, 0)))
+        on(0, 1, lambda: Z(0, 1))
+        on(0, 2, lambda: (DG(0, 0), XY(1, 0)))
+        on(0, 3, lambda: (XY(0, 2), Z(1, 3)))
+        on(1, 0, lambda: Z(2, 2))
+        on(1, 2, lambda: (DG(1, 0), Z(1, 2)))
+        on(2, 0, lambda: Z(2, 1))
+        on(2, 1, lambda: XY(1, 3))
+        on(2, 3, lambda: (Z(2, 3), XY(1, 2)))
+        on(3, 1, lambda: (XY(1, 1), XY(2, 3)))
+    attend_fwd(z, bs, q8o.at[zz], ko.at[zz], vt, dm, ct, lseo.at[zz], hook)
+    cv = ct[...].T
+    co[zz] = cv
+    acc[...] += nn(cv, wz[576:768, :]).astype(BF16).astype(F32)
+    at(0, lambda: (l1.wait(), l2.start(), XY(2, 0), fetch(0), Z(1, 1),))
+    at(1, lambda: (fetch(1), DG(2, 0),))
+    at(2, lambda: (fetch(2), XY(2, 2), XY(0, 1),))
+    @pl.when(g == 3)
+    def _():
+        XY(2, 1); DG(2, 2)
+        sout[...] = ssm[...]
+        for i in range(5):
+            rw = slice(128 * i, 128 * i + 128)
+            s = xb[i].astype(F32) + acc[rw, :] + vec[0:1, :]
+            n, r = norm_fwd(s)
+            n1o[rw, :] = n
+            r1o[rw, :] = jnp.broadcast_to(r, (128, 128))
+            hlo[rw, :] = (n * vec[1:2, :] + vec[2:3, :]).astype(BF16)
+        DG(1, 2); DG(0, 1); DG(1, 1); DG(2, 3); DG(0, 2); DG(1, 3); DG(2, 1)
+        for h in range(4):
+            zsend_wait(opiece(h, dp), z, h)
+        for j in range(3):
+            sm(j).wait_send()
+            for p in range(4): sent(j, p)
+            for p in (1, 2, 3): landed(j, p)
+        l2.wait()
+
+def run_kg(slen, llen, own, small, xl, xs, vec):
+    V, S = pltpu.VMEM, pltpu.SemaphoreType.DMA
+    o = lambda *s: const(s)
+    rz = lambda: sds((4, R, E), BF16)
     return pl.pallas_call(
-        ag_kernel,
-        out_shape=[jax.ShapeDtypeStruct((4, 4, 768, 768), jnp.bfloat16), jax.ShapeDtypeStruct((4, 8, 256), jnp.float32)],
-        in_specs=[A, V], out_specs=[A, V],
-        scratch_shapes=[pltpu.VMEM((4, 768, 768), jnp.bfloat16), S((4, 2, 10)), S((4, 2, 11)), S((2,)), S((3,)), S((4,))],
-        compiler_params=pltpu.CompilerParams(collective_id=0, has_side_effects=True, vmem_limit_bytes=60 << 20),
-        name="gather_weights",
-    )(own, small)
+        kg,
+        grid_spec=pltpu.PrefetchScalarGridSpec(num_scalar_prefetch=2, grid=(4,),
+            in_specs=[ANY, o(8, 256), ANY, ANY, o(8, D)],
+            out_specs=[ANY, o(4, 8, 256), o(4, R, E), o(4, R, E), o(4, R, E), o(4, R, E), o(4, 8, R), o(R, D), o(R, 128), o(R, D)],
+            scratch_shapes=[V((4, D, D), BF16), V((4, 8, 256), F32), V((5, 128, D), BF16), V((5, 512, 128), F32), V((E, R), BF16), V((E, R), BF16), V((R, D), F32), V((D, D), BF16),
+                            S((4, 4, 10)), S((4, 4, 11)), S((2,)), S((3,)), S((4,)), S((2,))]),
+        out_shape=[sds((4, 4, D, D), BF16), sds((4, 8, 256), F32), rz(), rz(), rz(), rz(), sds((4, 8, R), F32), sds((R, D), F32), sds((R, 128), F32), sds((R, D), BF16)],
+        compiler_params=pltpu.CompilerParams(dimension_semantics=("arbitrary",), collective_id=0, has_side_effects=True, vmem_limit_bytes=VM),
+        name="gather_attention_forward")(slen, llen, own, small, xl, xs, vec)
 
 ZO = (3, 0, 2, 1)
 
@@ -697,10 +755,9 @@
     return own, small
 def per_device(x_short, x_long, short_lengths, long_lengths, slope_index, w_qkv, b_qv, w_out, b_out, gain1, bias1, w_up, w_down, b_down, gain2, bias2, cot_short, cot_long):
     own, small = prep(slope_index, w_qkv, b_qv, w_out, w_up, w_down)
-    W, S = gather_weights(own, small)
     vec = jnp.stack([b_out, gain1, bias1, b_down, gain2, bias2, bias2, bias2], 0)
     xl, cl = x_long.reshape(8, 128, D), cot_long.reshape(8, 128, D)
-    q8, k, v, ctx, lse, n1, r1, hl = run_ka(short_lengths, long_lengths, xl, x_short, W, S, vec)
+    W, S, q8, k, v, ctx, lse, n1, r1, hl = run_kg(short_lengths, long_lengths, own, small, xl, x_short, vec)
     a, b, inner, y, gf, gs2, vg2 = run_kb(cl, cot_short, W, hl, n1, vec)
     go3, gs1, vg1 = run_kc(W, a, b, inner, gf, hl, gs2, n1, r1, vec)
     m, dpx = lax.axis_index("mp"), lax.axis_index("dp")

time: 360 us -> 328 us (0.911)
  Pallas kernels: 329 us -> 297 us
    pallas_call x3 -> x2, Pallas kernels: 86.5 us -> 54 us  [call(): pl.pallas_call(kernel, grid_spec=pltpu.PrefetchScalarGridSpec(num_scalar_...]
where the time goes in v3:
time: 328 us; the launch traced here: 327 us
  Pallas kernels  297 us (91%)
  local copies, waits for them, and re-layouts  24.4 us (7%)
  other arithmetic  4.82 us (1%)
    pallas_call x1, Pallas kernels, run_kx(): pl.pallas_call(kx, grid_spec=pltpu.PrefetchScalarGridSpec(num_scalar_pref...  163 us
    pallas_call x1, Pallas kernels, run_kg(): pl.pallas_call(kg, grid_spec=pltpu.PrefetchScalarGridSpec(num_scalar_pref...  80.8 us
    pallas_call x2, Pallas kernels, call(): pl.pallas_call(kernel, grid_spec=pltpu.PrefetchScalarGridSpec(num_scalar_...  54 us

profile of v3, /device:TPU:0, one launch (start us, length us, event | category | flops | bytes accessed | tf_op | source)
XLA Modules:
  0.0 327.4 jit_solution(12596692459948459622)
XLA Ops:
  0.6 6.5 %fusion.1 = (bf16[768,1,768]{2,1,0:T(2,128)(2,1)S(1)}, bf16[768,1,768]{2,1,0:T(2,128)(2,1)S(1)}) fusion(bf16[768,2,768]{2,1,0:T(2,128)(2,1)} %param.31), kind=kLoop, calls=%fused_computation.25 | loop fusion | bytes 4718592 | tf_op jit(solution)/shard_map/slice | solution.py:751
  7.2 0.4 copy_bitcast_fusion
  7.6 0.7 copy-done.3
  8.4 0.1 maximum_bitcast_fusion
  8.5 0.5 copy-done.1
  9.0 2.7 pad_maximum_fusion.own
  11.7 0.6 compare_reduce_fusion
  12.4 0.7 fusion
  13.0 0.1 reshape.89
  13.1 0.6 pad.9.small
  13.8 0.7 stack.44.vec
  14.5 80.8 %gather_attention_forward.1 = (bf16[4,4,768,768]{3,2,1,0:T(8,128)(2,1)}, f32[4,8,256]{2,1,0:T(8,128)}, bf16[4,640,192]{2,1,0:T(8,128)(2,1)}, bf16[4,640,192]{2,1...) custom-call(s32[9]{0:T(128)} %slen.3, s32[2]{0:T(128)} %llen.3, ...), custom_call_target="tpu_custom_call" | custom-call | tf_op jit(solution)/shard_map/gather_attention_forward/pallas_call | solution.py:482
  95.3 22.4 %feed_forward.1 = (f32[4,640,768]{2,1,0:T(8,128)}, f32[4,640,768]{2,1,0:T(8,128)}, bf16[4,640,768]{2,1,0:T(8,128)(2,1)}, bf16[640,768]{1,0:T(8,128)(2,1)}, bf16[...) custom-call(bf16[8,128,768]{2,1,0:T(8,128)(2,1)} %bitcast.49, bf16[9,128,768]{2,1,0:T(8,128)(2,1)} %cs.1, ...), custom_call_target="tpu_custom_call" | custom-call | tf_op jit(solution)/shard_map/feed_forward/pallas_call | solution.py:165
  117.8 31.5 %feed_backward.1 = (bf16[4,3,768,768]{3,2,1,0:T(8,128)(2,1)}, f32[640,768]{1,0:T(8,128)}, f32[8,768]{1,0:T(8,128)}) custom-call(bf16[4,4,768,768]{3,2,1,0:T(8,128)(2,1)} %get-tuple-element.51.wg.wu.wd.w, bf16[4,4,768,768]{3,2,1,0:T(8,128)(2,1)} %get-tuple-element.51.wg.wu.wd.w, bf16[4,4,768,768]{3,2,1,0:T(8,128)(2,1)} %get-tuple-element.51.wg.wu.wd.w, ...), custom_call_target="tpu_custom_call" | custom-call | tf_op jit(solution)/shard_map/feed_backward/pallas_call | solution.py:165
  149.3 0.7 slice.86
  150.0 0.1 pad.14.clone
  150.1 0.7 maximum_maximum_fusion.vin
  150.8 162.5 %attention_backward_send.1 = (f32[4,96,768]{2,1,0:T(8,128)}, bf16[17,128,768]{2,1,0:T(8,128)(2,1)}, bf16[17,128,768]{2,1,0:T(8,128)(2,1)}, f32[16,768]{1,0:T(8,128)}) custom-call(s32[9]{0:T(128)} %slen.3, s32[2]{0:T(128)} %llen.3, bf16[8,128,768]{2,1,0:T(8,128)(2,1)} %bitcast.46, bf16[9,128,768]{2,1,0:T(8,128)(2,1)} %xs.3, ...), custom_call_target="tpu_custom_call" | custom-call | tf_op jit(solution)/shard_map/attention_backward_send/pallas_call | solution.py:736
  313.4 2.9 slice.87
  316.3 2.7 slice.88
  319.0 1.3 slice.89
  320.3 1.2 slice.90
  321.6 0.6 copy-done.2
  322.2 0.8 slice_bitcast_fusion
  323.0 0.1 copy.42
  323.1 0.9 copy.44
  324.0 0.1 reshape.96
  324.2 0.6 copy.51
  324.8 0.7 slice.106
  325.5 0.1 constant_dynamic-slice_fusion
  325.6 0.5 slice_bitcast_fusion.4
  326.1 1.3 copy.45
  (42 shorter events, 0.3 us)
Async XLA Ops:
  7.2 1.2 copy-start.3
  7.2 1.2 copy-start.4
  7.6 1.4 copy-start.1
  9.0 3.4 %copy-start.14 = (s32[3]{0:T(128)S(1)}, s32[3]{0:T(128)}, u32[]{:S(2)}) copy-start(s32[3]{0:T(128)} %param.24) | copy-start | bytes 40
  9.0 4.1 %copy-start.13 = (f32[64,2,3]{0,1,2:T(2,128)S(1)}, f32[64,2,3]{0,1,2:T(2,128)}, u32[]{:S(2)}) copy-start(f32[64,2,3]{0,1,2:T(2,128)} %param.26) | copy-start | bytes 4612
  9.0 4.8 %copy-start.7 = (f32[768]{0:T(1024)S(1)}, f32[768]{0:T(1024)}, u32[]{:S(2)}) copy-start(f32[768]{0:T(1024)} %param.28) | copy-start | bytes 9220
  9.0 4.8 %copy-start.8 = (f32[768]{0:T(1024)S(1)}, f32[768]{0:T(1024)}, u32[]{:S(2)}) copy-start(f32[768]{0:T(1024)} %param.29) | copy-start | bytes 9220
  9.0 4.8 %copy-start.9 = (f32[768]{0:T(1024)S(1)}, f32[768]{0:T(1024)}, u32[]{:S(2)}) copy-start(f32[768]{0:T(1024)} %param.30) | copy-start | bytes 9220
  9.0 4.8 %copy-start.10 = (f32[768]{0:T(1024)S(1)}, f32[768]{0:T(1024)}, u32[]{:S(2)}) copy-start(f32[768]{0:T(1024)} %param.33) | copy-start | bytes 9220
  9.0 4.8 %copy-start.11 = (f32[768]{0:T(1024)S(1)}, f32[768]{0:T(1024)}, u32[]{:S(2)}) copy-start(f32[768]{0:T(1024)} %param.34) | copy-start | bytes 9220
  9.0 4.8 %copy-start.12 = (f32[768]{0:T(1024)S(1)}, f32[768]{0:T(1024)}, u32[]{:S(2)}) copy-start(f32[768]{0:T(1024)} %param.35) | copy-start | bytes 9220
  117.7 32.3 %copy-start.6 = (f32[8,768]{1,0:T(8,128)S(1)}, f32[8,768]{1,0:T(8,128)}, u32[]{:S(2)}) copy-start(f32[8,768]{1,0:T(8,128)} %get-tuple-element.69) | copy-start | bytes 73732
  313.4 5.6 %copy-start = (bf16[17,128,768]{2,1,0:T(8,128)(2,1)S(1)}, bf16[17,128,768]{2,1,0:T(8,128)(2,1)}, u32[]{:S(2)}) copy-start(bf16[17,128,768]{2,1,0:T(8,128)(2,1)} %get-tuple-element.72) | copy-start | bytes 10027012
  320.3 1.8 copy-start.2
  322.2 1.9 copy-start.5

commit v4 on v3

--- a/solution.py
+++ b/solution.py
@@ -76,7 +76,7 @@
     def _():
         lax.fori_loop(0, 5, lambda i, u: (block(i, 128, pl.multiple_of(i * 128, 128)), hook(i), u)[2], 0)
 
-def attend_bwd(m, small, q8, k, v, kt, gc, dm, lse, gqt, gk, gv):
+def attend_bwd(m, small, q8, k, v, kt, gc, dm, lse, gqt, gk, gv, hook=lambda i: None):
     gk[...] = jnp.zeros_like(gk)
     gv[...] = jnp.zeros_like(gv)
     def block(i, keys, koff):
@@ -105,11 +105,11 @@
         gv[rows, :] += ov
     @pl.when(m < 2)
     def _():
-        lax.fori_loop(0, 4, lambda i, u: (block(i, 512, 0), u)[1], 0)
+        lax.fori_loop(0, 4, lambda i, u: (block(i, 512, 0), hook(i), u)[2], 0)
         gqt[:, 512:640] = jnp.zeros((E, 128), F32)
     @pl.when(m >= 2)
     def _():
-        lax.fori_loop(0, 5, lambda i, u: (block(i, 128, pl.multiple_of(i * 128, 128)), u)[1], 0)
+        lax.fori_loop(0, 5, lambda i, u: (block(i, 128, pl.multiple_of(i * 128, 128)), hook(i), u)[2], 0)
 
 def norm_fwd(s):
     mean = jnp.mean(s, axis=1, keepdims=True)
@@ -598,26 +598,28 @@
                 lax.fori_loop(0, n, body, 0)
     order = far_order(z)
     def yb(s): return 4 * s + s // 3
-    def yc(t, src, s, hf, right):
-        n, off = (4, 0) if hf == 0 else (1, 4)
+    CHUNKS = ((2, 0), (2, 2), (1, 4))
+    def yc(t, src, s, h, right):
+        n, off = CHUNKS[h]
         dst = (yout, dxout)[t].at[pl.ds(yb(s) + off, n)]
         src = dst if src is None else src.at[pl.ds(off, n)]
-        return rc(src, dst, ys.at[t, s, hf, right], yr.at[t, s, hf], (dp, z + 1 if right else z - 1))
-    def ysend(t, src, s, act):
-        for right in (1, 0):
-            @pl.when((s <= z) & (z < 3) if right else (s >= z) & (z > 0))
+        return rc(src, dst, ys.at[t, s, h, right], yr.at[t, s, h], (dp, z + 1 if right else z - 1))
+    def ysend(t, src, s, act, hs=(0, 1, 2)):
+        for h in hs:
+            for right in (1, 0):
+                go = (s <= z) & (z < 3) if right else (s >= z) & (z > 0)
+                @pl.when(go & (s == 2) if h == 2 else go)
+                def _():
+                    getattr(yc(t, src, s, h, right), act)()
+    def yarr(t, j, h):
+        s = order[j]
+        if h == 2:
+            @pl.when(s == 2)
             def _():
-                getattr(yc(t, src, s, 0, right), act)()
-                @pl.when(s == 2)
-                def _():
-                    getattr(yc(t, src, s, 1, right), act)()
-    def yarr(t, j):
-        s = order[j]
-        yc(t, None, s, 0, 1).wait_recv()
-        @pl.when(s == 2)
-        def _():
-            yc(t, None, s, 1, 1).wait_recv()
-        ysend(t, None, s, "start")
+                yc(t, None, s, h, 1).wait_recv()
+        else:
+            yc(t, None, s, h, 1).wait_recv()
+        ysend(t, None, s, "start", (h,))
     def own(t, hf, way):
         n, off = (4, 0) if hf == 0 else (1, 4)
         if way == 0:
@@ -628,7 +630,7 @@
         @pl.when(z == 2)
         def _():
             fn(1)
-    vpeer = [(cn, z), (xn, z), (yn, z), (dp, z1), (dp, z2)]
+    vpeer = [(dp, z1), (dp, z2), (cn, z), (xn, z), (yn, z)]
     def vcopy(i): return rc(vs.at[i], vr.at[i], vsem_s.at[i], vsem_r.at[i], vpeer[i])
     def vstep(i):
         vcopy(i).wait_recv()
@@ -661,18 +663,31 @@
         ga[...] = acc[...].astype(BF16)
         gat[...] = ga[...].T
         ownall(lambda h: (own(0, h, 0).wait(), own(0, h, 1).start()))
+        yarr(0, 2, 2)
     wz, sm = w.at[0, 0], small.at[0]
     gc[...] = nt(ga[...], wz[576:768, :]).astype(BF16)
     kt[...] = k[0].T
-    attend_bwd(z, sm, q8.at[0], k.at[0], v.at[0], kt, gc, dm, lse.at[0], gqt, gk, gv)
+    @pl.when(g == 2)
+    def _():
+        yarr(0, 2, 0)
+    @pl.when(g == 3)
+    def _():
+        yarr(0, 2, 1)
+    def hook(i):
+        def on(n, j, fn):
+            @pl.when((g == n) & (i == j))
+            def _(): fn()
+        on(0, 0, lambda: A(F, 0))
+        on(0, 1, lambda: yarr(0, 0, 0))
+        on(0, 3, lambda: A(F, 1))
+        on(1, 0, lambda: yarr(0, 0, 1))
+        on(1, 2, lambda: yarr(0, 1, 1))
+        on(1, 3, lambda: B(F, 0))
+        on(2, 2, lambda: (A(T, 0), C(F, 0), Z(F, 0, 0)))
+    attend_bwd(z, sm, q8.at[0], k.at[0], v.at[0], kt, gc, dm, lse.at[0], gqt, gk, gv, hook)
     @pl.when(g == 0)
-    def _(): A(F, 0)
-    @pl.when(g == 1)
-    def _(): A(T, 0); B(F, 0)
-    @pl.when(g == 2)
-    def _(): A(T, 1); B(F, 1); C(F, 0); Z(F, 0, 0)
-    @pl.when(g == 3)
-    def _(): A(T, 2); B(F, 2); C(F, 1); Z(F, 0, 1); Z(F, 1, 0)
+    def _():
+        yarr(0, 1, 0)
     zg = zo(g)
     dq = gqt[...].astype(BF16).T
     dk = gk[...].astype(BF16)
@@ -680,31 +695,45 @@
     gbs[zg, 0:1, 0:192] = jnp.sum(dq.astype(F32), axis=0, keepdims=True)
     gbs[zg, 1:2, 0:192] = jnp.sum(dv.astype(F32), axis=0, keepdims=True)
     acc[...] += nn(dq, wz[0:192, :]) + nn(dk, wz[192:384, :]) + nn(dv, wz[384:576, :])
-    @pl.when(g == 3)
-    def _():
+    def X():
         for i in range(5):
             dxs[i] = acc[128 * i:128 * i + 128, :].astype(BF16)
-        ysend(1, dxs, z, "start")
-        ownall(lambda h: own(1, h, 1).start())
         vs[0] = vin[...]
         for i in range(4):
             vs[0, 6 + 2 * i:8 + 2 * i, 0:192] = gbs[i, 0:2, 0:192]
         vcopy(0).start()
+        ysend(1, dxs, z, "start")
+        ownall(lambda h: own(1, h, 1).start())
+    @pl.when(g == 1)
+    def _():
+        yarr(1, 2, 2)
+    @pl.when(g == 2)
+    def _():
+        C(F, 1); Z(F, 1, 0); yarr(0, 1, 2); A(F, 2)
+    @pl.when(g == 3)
+    def _():
+        X(); B(F, 2); A(T, 1)
     for i in range(6):
         rw = slice(128 * i, 128 * i + 128)
         gob[zg, 0, rw, :] = jnp.concatenate([nn(xt[rw, :], dq), nn(xt[rw, :], dk), nn(xt[rw, :], dv), nn(gat[rw, :], ctx[0])], axis=1).astype(BF16)
     @pl.when(g == 0)
-    def _(): S0(T, 0); A(F, 1)
+    def _():
+        S0(T, 0)
     @pl.when(g == 1)
-    def _(): S0(T, 1); A(F, 2); yarr(0, 0)
+    def _():
+        B(F, 1); S0(T, 1)
     @pl.when(g == 2)
-    def _(): S0(T, 2); A(F, 3); B(T, 0); yarr(0, 1)
+    def _():
+        S0(T, 2)
     @pl.when(g == 3)
     def _():
-        S0(T, 3); C(T, 0); B(T, 1); Z(T, 0, 0); yarr(0, 2); vstep(0); A(T, 3); Z(F, 0, 2); Z(F, 1, 1); B(F, 3); C(F, 2); Z(F, 2, 0)
-        B(T, 2); C(T, 1); Z(T, 1, 0); Z(T, 0, 1); vstep(1); B(T, 3); yarr(1, 0); Z(F, 0, 3); Z(F, 1, 2); Z(F, 2, 1); C(F, 3); Z(F, 3, 0); vstep(2)
-        C(T, 2); Z(T, 2, 0); C(T, 3); Z(T, 3, 0); Z(T, 0, 2); Z(T, 1, 1); yarr(1, 1); vstep(3); Z(F, 1, 3); Z(F, 2, 2); Z(F, 3, 1)
-        Z(T, 1, 2); Z(T, 2, 1); Z(T, 3, 1); Z(T, 0, 3); Z(T, 1, 3); Z(F, 3, 2); Z(T, 2, 2); Z(T, 3, 2); vstep(4); yarr(1, 2)
+        A(F, 3); C(F, 2); Z(F, 1, 1); S0(T, 3); Z(F, 2, 0); Z(F, 0, 1); vstep(0); B(T, 1); B(T, 0)
+        yarr(1, 1, 1); B(F, 3); A(T, 2); A(T, 3); C(T, 1); C(T, 0); Z(T, 0, 0); Z(T, 1, 0); yarr(1, 0, 0)
+        yarr(1, 0, 2); yarr(1, 1, 0); C(F, 3); Z(F, 0, 2); Z(F, 1, 2); yarr(0, 0, 2); yarr(1, 0, 1); Z(F, 3, 0); vstep(1)
+        B(T, 2); yarr(1, 1, 2); C(T, 2); Z(F, 0, 3); Z(T, 2, 0); Z(T, 1, 1); B(T, 3); C(T, 3); vstep(2)
+        Z(F, 1, 3); yarr(1, 2, 1); Z(F, 3, 1); Z(T, 0, 1); Z(T, 3, 0); vstep(3); Z(T, 0, 2); Z(T, 0, 3); Z(T, 1, 2)
+        Z(T, 1, 3); Z(F, 2, 1); yarr(1, 2, 0); Z(T, 2, 1); Z(F, 3, 2); Z(F, 2, 2); vstep(4); Z(T, 2, 2); Z(T, 3, 2)
+        Z(T, 3, 1)
         for kd in (0, 1):
             for zz in ZO:
                 for q in range(4): st0(kd, zz, q).wait_send()
@@ -732,7 +761,7 @@
     scratch = [V((5, 128, D), BF16), V((5, 512, 128), F32), V((E, R), BF16), V((R, E), BF16), V((E, R), F32), V((R, E), F32), V((R, E), F32),
                V((R, D), BF16), V((D, R), BF16), V((D, R), BF16), V((R, D), F32), V((4, 1, D, D), BF16), V((5, 128, D), BF16), V((4, 8, 256), F32),
                V((5, 128, D), BF16), V((5, 16, D), F32), V((5, 16, D), F32), b(4, 4, 3)] + bufs(3) + bufs(1) + [
-               S((2,)), S((2, 4, 4)), S((2, 4, 4)), S((4, 4)), S((2, 4, 6)), S((2, 4, 6)), S((2, 4)), S((2, 4, 2)), S((2, 4, 2, 2)), S((2, 4, 2)), S((5,)), S((5,)), S((2, 2, 2))]
+               S((2,)), S((2, 4, 4)), S((2, 4, 4)), S((4, 4)), S((2, 4, 6)), S((2, 4, 6)), S((2, 4)), S((2, 4, 2)), S((2, 4, 3, 2)), S((2, 4, 3)), S((5,)), S((5,)), S((2, 2, 2))]
     return pl.pallas_call(
         kx,
         grid_spec=pltpu.PrefetchScalarGridSpec(num_scalar_prefetch=2, grid=(4,),

time: 328 us -> 300 us (0.915)
  Pallas kernels: 297 us -> 269 us
    pallas_call x1, Pallas kernels: 163 us -> 134 us  [run_kx(): pl.pallas_call(kx, grid_spec=pltpu.PrefetchScalarGridSpec(num_scalar_pref...]
where the time goes in v4:
time: 300 us; the launch traced here: 299 us
  Pallas kernels  269 us (90%)
  local copies, waits for them, and re-layouts  24.4 us (8%)
  other arithmetic  4.82 us (2%)
    pallas_call x1, Pallas kernels, run_kx(): pl.pallas_call(kx, grid_spec=pltpu.PrefetchScalarGridSpec(num_scalar_pref...  134 us
    pallas_call x1, Pallas kernels, run_kg(): pl.pallas_call(kg, grid_spec=pltpu.PrefetchScalarGridSpec(num_scalar_pref...  80.8 us
    pallas_call x2, Pallas kernels, call(): pl.pallas_call(kernel, grid_spec=pltpu.PrefetchScalarGridSpec(num_scalar_...  54 us
    slice x1, local copies, waits for them, and re-layouts, prep(): own = jnp.stack([a, w_up[:, 0], w_up[:, 1], w_down], 0)  6.52 us

profile of v4, /device:TPU:0, one launch (start us, length us, event | category | flops | bytes accessed | tf_op | source)
XLA Modules:
  0.0 299.1 jit_solution(10113848066552647364)
XLA Ops:
  0.6 6.5 %fusion.1 = (bf16[768,1,768]{2,1,0:T(2,128)(2,1)S(1)}, bf16[768,1,768]{2,1,0:T(2,128)(2,1)S(1)}) fusion(bf16[768,2,768]{2,1,0:T(2,128)(2,1)} %param.31), kind=kLoop, calls=%fused_computation.25 | loop fusion | bytes 4718592 | tf_op jit(solution)/shard_map/slice | solution.py:780
  7.2 0.4 copy_bitcast_fusion
  7.6 0.7 copy-done.3
  8.4 0.1 maximum_bitcast_fusion
  8.5 0.5 copy-done.1
  9.0 2.7 pad_maximum_fusion.own
  11.7 0.6 compare_reduce_fusion
  12.4 0.7 fusion
  13.0 0.1 reshape.89
  13.1 0.6 pad.9.small
  13.8 0.7 stack.44.vec
  14.5 80.8 %gather_attention_forward.1 = (bf16[4,4,768,768]{3,2,1,0:T(8,128)(2,1)}, f32[4,8,256]{2,1,0:T(8,128)}, bf16[4,640,192]{2,1,0:T(8,128)(2,1)}, bf16[4,640,192]{2,1...) custom-call(s32[9]{0:T(128)} %slen.3, s32[2]{0:T(128)} %llen.3, ...), custom_call_target="tpu_custom_call" | custom-call | tf_op jit(solution)/shard_map/gather_attention_forward/pallas_call | solution.py:482
  95.3 22.4 %feed_forward.1 = (f32[4,640,768]{2,1,0:T(8,128)}, f32[4,640,768]{2,1,0:T(8,128)}, bf16[4,640,768]{2,1,0:T(8,128)(2,1)}, bf16[640,768]{1,0:T(8,128)(2,1)}, bf16[...) custom-call(bf16[8,128,768]{2,1,0:T(8,128)(2,1)} %bitcast.49, bf16[9,128,768]{2,1,0:T(8,128)(2,1)} %cs.1, ...), custom_call_target="tpu_custom_call" | custom-call | tf_op jit(solution)/shard_map/feed_forward/pallas_call | solution.py:165
  117.8 31.5 %feed_backward.1 = (bf16[4,3,768,768]{3,2,1,0:T(8,128)(2,1)}, f32[640,768]{1,0:T(8,128)}, f32[8,768]{1,0:T(8,128)}) custom-call(bf16[4,4,768,768]{3,2,1,0:T(8,128)(2,1)} %get-tuple-element.51.wg.wu.wd.w, bf16[4,4,768,768]{3,2,1,0:T(8,128)(2,1)} %get-tuple-element.51.wg.wu.wd.w, bf16[4,4,768,768]{3,2,1,0:T(8,128)(2,1)} %get-tuple-element.51.wg.wu.wd.w, ...), custom_call_target="tpu_custom_call" | custom-call | tf_op jit(solution)/shard_map/feed_backward/pallas_call | solution.py:165
  149.3 0.7 slice.86
  150.0 0.1 pad.14.clone
  150.1 0.7 maximum_maximum_fusion.vin
  150.8 134.2 %attention_backward_send.1 = (f32[4,96,768]{2,1,0:T(8,128)}, bf16[17,128,768]{2,1,0:T(8,128)(2,1)}, bf16[17,128,768]{2,1,0:T(8,128)(2,1)}, f32[16,768]{1,0:T(8,128)}) custom-call(s32[9]{0:T(128)} %slen.3, s32[2]{0:T(128)} %llen.3, bf16[8,128,768]{2,1,0:T(8,128)(2,1)} %bitcast.46, bf16[9,128,768]{2,1,0:T(8,128)(2,1)} %xs.3, ...), custom_call_target="tpu_custom_call" | custom-call | tf_op jit(solution)/shard_map/attention_backward_send/pallas_call | solution.py:765
  285.0 2.9 slice.87
  288.0 2.7 slice.88
  290.6 1.3 slice.89
  292.0 1.2 slice.90
  293.2 0.6 copy-done.2
  293.8 0.8 slice_bitcast_fusion
  294.6 0.1 copy.42
  294.8 0.9 copy.44
  295.7 0.1 reshape.96
  295.8 0.1 constant_dynamic-slice_fusion.1
  295.8 0.6 copy.51
  296.4 0.7 slice.106
  297.2 0.5 slice_bitcast_fusion.4
  297.8 1.3 copy.45
  (42 shorter events, 0.3 us)
Async XLA Ops:
  7.2 1.2 copy-start.3
  7.2 1.2 copy-start.4
  7.6 1.4 copy-start.1
  9.0 3.4 %copy-start.14 = (s32[3]{0:T(128)S(1)}, s32[3]{0:T(128)}, u32[]{:S(2)}) copy-start(s32[3]{0:T(128)} %param.24) | copy-start | bytes 40
  9.0 4.1 %copy-start.13 = (f32[64,2,3]{0,1,2:T(2,128)S(1)}, f32[64,2,3]{0,1,2:T(2,128)}, u32[]{:S(2)}) copy-start(f32[64,2,3]{0,1,2:T(2,128)} %param.26) | copy-start | bytes 4612
  9.0 4.8 %copy-start.7 = (f32[768]{0:T(1024)S(1)}, f32[768]{0:T(1024)}, u32[]{:S(2)}) copy-start(f32[768]{0:T(1024)} %param.28) | copy-start | bytes 9220
  9.0 4.8 %copy-start.8 = (f32[768]{0:T(1024)S(1)}, f32[768]{0:T(1024)}, u32[]{:S(2)}) copy-start(f32[768]{0:T(1024)} %param.29) | copy-start | bytes 9220
  9.0 4.8 %copy-start.9 = (f32[768]{0:T(1024)S(1)}, f32[768]{0:T(1024)}, u32[]{:S(2)}) copy-start(f32[768]{0:T(1024)} %param.30) | copy-start | bytes 9220
  9.0 4.8 %copy-start.10 = (f32[768]{0:T(1024)S(1)}, f32[768]{0:T(1024)}, u32[]{:S(2)}) copy-start(f32[768]{0:T(1024)} %param.33) | copy-start | bytes 9220
  9.0 4.8 %copy-start.11 = (f32[768]{0:T(1024)S(1)}, f32[768]{0:T(1024)}, u32[]{:S(2)}) copy-start(f32[768]{0:T(1024)} %param.34) | copy-start | bytes 9220
  9.0 4.8 %copy-start.12 = (f32[768]{0:T(1024)S(1)}, f32[768]{0:T(1024)}, u32[]{:S(2)}) copy-start(f32[768]{0:T(1024)} %param.35) | copy-start | bytes 9220
  117.7 32.3 %copy-start.6 = (f32[8,768]{1,0:T(8,128)S(1)}, f32[8,768]{1,0:T(8,128)}, u32[]{:S(2)}) copy-start(f32[8,768]{1,0:T(8,128)} %get-tuple-element.69) | copy-start | bytes 73732
  285.0 5.6 %copy-start = (bf16[17,128,768]{2,1,0:T(8,128)(2,1)S(1)}, bf16[17,128,768]{2,1,0:T(8,128)(2,1)}, u32[]{:S(2)}) copy-start(bf16[17,128,768]{2,1,0:T(8,128)(2,1)} %get-tuple-element.72) | copy-start | bytes 10027012
  292.0 1.8 copy-start.2
  293.8 1.9 copy-start.5

commit v5 on v4

--- a/solution.py
+++ b/solution.py
@@ -315,8 +315,8 @@
         pl.semaphore_signal(b, inc=1, device_id=d, device_id_type=MESH)
     pl.semaphore_wait(b, len(peers))
 
-def kg(slen, llen, own, small, xl, xs, vec, out, sout, q8o, ko, vo, co, lseo, n1o, r1o, hlo,
-       stage, ssm, xb, dm, vt, ct, acc, wz, recv, send, loc, ss, sr, sem):
+def kg(slen, llen, own, small, xl, xs, cl, cs, vec, out, sout, q8o, ko, vo, co, lseo, n1o, r1o, hlo, ao, bo, io, yo, gfo, gs2o, vgo,
+       ssm, xb, dm, vt, ct, acc, wz, wf, ab, bb, ib, recv, send, loc, ss, sr, sem, lsem, osem):
     g = pl.program_id(0)
     dp, y, x, c, z = place()
     xn, yn, cn = dpi(y, 1 - x, c), dpi(1 - y, x, c), dpi(y, x, 1 - c)
@@ -395,23 +395,28 @@
         zsend_wait(piece(s, g, dp), s, g)
         for k in ("x", "y", "c", "cx", "cy", "yf", "xf", "cd0", "cd1"):
             m[k]().wait_send()
-    l1 = pltpu.make_async_copy(own, stage, loc.at[0])
-    l2 = pltpu.make_async_copy(stage, out.at[z], loc.at[1])
+    l0 = pltpu.make_async_copy(wz, out.at[z, 0], loc.at[0])
+    l1 = pltpu.make_async_copy(own.at[pl.ds(1, 3)], wf.at[0], lsem.at[0])
+    l2 = pltpu.make_async_copy(wf.at[0], out.at[z, pl.ds(1, 3)], loc.at[1])
     def fetch(j):
         landed(j, 0)
         cw = pltpu.make_async_copy(out.at[srcs[j], 0], wz, sem.at[1]); cw.start()
         pltpu.make_async_remote_copy(src_ref=small, dst_ref=ssm.at[srcs[j]], send_sem=ss.at[j], recv_sem=sr.at[srcs[j]], device_id=(cn, z), device_id_type=MESH).wait_recv()
         cw.wait()
+    def fcopy(j): return pltpu.make_async_copy(out.at[srcs[j], pl.ds(1, 3)], wf.at[(j + 1) % 2], lsem.at[(j + 1) % 2])
+    def load(j):
+        for p in (1, 2, 3): landed(j, p)
+        fcopy(j).start()
+    blocks = [z] + srcs
+    def stores(n):
+        return [pltpu.make_async_copy(f.at[n % 2], t.at[blocks[n]], osem.at[i, n % 2]) for i, (f, t) in enumerate(((ab, ao), (bb, bo), (ib, io)))]
     Z, XY, DG = zarr, xyarr, diag
     def mine(p): zsend(opiece(p, dp), z, p)
-    def at(n, fn):
-        @pl.when(g == n)
-        def _(): fn()
 
     @pl.when(g == 0)
     def _():
         barrier_all([(xn, z), (yn, z), (cn, z)] + [(dp, (z + j) % 4) for j in (1, 2, 3)])
-        mine(0); mine(2); mine(3)
+        mine(0); mine(1)
         for j in range(3): sm(j).start()
         cw = pltpu.make_async_copy(own.at[0], wz, sem.at[1]); cw.start()
         l1.start()
@@ -422,42 +427,55 @@
         lseo[...] = jnp.zeros_like(lseo)
         acc[...] = jnp.zeros_like(acc)
         cw.wait()
-        Z(0, 0); mine(1)
-    zz = jnp.where(g == 0, z, jnp.where(g == 1, srcs[0], jnp.where(g == 2, srcs[1], srcs[2])))
-    xv = xb[...].reshape(R, D)
-    bs = ssm.at[zz]
-    q8o[zz] = ((nt(xv, wz[0:192, :]) + bs[0:1, 0:192]).astype(BF16).astype(F32) * 0.125).astype(BF16)
-    ko[zz] = nt(xv, wz[192:384, :]).astype(BF16)
-    v = (nt(xv, wz[384:576, :]) + bs[1:2, 0:192]).astype(BF16)
-    vo[zz] = v
-    vt[...] = v.T
-    at(0, lambda: Z(0, 2))
-    at(1, lambda: XY(0, 3))
-    at(3, lambda: DG(0, 3))
-    def hook(i):
-        def on(n, j, fn):
-            @pl.when((g == n) & (i == j))
-            def _(): fn()
-        on(0, 0, lambda: (Z(0, 3), XY(0, 0), Z(1, 0), Z(2, 0)))
-        on(0, 1, lambda: Z(0, 1))
-        on(0, 2, lambda: (DG(0, 0), XY(1, 0)))
-        on(0, 3, lambda: (XY(0, 2), Z(1, 3)))
-        on(1, 0, lambda: Z(2, 2))
-        on(1, 2, lambda: (DG(1, 0), Z(1, 2)))
-        on(2, 0, lambda: Z(2, 1))
-        on(2, 1, lambda: XY(1, 3))
-        on(2, 3, lambda: (Z(2, 3), XY(1, 2)))
-        on(3, 1, lambda: (XY(1, 1), XY(2, 3)))
-    attend_fwd(z, bs, q8o.at[zz], ko.at[zz], vt, dm, ct, lseo.at[zz], hook)
-    cv = ct[...].T
-    co[zz] = cv
-    acc[...] += nn(cv, wz[576:768, :]).astype(BF16).astype(F32)
-    at(0, lambda: (l1.wait(), l2.start(), XY(2, 0), fetch(0), Z(1, 1),))
-    at(1, lambda: (fetch(1), DG(2, 0),))
-    at(2, lambda: (fetch(2), XY(2, 2), XY(0, 1),))
+        l0.start()
+        Z(0, 0); Z(1, 0); mine(2)
+    n4 = lax.rem(g, 4)
+    zz = jnp.where(n4 == 0, z, jnp.where(n4 == 1, srcs[0], jnp.where(n4 == 2, srcs[1], srcs[2])))
+    @pl.when(g < 4)
+    def _():
+        xv = xb[...].reshape(R, D)
+        bs = ssm.at[zz]
+        q8o[zz] = ((nt(xv, wz[0:192, :]) + bs[0:1, 0:192]).astype(BF16).astype(F32) * 0.125).astype(BF16)
+        ko[zz] = nt(xv, wz[192:384, :]).astype(BF16)
+        v = (nt(xv, wz[384:576, :]) + bs[1:2, 0:192]).astype(BF16)
+        vo[zz] = v
+        vt[...] = v.T
+        @pl.when(g == 2)
+        def _():
+            Z(0, 3)
+        def hook(i):
+            def on(n, j, fn):
+                @pl.when((g == n) & (i == j))
+                def _(): fn()
+            on(0, 0, lambda: (XY(0, 0),))
+            on(0, 1, lambda: (Z(0, 1), Z(2, 0),))
+            on(0, 2, lambda: (XY(1, 0),))
+            on(0, 3, lambda: (DG(0, 0), Z(1, 2), mine(3),))
+            on(1, 0, lambda: (XY(2, 0),))
+            on(1, 2, lambda: (DG(1, 0), Z(1, 1),))
+            on(2, 1, lambda: (DG(2, 0),))
+            on(2, 2, lambda: (XY(0, 1),))
+            on(2, 3, lambda: (XY(1, 2), XY(1, 1), XY(0, 2),))
+            on(3, 0, lambda: (XY(1, 3),))
+            on(3, 1, lambda: (XY(0, 3), Z(2, 2),))
+        attend_fwd(z, bs, q8o.at[zz], ko.at[zz], vt, dm, ct, lseo.at[zz], hook)
+        cv = ct[...].T
+        co[zz] = cv
+        acc[...] += nn(cv, wz[576:768, :]).astype(BF16).astype(F32)
+    @pl.when(g == 0)
+    def _():
+        l1.wait(); l2.start(); l0.wait(); Z(0, 2); fetch(0)
+    @pl.when(g == 1)
+    def _():
+        fetch(1); Z(1, 3)
+    @pl.when(g == 2)
+    def _():
+        fetch(2)
     @pl.when(g == 3)
     def _():
-        XY(2, 1); DG(2, 2)
+        Z(2, 3); DG(1, 1)
+    @pl.when(g == 3)
+    def _():
         sout[...] = ssm[...]
         for i in range(5):
             rw = slice(128 * i, 128 * i + 128)
@@ -466,29 +484,86 @@
             n1o[rw, :] = n
             r1o[rw, :] = jnp.broadcast_to(r, (128, 128))
             hlo[rw, :] = (n * vec[1:2, :] + vec[2:3, :]).astype(BF16)
-        DG(1, 2); DG(0, 1); DG(1, 1); DG(2, 3); DG(0, 2); DG(1, 3); DG(2, 1)
-        for h in range(4):
-            zsend_wait(opiece(h, dp), z, h)
+        acc[...] = jnp.zeros_like(acc)
+        DG(1, 3); DG(0, 1); Z(2, 1); DG(0, 3); DG(0, 2)
+        load_rows(z, cl, cs, xb, sem.at[0])
+        DG(1, 2)
+    for n in (1, 2, 3):
+        @pl.when(g == 4 + n)
+        def _():
+            fcopy(n - 1).wait()
+            if n > 1:
+                for d in stores(n - 2): d.wait()
+    @pl.when(g >= 4)
+    def _():
+        p = lax.rem(g, 2)
+        def on(n, i, j, fn):
+            @pl.when((g == n) & (i == j))
+            def _(): fn()
+        def tile(i, u):
+            rw = pl.ds(pl.multiple_of(i * (R // 2), 64), R // 2)
+            h = hlo[rw, :]
+            gate = nn(h, wf[p, 0])
+            up = nn(h, wf[p, 1])
+            a, slope = gelu_parts(gate)
+            ab[p, rw, :] = a
+            bb[p, rw, :] = up * slope
+            inner = (a * up).astype(BF16)
+            ib[p, rw, :] = inner
+            acc[rw, :] += nt(inner, wf[p, 2]).astype(BF16).astype(F32)
+            on(4, i, 0, lambda: (load(0), XY(2, 3),))
+            on(6, i, 0, lambda: (load(2),))
+            return u
+        lax.fori_loop(0, 2, tile, 0)
+    for n in range(4):
+        @pl.when(g == 4 + n)
+        def _():
+            for d in stores(n): d.start()
+    @pl.when(g == 4)
+    def _():
+        l2.wait(); XY(2, 2); load(1); XY(2, 1)
+    @pl.when(g == 5)
+    def _():
+        DG(2, 1); DG(2, 2); DG(2, 3)
+    @pl.when(g == 7)
+    def _():
+        tot = [jnp.zeros((1, D), F32)] * 3
+        for i in range(5):
+            rw = slice(128 * i, 128 * i + 128)
+            h1 = n1o[rw, :] * vec[1:2, :] + vec[2:3, :]
+            n, r = norm_fwd(h1 + acc[rw, :] + vec[3:4, :])
+            yo[rw, :] = (n * vec[4:5, :] + vec[5:6, :]).astype(BF16)
+            gy = xb[i].astype(F32)
+            gs = norm_bwd(gy * vec[4:5, :], n, r)
+            gs2o[rw, :] = gs
+            gfo[rw, :] = gs.astype(BF16)
+            tot = [tot[0] + jnp.sum(gy * n, axis=0, keepdims=True), tot[1] + jnp.sum(gy, axis=0, keepdims=True), tot[2] + jnp.sum(gs, axis=0, keepdims=True)]
+        vgo[...] = jnp.concatenate(tot + [jnp.zeros((5, D), F32)], axis=0)
+        pass
+        for p in range(4):
+            zsend_wait(opiece(p, dp), z, p)
         for j in range(3):
             sm(j).wait_send()
             for p in range(4): sent(j, p)
-            for p in (1, 2, 3): landed(j, p)
-        l2.wait()
-
-def run_kg(slen, llen, own, small, xl, xs, vec):
+        for n in (2, 3):
+            for d in stores(n): d.wait()
+
+def run_kg(slen, llen, own, small, xl, xs, cl, cs, vec):
     V, S = pltpu.VMEM, pltpu.SemaphoreType.DMA
     o = lambda *s: const(s)
     rz = lambda: sds((4, R, E), BF16)
     return pl.pallas_call(
         kg,
-        grid_spec=pltpu.PrefetchScalarGridSpec(num_scalar_prefetch=2, grid=(4,),
-            in_specs=[ANY, o(8, 256), ANY, ANY, o(8, D)],
-            out_specs=[ANY, o(4, 8, 256), o(4, R, E), o(4, R, E), o(4, R, E), o(4, R, E), o(4, 8, R), o(R, D), o(R, 128), o(R, D)],
-            scratch_shapes=[V((4, D, D), BF16), V((4, 8, 256), F32), V((5, 128, D), BF16), V((5, 512, 128), F32), V((E, R), BF16), V((E, R), BF16), V((R, D), F32), V((D, D), BF16),
-                            S((4, 4, 10)), S((4, 4, 11)), S((2,)), S((3,)), S((4,)), S((2,))]),
-        out_shape=[sds((4, 4, D, D), BF16), sds((4, 8, 256), F32), rz(), rz(), rz(), rz(), sds((4, 8, R), F32), sds((R, D), F32), sds((R, 128), F32), sds((R, D), BF16)],
+        grid_spec=pltpu.PrefetchScalarGridSpec(num_scalar_prefetch=2, grid=(8,),
+            in_specs=[ANY, o(8, 256), ANY, ANY, ANY, ANY, o(8, D)],
+            out_specs=[ANY, o(4, 8, 256), o(4, R, E), o(4, R, E), o(4, R, E), o(4, R, E), o(4, 8, R), o(R, D), o(R, 128), o(R, D), ANY, ANY, ANY, o(R, D), o(R, D), o(R, D), o(8, D)],
+            scratch_shapes=[V((4, 8, 256), F32), V((5, 128, D), BF16), V((5, 512, 128), F32), V((E, R), BF16), V((E, R), BF16), V((R, D), F32), V((D, D), BF16),
+                            V((2, 3, D, D), BF16), V((2, R, D), F32), V((2, R, D), F32), V((2, R, D), BF16),
+                            S((4, 4, 10)), S((4, 4, 11)), S((2,)), S((3,)), S((4,)), S((2,)), S((2,)), S((3, 2))]),
+        out_shape=[sds((4, 4, D, D), BF16), sds((4, 8, 256), F32), rz(), rz(), rz(), rz(), sds((4, 8, R), F32), sds((R, D), F32), sds((R, 128), F32), sds((R, D), BF16),
+                   sds((4, R, D), F32), sds((4, R, D), F32), sds((4, R, D), BF16), sds((R, D), BF16), sds((R, D), BF16), sds((R, D), F32), sds((8, D), F32)],
         compiler_params=pltpu.CompilerParams(dimension_semantics=("arbitrary",), collective_id=0, has_side_effects=True, vmem_limit_bytes=VM),
-        name="gather_attention_forward")(slen, llen, own, small, xl, xs, vec)
+        name="gather_forward")(slen, llen, own, small, xl, xs, cl, cs, vec)
 
 ZO = (3, 0, 2, 1)
 
@@ -509,7 +584,7 @@
         return u
     lax.fori_loop(0, n, body, 0)
 
-def kx(slen, llen, xl, xs, w, small, q8, k, v, ctx, lse, gs1, g3, yin, vin, gout, yout, dxout, vout,
+def kx(slen, llen, xl, xs, w, small, q8, k, v, ctx, lse, gs1, g3, yin, vin, gqo, gwo, guo, gdo, yout, dxout, vout,
        xb, dm, kt, gc, gqt, gk, gv, ga, gat, xt, acc, gob, dxs, gbs, stage, vr, vs, l0,
        r03, rx3, ry3, rxy3, ryx3, rl3, rr3, r01, rx1, ry1, rxy1, ryx1, rl1, rr1,
        sem, s0s, s0r, s0l, s1s, s1r, s2s, s2r, ys, yr, vsem_s, vsem_r, loc):
@@ -589,13 +664,16 @@
             def _():
                 if zz > 0: zs(kd, zz, True).wait_recv()
                 if zz < 3: zs(kd, zz, False).wait_recv()
-                def body(i, u):
+                for i in range(n):
                     t = mine(kd, zz)[i].astype(F32)
                     if zz > 0: t += rl[kd][zz, i].astype(F32)
                     if zz < 3: t += rr[kd][zz, i].astype(F32)
-                    gout[kd + i] = t
-                    return u
-                lax.fori_loop(0, n, body, 0)
+                    if kd:
+                        if i < 2: guo[i] = t
+                        else: gdo[...] = t
+                    else:
+                        for j in range(3): gqo[j] = t[:, j * E:j * E + E]
+                        gwo[...] = t[:, 3 * E:4 * E]
     order = far_order(z)
     def yb(s): return 4 * s + s // 3
     CHUNKS = ((2, 0), (2, 2), (1, 4))
@@ -766,8 +844,8 @@
         kx,
         grid_spec=pltpu.PrefetchScalarGridSpec(num_scalar_prefetch=2, grid=(4,),
             in_specs=[ANY, ANY, pl.BlockSpec((1, 1, D, D), lambda g, *_: (zo(g), 0, 0, 0)), pz(8, 256), rz(), rz(), rz(), rz(), pz(8, R), ANY, ANY, ANY, const((16, D))],
-            out_specs=[const((4, PR, D)), ANY, ANY, const((16, D))], scratch_shapes=scratch),
-        out_shape=[sds((4, PR, D), F32), sds((17, 128, D), BF16), sds((17, 128, D), BF16), sds((16, D), F32)],
+            out_specs=[const((3, PR, E)), const((PR, E)), const((2, PR, D)), const((PR, D)), ANY, ANY, const((16, D))], scratch_shapes=scratch),
+        out_shape=[sds((3, PR, E), F32), sds((PR, E), F32), sds((2, PR, D), F32), sds((PR, D), F32), sds((17, 128, D), BF16), sds((17, 128, D), BF16), sds((16, D), F32)],
         compiler_params=pltpu.CompilerParams(dimension_semantics=("arbitrary",), collective_id=1, has_side_effects=True, vmem_limit_bytes=VM),
         name="attention_backward_send")(slen, llen, xl, xs, W, small, q8, k, v, ctx, lse, gs1, g3, yv, vec)
 
@@ -779,23 +857,24 @@
     a = jnp.concatenate([jnp.transpose(w_qkv, (1, 2, 0)).reshape(576, D), w_out.T], 0)
     own = jnp.stack([a, w_up[:, 0], w_up[:, 1], w_down], 0)
     bt = jnp.transpose(b_qv, (1, 2, 0)).reshape(2, 192)
-    sl = jnp.zeros((1, 192), F32).at[0, 0:3].set(alibi_slopes(slope_index, 12))
+    sl = jnp.pad(alibi_slopes(slope_index, 12)[None], ((0, 0), (0, 189)))
     small = jnp.pad(jnp.concatenate([bt, sl], 0), ((0, 5), (0, 64)))
     return own, small
 def per_device(x_short, x_long, short_lengths, long_lengths, slope_index, w_qkv, b_qv, w_out, b_out, gain1, bias1, w_up, w_down, b_down, gain2, bias2, cot_short, cot_long):
     own, small = prep(slope_index, w_qkv, b_qv, w_out, w_up, w_down)
-    vec = jnp.stack([b_out, gain1, bias1, b_down, gain2, bias2, bias2, bias2], 0)
+    row = lax.broadcasted_iota(jnp.int32, (8, D), 0)
+    vec = jnp.broadcast_to(bias2[None], (8, D))
+    for i, t in enumerate((b_out, gain1, bias1, b_down, gain2)):
+        vec = jnp.where(row == i, t[None], vec)
     xl, cl = x_long.reshape(8, 128, D), cot_long.reshape(8, 128, D)
-    W, S, q8, k, v, ctx, lse, n1, r1, hl = run_kg(short_lengths, long_lengths, own, small, xl, x_short, vec)
-    a, b, inner, y, gf, gs2, vg2 = run_kb(cl, cot_short, W, hl, n1, vec)
+    W, S, q8, k, v, ctx, lse, n1, r1, hl, a, b, inner, y, gf, gs2, vg2 = run_kg(short_lengths, long_lengths, own, small, xl, x_short, cl, cot_short, vec)
     go3, gs1, vg1 = run_kc(W, a, b, inner, gf, hl, gs2, n1, r1, vec)
     m, dpx = lax.axis_index("mp"), lax.axis_index("dp")
     vsum = jnp.concatenate([vg2[:3], vg1[:3], jnp.zeros((10, D), F32)], 0)
-    G, Y, DX, vs = run_kx(short_lengths, long_lengths, xl, x_short, W, S, q8, k, v, ctx, lse, gs1, go3, y.reshape(5, 128, D), vsum)
+    gq, gwo, gup, gdn, Y, DX, vs = run_kx(short_lengths, long_lengths, xl, x_short, W, S, q8, k, v, ctx, lse, gs1, go3, y.reshape(5, 128, D), vsum)
     b = lax.dynamic_slice(vs[6:14, :192].reshape(4, 2, 3, 64), (m, 0, 0, 8 * dpx), (1, 2, 3, 8))[0]
     vs = lax.dynamic_slice(vs[:6], (0, 96 * dpx), (6, 96))
-    gq = G[0][:, :576].reshape(-1, 3, 192)
-    return (Y[8:], Y[:8].reshape(2, 512, D), DX[8:], DX[:8].reshape(2, 512, D), gq, jnp.transpose(b, (2, 0, 1)), G[0][:, 576:], vs[5], vs[3], vs[4], jnp.stack([G[1], G[2]], 1), G[3], vs[2], vs[0], vs[1])
+    return (Y[8:], Y[:8].reshape(2, 512, D), DX[8:], DX[:8].reshape(2, 512, D), jnp.transpose(gq, (1, 0, 2)), jnp.transpose(b, (2, 0, 1)), gwo, vs[5], vs[3], vs[4], jnp.transpose(gup, (1, 0, 2)), gdn, vs[2], vs[0], vs[1])
 def per_device_any(x_short, x_long, short_lengths, long_lengths, slope_index, w_qkv, b_qv, w_out, b_out, gain1, bias1, w_up, w_down, b_down, gain2, bias2, cot_short, cot_long):
     own, small = prep(slope_index, w_qkv, b_qv, w_out, w_up, w_down)
     W = lax.all_gather(own, "mp"); S = lax.all_gather(small, "mp")

time: 300 us -> 288 us (0.960)
  Pallas kernels: 269 us -> 257 us
    pallas_call x2 -> x1, Pallas kernels: 54 us -> 31.7 us  [call(): pl.pallas_call(kernel, grid_spec=pltpu.PrefetchScalarGridSpec(num_scalar_...]
    pallas_call x1, Pallas kernels: 80.8 us -> 91 us  [run_kg(): pl.pallas_call(kg, grid_spec=pltpu.PrefetchScalarGridSpec(num_scalar_pref...]
    slice x1, local copies, waits for them, and re-layouts: 6.52 us -> 3.36 us  [prep(): own = jnp.stack([a, w_up[:, 0], w_up[:, 1], w_down], 0)]
    unnamed x32 -> x18, local copies, waits for them, and re-layouts: 4.08 us -> 6.69 us
where the time goes in v5:
time: 288 us; the launch traced here: 287 us
  Pallas kernels  257 us (89%)
  local copies, waits for them, and re-layouts  22.7 us (8%)
  other arithmetic  6.85 us (2%)
    pallas_call x1, Pallas kernels, run_kx(): pl.pallas_call(kx, grid_spec=pltpu.PrefetchScalarGridSpec(num_scalar_pref...  134 us
    pallas_call x1, Pallas kernels, run_kg(): pl.pallas_call(kg, grid_spec=pltpu.PrefetchScalarGridSpec(num_scalar_pref...  91 us
    pallas_call x1, Pallas kernels, call(): pl.pallas_call(kernel, grid_spec=pltpu.PrefetchScalarGridSpec(num_scalar_...  31.7 us
    unnamed x18, local copies, waits for them, and re-layouts  6.69 us

profile of v5, /device:TPU:0, one launch (start us, length us, event | category | flops | bytes accessed | tf_op | source)
XLA Modules:
  0.0 287.4 jit_solution(14782629040249517541)
XLA Ops:
  0.7 0.8 fusion
  1.5 0.1 pad.12.clone
  1.6 0.7 copy.40
  2.3 0.1 reshape.62
  2.4 0.6 pad.9.small
  3.0 1.5 select_select_fusion.vec
  4.4 1.3 maximum_bitcast_fusion
  5.8 3.4 %fusion.1 = (bf16[768,1,768]{2,1,0:T(2,128)(2,1)S(1)}, bf16[768,1,768]{2,1,0:T(2,128)(2,1)S(1)}) fusion(bf16[768,2,768]{2,1,0:T(2,128)(2,1)S(1)} %copy-done), kind=kLoop, calls=%fused_computation.24 | loop fusion | bytes 4718592 | tf_op jit(solution)/shard_map/slice | solution.py:858
  9.2 0.4 copy_bitcast_fusion
  9.6 0.9 copy-done.3
  10.4 2.5 pad_maximum_fusion.own
  12.9 91.0 %gather_forward.1 = (bf16[4,4,768,768]{3,2,1,0:T(8,128)(2,1)}, f32[4,8,256]{2,1,0:T(8,128)}, bf16[4,640,192]{2,1,0:T(8,128)(2,1)}, bf16[4,640,192]{2,1,0:T(8,128...) custom-call(s32[9]{0:T(128)} %slen.3, s32[2]{0:T(128)} %llen.3, ...), custom_call_target="tpu_custom_call" | custom-call | tf_op jit(solution)/shard_map/gather_forward/pallas_call | solution.py:555
  104.0 0.7 slice.50
  104.7 31.7 %feed_backward.1 = (bf16[4,3,768,768]{3,2,1,0:T(8,128)(2,1)}, f32[640,768]{1,0:T(8,128)}, f32[8,768]{1,0:T(8,128)}) custom-call(bf16[4,4,768,768]{3,2,1,0:T(8,128)(2,1)} %get-tuple-element.42.wg.wu.wd.w, bf16[4,4,768,768]{3,2,1,0:T(8,128)(2,1)} %get-tuple-element.42.wg.wu.wd.w, bf16[4,4,768,768]{3,2,1,0:T(8,128)(2,1)} %get-tuple-element.42.wg.wu.wd.w, ...), custom_call_target="tpu_custom_call" | custom-call | tf_op jit(solution)/shard_map/feed_backward/pallas_call | solution.py:165
  136.5 0.7 slice.51
  137.2 0.7 maximum_maximum_fusion.vin
  137.9 134.2 %attention_backward_send.1 = (f32[3,96,192]{2,1,0:T(8,128)}, f32[96,192]{1,0:T(8,128)}, f32[2,96,768]{2,1,0:T(8,128)}, f32[96,768]{1,0:T(8,128)}, bf16[17,128,76...) custom-call(s32[9]{0:T(128)} %slen.3, s32[2]{0:T(128)} %llen.3, bf16[8,128,768]{2,1,0:T(8,128)(2,1)} %bitcast.39, ...), custom_call_target="tpu_custom_call" | custom-call | tf_op jit(solution)/shard_map/attention_backward_send/pallas_call | solution.py:843
  272.2 0.7 slice.56
  272.9 0.7 slice.57
  273.6 0.1 constant_dynamic-slice_fusion
  273.7 0.5 slice_bitcast_fusion
  274.2 0.1 reshape.67
  274.4 0.6 copy.48
  275.0 2.5 copy.42
  277.4 2.7 slice.53
  280.1 1.3 slice.52
  281.4 1.2 copy-done.1
  282.7 1.2 slice.55
  283.9 1.3 slice.54
  285.3 0.7 copy.52
  286.0 0.6 copy.53
  286.6 0.7 copy.54
  (18 shorter events, 0.1 us)
Async XLA Ops:
  0.6 5.1 %copy-start = (bf16[768,2,768]{2,1,0:T(2,128)(2,1)S(1)}, bf16[768,2,768]{2,1,0:T(2,128)(2,1)}, u32[]{:S(2)}) copy-start(bf16[768,2,768]{2,1,0:T(2,128)(2,1)} %param.29) | copy-start | bytes 7077892
  9.2 1.3 copy-start.3
  275.0 5.1 %copy-start.2 = (bf16[17,128,768]{2,1,0:T(8,128)(2,1)S(1)}, bf16[17,128,768]{2,1,0:T(8,128)(2,1)}, u32[]{:S(2)}) copy-start(bf16[17,128,768]{2,1,0:T(8,128)(2,1)} %get-tuple-element.62) | copy-start | bytes 10027012
  280.1 2.6 copy-start.1
  283.9 1.3 copy-start.5
  283.9 2.1 copy-start.6
  283.9 2.7 copy-start.4

commit v6 on v5

--- a/solution.py
+++ b/solution.py
@@ -584,7 +584,7 @@
         return u
     lax.fori_loop(0, n, body, 0)
 
-def kx(slen, llen, xl, xs, w, small, q8, k, v, ctx, lse, gs1, g3, yin, vin, gqo, gwo, guo, gdo, yout, dxout, vout,
+def kx(slen, llen, xl, xs, w, small, q8, k, v, ctx, lse, gs1, g3, yin, vin2, vin1, gqo, gwo, guo, gdo, yout, dxout, vout,
        xb, dm, kt, gc, gqt, gk, gv, ga, gat, xt, acc, gob, dxs, gbs, stage, vr, vs, l0,
        r03, rx3, ry3, rxy3, ryx3, rl3, rr3, r01, rx1, ry1, rxy1, ryx1, rl1, rr1,
        sem, s0s, s0r, s0l, s1s, s1r, s2s, s2r, ys, yr, vsem_s, vsem_r, loc):
@@ -776,7 +776,9 @@
     def X():
         for i in range(5):
             dxs[i] = acc[128 * i:128 * i + 128, :].astype(BF16)
-        vs[0] = vin[...]
+        vs[0] = jnp.zeros((16, D), F32)
+        vs[0, 0:3, :] = vin2[0:3, :]
+        vs[0, 3:6, :] = vin1[0:3, :]
         for i in range(4):
             vs[0, 6 + 2 * i:8 + 2 * i, 0:192] = gbs[i, 0:2, 0:192]
         vcopy(0).start()
@@ -829,7 +831,7 @@
             ownall(lambda h: own(t, h, 1).wait())
         for i in range(5): vcopy(i).wait_send()
 
-def run_kx(slen, llen, xl, xs, W, small, q8, k, v, ctx, lse, gs1, g3, yv, vec):
+def run_kx(slen, llen, xl, xs, W, small, q8, k, v, ctx, lse, gs1, g3, yv, v2, v1):
     pz = lambda *s: pl.BlockSpec((1,) + s, lambda g, *_: (zo(g),) + (0,) * len(s))
     rz = lambda: pz(R, E)
     V, S = pltpu.VMEM, pltpu.SemaphoreType.DMA
@@ -843,11 +845,32 @@
     return pl.pallas_call(
         kx,
         grid_spec=pltpu.PrefetchScalarGridSpec(num_scalar_prefetch=2, grid=(4,),
-            in_specs=[ANY, ANY, pl.BlockSpec((1, 1, D, D), lambda g, *_: (zo(g), 0, 0, 0)), pz(8, 256), rz(), rz(), rz(), rz(), pz(8, R), ANY, ANY, ANY, const((16, D))],
+            in_specs=[ANY, ANY, pl.BlockSpec((1, 1, D, D), lambda g, *_: (zo(g), 0, 0, 0)), pz(8, 256), rz(), rz(), rz(), rz(), pz(8, R), ANY, ANY, ANY, const((8, D)), const((8, D))],
             out_specs=[const((3, PR, E)), const((PR, E)), const((2, PR, D)), const((PR, D)), ANY, ANY, const((16, D))], scratch_shapes=scratch),
         out_shape=[sds((3, PR, E), F32), sds((PR, E), F32), sds((2, PR, D), F32), sds((PR, D), F32), sds((17, 128, D), BF16), sds((17, 128, D), BF16), sds((16, D), F32)],
         compiler_params=pltpu.CompilerParams(dimension_semantics=("arbitrary",), collective_id=1, has_side_effects=True, vmem_limit_bytes=VM),
-        name="attention_backward_send")(slen, llen, xl, xs, W, small, q8, k, v, ctx, lse, gs1, g3, yv, vec)
+        name="attention_backward_send")(slen, llen, xl, xs, W, small, q8, k, v, ctx, lse, gs1, g3, yv, v2, v1)
+
+def split_rows(y, d, gq, gw, gd, yl, ys, dl, ds, gqo, gwo, gdo, buf, si, so):
+    moves = [(y, 0, 0, 8, yl), (y, 0, 8, 9, ys), (d, 1, 0, 8, dl), (d, 1, 8, 9, ds)]
+    put = lambda i: pltpu.make_async_copy(moves[i][0].at[pl.ds(moves[i][2], moves[i][3])], buf.at[moves[i][1], pl.ds(moves[i][2], moves[i][3])], si.at[i])
+    out = lambda i: pltpu.make_async_copy(buf.at[moves[i][1], pl.ds(moves[i][2], moves[i][3])], moves[i][4], so.at[i])
+    for i in range(4): put(i).start()
+    gqo[...] = gq[...]
+    gwo[...] = gw[...]
+    gdo[...] = gd[...]
+    for i in range(4):
+        put(i).wait(); out(i).start()
+    for i in range(4): out(i).wait()
+
+def run_split(Y, DX, gq, gwo, gdn):
+    V = pl.BlockSpec(memory_space=pltpu.VMEM)
+    S = pltpu.SemaphoreType.DMA
+    r = lambda n: sds((n, 128, D), BF16)
+    return pl.pallas_call(split_rows, in_specs=[ANY, ANY, V, V, V], out_specs=[ANY] * 4 + [V] * 3,
+        out_shape=[r(8), r(9), r(8), r(9), sds((3, PR, E), F32), sds((PR, E), F32), sds((PR, D), F32)],
+        scratch_shapes=[pltpu.VMEM((2, 17, 128, D), BF16), S((4,)), S((4,))],
+        compiler_params=pltpu.CompilerParams(vmem_limit_bytes=VM), name="split_rows")(Y, DX, gq, gwo, gdn)
 
 def alibi_slopes(slope_index, head_total):
     power = 1 << head_total.bit_length() - 1
@@ -870,11 +893,11 @@
     W, S, q8, k, v, ctx, lse, n1, r1, hl, a, b, inner, y, gf, gs2, vg2 = run_kg(short_lengths, long_lengths, own, small, xl, x_short, cl, cot_short, vec)
     go3, gs1, vg1 = run_kc(W, a, b, inner, gf, hl, gs2, n1, r1, vec)
     m, dpx = lax.axis_index("mp"), lax.axis_index("dp")
-    vsum = jnp.concatenate([vg2[:3], vg1[:3], jnp.zeros((10, D), F32)], 0)
-    gq, gwo, gup, gdn, Y, DX, vs = run_kx(short_lengths, long_lengths, xl, x_short, W, S, q8, k, v, ctx, lse, gs1, go3, y.reshape(5, 128, D), vsum)
+    gq, gwo, gup, gdn, Y, DX, vs = run_kx(short_lengths, long_lengths, xl, x_short, W, S, q8, k, v, ctx, lse, gs1, go3, y.reshape(5, 128, D), vg2, vg1)
     b = lax.dynamic_slice(vs[6:14, :192].reshape(4, 2, 3, 64), (m, 0, 0, 8 * dpx), (1, 2, 3, 8))[0]
     vs = lax.dynamic_slice(vs[:6], (0, 96 * dpx), (6, 96))
-    return (Y[8:], Y[:8].reshape(2, 512, D), DX[8:], DX[:8].reshape(2, 512, D), jnp.transpose(gq, (1, 0, 2)), jnp.transpose(b, (2, 0, 1)), gwo, vs[5], vs[3], vs[4], jnp.transpose(gup, (1, 0, 2)), gdn, vs[2], vs[0], vs[1])
+    yl, ys, dl, ds, gq, gwo, gdn = run_split(Y, DX, gq, gwo, gdn)
+    return (ys, yl.reshape(2, 512, D), ds, dl.reshape(2, 512, D), jnp.transpose(gq, (1, 0, 2)), jnp.transpose(b, (2, 0, 1)), gwo, vs[5], vs[3], vs[4], jnp.transpose(gup, (1, 0, 2)), gdn, vs[2], vs[0], vs[1])
 def per_device_any(x_short, x_long, short_lengths, long_lengths, slope_index, w_qkv, b_qv, w_out, b_out, gain1, bias1, w_up, w_down, b_down, gain2, bias2, cot_short, cot_long):
     own, small = prep(slope_index, w_qkv, b_qv, w_out, w_up, w_down)
     W = lax.all_gather(own, "mp"); S = lax.all_gather(small, "mp")

time: 288 us -> 281 us (0.976)
  local copies, waits for them, and re-layouts: 22.7 us -> 11.6 us
  Pallas kernels: 257 us -> 265 us
  other arithmetic: 6.85 us -> 3.52 us
    slice x6 -> x0, local copies, waits for them, and re-layouts: 8.04 us -> none  [the longest x1 2.65 us: per_device(): Y[:8].reshape(2, 512, D)]
    pallas_call x0 -> x1, Pallas kernels: none -> 7.64 us  [run_split(): pl.pallas_call(split_rows, in_specs=[ANY, ANY, V, V, V], out_specs=[ANY]...]
    unnamed x18 -> x27, local copies, waits for them, and re-layouts: 6.69 us -> 2.6 us
    slice x1, local copies, waits for them, and re-layouts: 3.36 us -> 6.52 us  [prep(): own = jnp.stack([a, w_up[:, 0], w_up[:, 1], w_down], 0)]
where the time goes in v6:
time: 281 us; the launch traced here: 280 us
  Pallas kernels  265 us (94%)
  local copies, waits for them, and re-layouts  11.6 us (4%)
  other arithmetic  3.52 us (1%)
    pallas_call x1, Pallas kernels, run_kx(): pl.pallas_call(kx, grid_spec=pltpu.PrefetchScalarGridSpec(num_scalar_pref...  134 us
    pallas_call x1, Pallas kernels, run_kg(): pl.pallas_call(kg, grid_spec=pltpu.PrefetchScalarGridSpec(num_scalar_pref...  90.9 us
    pallas_call x1, Pallas kernels, call(): pl.pallas_call(kernel, grid_spec=pltpu.PrefetchScalarGridSpec(num_scalar_...  31.8 us
    pallas_call x1, Pallas kernels, run_split(): pl.pallas_call(split_rows, in_specs=[ANY, ANY, V, V, V], out_specs=[ANY]...  7.64 us
    slice x1, local copies, waits for them, and re-layouts, prep(): own = jnp.stack([a, w_up[:, 0], w_up[:, 1], w_down], 0)  6.52 us

profile of v6, /device:TPU:0, one launch (start us, length us, event | category | flops | bytes accessed | tf_op | source)
XLA Modules:
  0.0 280.4 jit_solution(14600505576973241331)
XLA Ops:
  0.6 6.5 %fusion.1 = (bf16[768,1,768]{2,1,0:T(2,128)(2,1)S(1)}, bf16[768,1,768]{2,1,0:T(2,128)(2,1)S(1)}) fusion(bf16[768,2,768]{2,1,0:T(2,128)(2,1)} %param.29), kind=kLoop, calls=%fused_computation.23 | loop fusion | bytes 4718592 | tf_op jit(solution)/shard_map/slice | solution.py:881
  7.2 0.0 copy-start.1
  7.2 0.0 copy-start.3
  7.2 0.4 copy_bitcast_fusion
  7.6 0.0 copy-start
  7.6 0.7 copy-done.1
  8.3 0.1 copy-done.3
  8.4 0.1 maximum_bitcast_fusion
  8.5 0.5 copy-done
  9.0 0.0 copy-start.9
  9.0 0.0 copy-start.10
  9.0 0.0 copy-start.11
  9.0 0.0 copy-start.12
  9.0 2.7 pad_maximum_fusion.own
  11.8 0.0 copy-done.5
  11.8 0.0 copy-done.6
  11.8 0.0 copy-done.7
  11.8 0.0 copy-done.8
  11.8 0.0 copy-done.9
  11.8 0.7 select_select_fusion.vec
  12.5 0.1 reshape.62
  12.6 0.6 pad.9.small
  13.2 90.9 %gather_forward.1 = (bf16[4,4,768,768]{3,2,1,0:T(8,128)(2,1)}, f32[4,8,256]{2,1,0:T(8,128)}, bf16[4,640,192]{2,1,0:T(8,128)(2,1)}, bf16[4,640,192]{2,1,0:T(8,128...) custom-call(s32[9]{0:T(128)} %slen.3, s32[2]{0:T(128)} %llen.3, ...), custom_call_target="tpu_custom_call" | custom-call | tf_op jit(solution)/shard_map/gather_forward/pallas_call | solution.py:555
  104.1 31.8 %feed_backward.1 = (bf16[4,3,768,768]{3,2,1,0:T(8,128)(2,1)}, f32[640,768]{1,0:T(8,128)}, f32[8,768]{1,0:T(8,128)}) custom-call(bf16[4,4,768,768]{3,2,1,0:T(8,128)(2,1)} %get-tuple-element.49.wg.wu.wd.w, bf16[4,4,768,768]{3,2,1,0:T(8,128)(2,1)} %get-tuple-element.49.wg.wu.wd.w, bf16[4,4,768,768]{3,2,1,0:T(8,128)(2,1)} %get-tuple-element.49.wg.wu.wd.w, ...), custom_call_target="tpu_custom_call" | custom-call | tf_op jit(solution)/shard_map/feed_backward/pallas_call | solution.py:165
  135.9 134.2 %attention_backward_send.1 = (f32[3,96,192]{2,1,0:T(8,128)}, f32[96,192]{1,0:T(8,128)}, f32[2,96,768]{2,1,0:T(8,128)}, f32[96,768]{1,0:T(8,128)}, bf16[17,128,76...) custom-call(s32[9]{0:T(128)} %slen.3, s32[2]{0:T(128)} %llen.3, bf16[8,128,768]{2,1,0:T(8,128)(2,1)} %bitcast.39, ...), custom_call_target="tpu_custom_call" | custom-call | tf_op jit(solution)/shard_map/attention_backward_send/pallas_call | solution.py:845
  270.2 7.6 %split_rows.1 = (bf16[8,128,768]{2,1,0:T(8,128)(2,1)}, bf16[9,128,768]{2,1,0:T(8,128)(2,1)}, bf16[8,128,768]{2,1,0:T(8,128)(2,1)}, bf16[9,128,768]{2,1,0:T(8,128...) custom-call(bf16[17,128,768]{2,1,0:T(8,128)(2,1)} %get-tuple-element.69.y, ...), custom_call_target="tpu_custom_call" | custom-call | tf_op jit(solution)/shard_map/split_rows/pallas_call | solution.py:870
  277.8 1.3 copy.42
  279.1 0.1 reshape.67
  279.2 0.1 constant_dynamic-slice_fusion.1
  279.2 0.6 copy.48
  279.8 0.1 constant_dynamic-slice_fusion
  279.9 0.5 slice_bitcast_fusion
  (19 shorter events, 0.1 us)
Async XLA Ops:
  7.2 1.2 copy-start.1
  7.2 1.2 copy-start.3
  7.6 1.4 copy-start
  9.0 2.8 %copy-start.5 = (f32[768]{0:T(1024)S(1)}, f32[768]{0:T(1024)}, u32[]{:S(2)}) copy-start(f32[768]{0:T(1024)} %param.33) | copy-start | bytes 9220
  9.0 2.8 %copy-start.6 = (f32[768]{0:T(1024)S(1)}, f32[768]{0:T(1024)}, u32[]{:S(2)}) copy-start(f32[768]{0:T(1024)} %param.26) | copy-start | bytes 9220
  9.0 2.8 %copy-start.7 = (f32[768]{0:T(1024)S(1)}, f32[768]{0:T(1024)}, u32[]{:S(2)}) copy-start(f32[768]{0:T(1024)} %param.27) | copy-start | bytes 9220
  9.0 2.8 %copy-start.8 = (f32[768]{0:T(1024)S(1)}, f32[768]{0:T(1024)}, u32[]{:S(2)}) copy-start(f32[768]{0:T(1024)} %param.28) | copy-start | bytes 9220
  9.0 2.8 %copy-start.9 = (f32[768]{0:T(1024)S(1)}, f32[768]{0:T(1024)}, u32[]{:S(2)}) copy-start(f32[768]{0:T(1024)} %param.31) | copy-start | bytes 9220
  9.0 2.8 %copy-start.10 = (f32[768]{0:T(1024)S(1)}, f32[768]{0:T(1024)}, u32[]{:S(2)}) copy-start(f32[768]{0:T(1024)} %param.32) | copy-start | bytes 9220
  9.0 3.5 %copy-start.11 = (f32[64,2,3]{0,1,2:T(2,128)S(1)}, f32[64,2,3]{0,1,2:T(2,128)}, u32[]{:S(2)}) copy-start(f32[64,2,3]{0,1,2:T(2,128)} %param.24) | copy-start | bytes 4612
  9.0 3.6 %copy-start.12 = (s32[3]{0:T(128)S(1)}, s32[3]{0:T(128)}, u32[]{:S(2)}) copy-start(s32[3]{0:T(128)} %param.22) | copy-start | bytes 40
  270.1 7.7 %copy-start.2 = (f32[2,96,768]{2,1,0:T(8,128)S(1)}, f32[2,96,768]{2,1,0:T(8,128)}, u32[]{:S(2)}) copy-start(f32[2,96,768]{2,1,0:T(8,128)} %get-tuple-element.81) | copy-start | bytes 1769476
  270.1 8.9 %copy-start.4 = (f32[16,768]{1,0:T(8,128)S(1)}, f32[16,768]{1,0:T(8,128)}, u32[]{:S(2)}) copy-start(f32[16,768]{1,0:T(8,128)} %get-tuple-element.79) | copy-start | bytes 147460

commit v7 on v6

--- a/solution.py
+++ b/solution.py
@@ -852,16 +852,20 @@
         name="attention_backward_send")(slen, llen, xl, xs, W, small, q8, k, v, ctx, lse, gs1, g3, yv, v2, v1)
 
 def split_rows(y, d, gq, gw, gd, yl, ys, dl, ds, gqo, gwo, gdo, buf, si, so):
-    moves = [(y, 0, 0, 8, yl), (y, 0, 8, 9, ys), (d, 1, 0, 8, dl), (d, 1, 8, 9, ds)]
-    put = lambda i: pltpu.make_async_copy(moves[i][0].at[pl.ds(moves[i][2], moves[i][3])], buf.at[moves[i][1], pl.ds(moves[i][2], moves[i][3])], si.at[i])
-    out = lambda i: pltpu.make_async_copy(buf.at[moves[i][1], pl.ds(moves[i][2], moves[i][3])], moves[i][4], so.at[i])
-    for i in range(4): put(i).start()
+    moves = [(t, i, f, n, h, f - 8 * (f // 8)) for i, (t, lo, sh) in enumerate(((y, yl, ys), (d, dl, ds))) for f, n, h in ((0, 4, lo), (4, 4, lo), (8, 5, sh), (13, 4, sh))]
+    def put(i):
+        t, j, f, n, _, _ = moves[i]
+        return pltpu.make_async_copy(t.at[pl.ds(f, n)], buf.at[j, pl.ds(f, n)], si.at[i])
+    def out(i):
+        _, j, f, n, h, o = moves[i]
+        return pltpu.make_async_copy(buf.at[j, pl.ds(f, n)], h.at[pl.ds(o, n)], so.at[i])
+    for i in range(8): put(i).start()
     gqo[...] = gq[...]
     gwo[...] = gw[...]
     gdo[...] = gd[...]
-    for i in range(4):
+    for i in range(8):
         put(i).wait(); out(i).start()
-    for i in range(4): out(i).wait()
+    for i in range(8): out(i).wait()
 
 def run_split(Y, DX, gq, gwo, gdn):
     V = pl.BlockSpec(memory_space=pltpu.VMEM)
@@ -869,7 +873,7 @@
     r = lambda n: sds((n, 128, D), BF16)
     return pl.pallas_call(split_rows, in_specs=[ANY, ANY, V, V, V], out_specs=[ANY] * 4 + [V] * 3,
         out_shape=[r(8), r(9), r(8), r(9), sds((3, PR, E), F32), sds((PR, E), F32), sds((PR, D), F32)],
-        scratch_shapes=[pltpu.VMEM((2, 17, 128, D), BF16), S((4,)), S((4,))],
+        scratch_shapes=[pltpu.VMEM((2, 17, 128, D), BF16), S((8,)), S((8,))],
         compiler_params=pltpu.CompilerParams(vmem_limit_bytes=VM), name="split_rows")(Y, DX, gq, gwo, gdn)
 
 def alibi_slopes(slope_index, head_total):

time: 281 us -> 281 us (level)
  no operation moved by 1% of the time
where the time goes in v7:
time: 281 us
  Pallas kernels  265 us (94%)
  local copies, waits for them, and re-layouts  11.6 us (4%)
  other arithmetic  3.52 us (1%)
    pallas_call x1, Pallas kernels, run_kx(): pl.pallas_call(kx, grid_spec=pltpu.PrefetchScalarGridSpec(num_scalar_pref...  134 us
    pallas_call x1, Pallas kernels, run_kg(): pl.pallas_call(kg, grid_spec=pltpu.PrefetchScalarGridSpec(num_scalar_pref...  90.9 us
    pallas_call x1, Pallas kernels, call(): pl.pallas_call(kernel, grid_spec=pltpu.PrefetchScalarGridSpec(num_scalar_...  31.8 us
    pallas_call x1, Pallas kernels, run_split(): pl.pallas_call(split_rows, in_specs=[ANY, ANY, V, V, V], out_specs=[ANY]...  7.7 us
    slice x1, local copies, waits for them, and re-layouts, prep(): own = jnp.stack([a, w_up[:, 0], w_up[:, 1], w_down], 0)  6.52 us

profile of v7, /device:TPU:0, one launch (start us, length us, event | category | flops | bytes accessed | tf_op | source)
XLA Modules:
  0.0 280.5 jit_solution(5178243513190857835)
XLA Ops:
  0.6 6.5 %fusion.1 = (bf16[768,1,768]{2,1,0:T(2,128)(2,1)S(1)}, bf16[768,1,768]{2,1,0:T(2,128)(2,1)S(1)}) fusion(bf16[768,2,768]{2,1,0:T(2,128)(2,1)} %param.29), kind=kLoop, calls=%fused_computation.23 | loop fusion | bytes 4718592 | tf_op jit(solution)/shard_map/slice | solution.py:885
  7.2 0.0 copy-start.1
  7.2 0.0 copy-start.3
  7.2 0.4 copy_bitcast_fusion
  7.6 0.0 copy-start
  7.6 0.7 copy-done.1
  8.3 0.1 copy-done.3
  8.4 0.1 maximum_bitcast_fusion
  8.5 0.5 copy-done
  9.0 0.0 copy-start.9
  9.0 0.0 copy-start.10
  9.0 0.0 copy-start.11
  9.0 0.0 copy-start.12
  9.0 2.7 pad_maximum_fusion.own
  11.8 0.0 copy-done.5
  11.8 0.0 copy-done.6
  11.8 0.0 copy-done.7
  11.8 0.0 copy-done.8
  11.8 0.0 copy-done.9
  11.8 0.7 select_select_fusion.vec
  12.5 0.1 reshape.62
  12.6 0.6 pad.9.small
  13.2 90.9 %gather_forward.1 = (bf16[4,4,768,768]{3,2,1,0:T(8,128)(2,1)}, f32[4,8,256]{2,1,0:T(8,128)}, bf16[4,640,192]{2,1,0:T(8,128)(2,1)}, bf16[4,640,192]{2,1,0:T(8,128...) custom-call(s32[9]{0:T(128)} %slen.3, s32[2]{0:T(128)} %llen.3, ...), custom_call_target="tpu_custom_call" | custom-call | tf_op jit(solution)/shard_map/gather_forward/pallas_call | solution.py:555
  104.1 31.8 %feed_backward.1 = (bf16[4,3,768,768]{3,2,1,0:T(8,128)(2,1)}, f32[640,768]{1,0:T(8,128)}, f32[8,768]{1,0:T(8,128)}) custom-call(bf16[4,4,768,768]{3,2,1,0:T(8,128)(2,1)} %get-tuple-element.49.wg.wu.wd.w, bf16[4,4,768,768]{3,2,1,0:T(8,128)(2,1)} %get-tuple-element.49.wg.wu.wd.w, bf16[4,4,768,768]{3,2,1,0:T(8,128)(2,1)} %get-tuple-element.49.wg.wu.wd.w, ...), custom_call_target="tpu_custom_call" | custom-call | tf_op jit(solution)/shard_map/feed_backward/pallas_call | solution.py:165
  135.9 134.2 %attention_backward_send.1 = (f32[3,96,192]{2,1,0:T(8,128)}, f32[96,192]{1,0:T(8,128)}, f32[2,96,768]{2,1,0:T(8,128)}, f32[96,768]{1,0:T(8,128)}, bf16[17,128,76...) custom-call(s32[9]{0:T(128)} %slen.3, s32[2]{0:T(128)} %llen.3, bf16[8,128,768]{2,1,0:T(8,128)(2,1)} %bitcast.39, ...), custom_call_target="tpu_custom_call" | custom-call | tf_op jit(solution)/shard_map/attention_backward_send/pallas_call | solution.py:845
  270.2 7.7 %split_rows.1 = (bf16[8,128,768]{2,1,0:T(8,128)(2,1)}, bf16[9,128,768]{2,1,0:T(8,128)(2,1)}, bf16[8,128,768]{2,1,0:T(8,128)(2,1)}, bf16[9,128,768]{2,1,0:T(8,128...) custom-call(bf16[17,128,768]{2,1,0:T(8,128)(2,1)} %get-tuple-element.69.y, ...), custom_call_target="tpu_custom_call" | custom-call | tf_op jit(solution)/shard_map/split_rows/pallas_call | solution.py:874
  277.9 1.3 copy.42
  279.1 0.1 reshape.67
  279.2 0.1 constant_dynamic-slice_fusion.1
  279.3 0.6 copy.48
  279.9 0.1 constant_dynamic-slice_fusion
  280.0 0.5 slice_bitcast_fusion
  (19 shorter events, 0.1 us)
Async XLA Ops:
  7.2 1.2 copy-start.1
  7.2 1.2 copy-start.3
  7.6 1.4 copy-start
  9.0 2.8 %copy-start.5 = (f32[768]{0:T(1024)S(1)}, f32[768]{0:T(1024)}, u32[]{:S(2)}) copy-start(f32[768]{0:T(1024)} %param.33) | copy-start | bytes 9220
  9.0 2.8 %copy-start.6 = (f32[768]{0:T(1024)S(1)}, f32[768]{0:T(1024)}, u32[]{:S(2)}) copy-start(f32[768]{0:T(1024)} %param.26) | copy-start | bytes 9220
  9.0 2.8 %copy-start.7 = (f32[768]{0:T(1024)S(1)}, f32[768]{0:T(1024)}, u32[]{:S(2)}) copy-start(f32[768]{0:T(1024)} %param.27) | copy-start | bytes 9220
  9.0 2.8 %copy-start.8 = (f32[768]{0:T(1024)S(1)}, f32[768]{0:T(1024)}, u32[]{:S(2)}) copy-start(f32[768]{0:T(1024)} %param.28) | copy-start | bytes 9220
  9.0 2.8 %copy-start.9 = (f32[768]{0:T(1024)S(1)}, f32[768]{0:T(1024)}, u32[]{:S(2)}) copy-start(f32[768]{0:T(1024)} %param.31) | copy-start | bytes 9220
  9.0 2.8 %copy-start.10 = (f32[768]{0:T(1024)S(1)}, f32[768]{0:T(1024)}, u32[]{:S(2)}) copy-start(f32[768]{0:T(1024)} %param.32) | copy-start | bytes 9220
  9.0 3.5 %copy-start.11 = (f32[64,2,3]{0,1,2:T(2,128)S(1)}, f32[64,2,3]{0,1,2:T(2,128)}, u32[]{:S(2)}) copy-start(f32[64,2,3]{0,1,2:T(2,128)} %param.24) | copy-start | bytes 4612
  9.0 3.6 %copy-start.12 = (s32[3]{0:T(128)S(1)}, s32[3]{0:T(128)}, u32[]{:S(2)}) copy-start(s32[3]{0:T(128)} %param.22) | copy-start | bytes 40
  270.1 7.7 %copy-start.2 = (f32[2,96,768]{2,1,0:T(8,128)S(1)}, f32[2,96,768]{2,1,0:T(8,128)}, u32[]{:S(2)}) copy-start(f32[2,96,768]{2,1,0:T(8,128)} %get-tuple-element.81) | copy-start | bytes 1769476
  270.1 9.0 %copy-start.4 = (f32[16,768]{1,0:T(8,128)S(1)}, f32[16,768]{1,0:T(8,128)}, u32[]{:S(2)}) copy-start(f32[16,768]{1,0:T(8,128)} %get-tuple-element.79) | copy-start | bytes 147460
